TPU v7x, 256 devices: a whole 4x4x8 slice. The times are simulated.
256 devices in a mesh: freq: 32 (over z, x), panel: 8 (over y, core).
Axes of the slice: x: 4, y: 4, z: 8, core: 2. Of those that a mesh axis runs over, the one named last changes fastest.
Arguments:
- wavefield: float32 [32, 2, 128, 8192], P('freq', None, None, 'panel'), may hold values from -6 to 6
- direct: float32 [32, 2, 128, 8192], P('freq', None, None, 'panel'), may hold values from -6 to 6
- left_factors: float32 [32, 8192, 6, 128], P('freq', 'panel'), may hold values from -0.375 to 0.375
- right_factors: float32 [32, 32, 6, 256, 128], P('freq', 'panel'), may hold values from -0.3125 to 0.3125
- tile_src: int32 [32, 6], P('panel'), may hold values from -1 to 7, as said below
- onset: int32 [128, 2048], P('freq'), may hold values from 128 to 895
Outputs:
- focusing: float32 [32, 2, 128, 8192], P('freq', None, None, 'panel')
Inputs may be any that keep to these rules, and one draw needn't show every extreme that they name: `tile_src`: in each receiver panel's row the first k slots name distinct source tiles, with 2 <= k <= 6, and the other slots hold -1; in every aligned block of 4 panels at least one panel fills all 6 slots.
All inputs are finite; a program needn't handle non-finite values.
Results may differ from a plain program's by a relative error of at most 0.0003.
Values sent between devices are 32-bit elements; how exact they have to be, the bound alone decides.
No kernel may reach another device: no remote copies, remote signals or barrier semaphores. Data moves between devices by JAX's collectives and lax.ppermute only.
A program may use at most 128 MiB of HBM per device.

v0:
```python
import math

import jax
import jax.numpy as jnp
import ml_dtypes
import numpy as np
from jax import lax
from jax.experimental import pallas as pl
from jax.experimental.pallas import tpu as pltpu
from jax.sharding import PartitionSpec as P

NT = 1024
FIRST_BIN = 8
T_USED = 896

F32 = jnp.float32
BF16 = jnp.bfloat16
NN = (((1,), (0,)), ((), ()))
NT_DIMS = (((1,), (1,)), ((), ()))


def split(x):
    high = x.astype(BF16)
    low = (x - high.astype(F32)).astype(BF16)
    return high, low


def dot(a, b, dims=NN):
    return lax.dot_general(a, b, dims, preferred_element_type=F32)


def pair_coef(products, rank):
    half = products.shape[0] // 2
    real, imag = products[:half], products[half:]
    lane = lax.broadcasted_iota(jnp.int32, real.shape, 1)
    sign = jnp.where(lane < rank, 1.0, -1.0).astype(F32)
    first = real + sign * pltpu.roll(imag, rank, 1)
    second = imag - sign * pltpu.roll(real, rank, 1)
    return jnp.concatenate([first, second], axis=0)


def adjoint_kernel(src_ref, me_ref, field_ref, left_ref, right_ref, own_ref, other_ref):
    p = pl.program_id(0)
    slots, tile, width = left_ref.shape
    rank = width // 2
    me = me_ref[0]

    @pl.when(p == 0)
    def _():
        own_ref[...] = jnp.zeros_like(own_ref)
        other_ref[...] = jnp.zeros_like(other_ref)

    field = field_ref[...]
    field_h, field_l = split(field.reshape(field.shape[0] * field.shape[1], tile))
    for s in range(0, slots, 2):
        left_h, left_l = split(jnp.concatenate([left_ref[s], left_ref[s + 1]], axis=1))
        both = dot(field_h, left_h) + dot(field_l, left_h) + dot(field_h, left_l)
        for k in range(2):
            target = src_ref[p, s + k]

            @pl.when(target >= 0)
            def _():
                coef_h, coef_l = split(pair_coef(both[:, k * width : (k + 1) * width], rank))
                right_h, right_l = split(right_ref[0, s + k])
                value = dot(
                    jnp.concatenate([coef_h, coef_l], axis=1),
                    jnp.concatenate([right_h, right_h], axis=1),
                    NT_DIMS,
                ) + dot(coef_h, right_l, NT_DIMS)
                step = lax.rem(target // 2 - me // 2 + 4, 4)
                mine = lax.rem(target, 2) == lax.rem(me, 2)

                @pl.when(mine)
                def _():
                    own_ref[step] += value

                @pl.when(jnp.logical_not(mine))
                def _():
                    other_ref[step] += value


def sum_kernel(a_ref, b_ref, c_ref, d_ref, out_ref):
    total = (a_ref[...] + b_ref[...]) + (c_ref[...] + d_ref[...])
    rows, cols = total.shape
    lanes = cols // 2
    half = total.reshape(2, rows // 16, 8, cols)
    for c in range(2):
        left, right = half[c, :, :, :lanes], half[c, :, :, lanes:]
        low = lax.broadcasted_iota(jnp.int32, left.shape, 1) < 4
        even = jnp.where(low, left, pltpu.roll(right, 4, 1))
        odd = jnp.where(low, pltpu.roll(left, 4, 1), right)
        out_ref[:, 8 * c : 8 * c + 8, :] = jnp.stack([even, odd], axis=1).reshape(rows // 8, 8, lanes)


def gate_kernel(me_ref, x_ref, onset_ref, into_ref, outof_ref, y_ref):
    group = onset_ref.shape[0]
    lanes = x_ref.shape[1]
    bands = outof_ref.shape[0] // 2
    for v in range(group):
        picks = [pl.ds(h * group + v, bands, stride=2 * group) for h in range(2)]
        high, low = split(jnp.concatenate([x_ref[pick, :] for pick in picks], axis=1))
        traces = dot(into_ref[...], jnp.concatenate([high, high, low], axis=0))
        when = lax.broadcasted_iota(jnp.int32, traces.shape, 0)
        gated = jnp.where(when < onset_ref[v : v + 1, :], traces, 0.0)
        high, low = split(gated)
        pair = dot(outof_ref[...], high)
        back = pair[:bands] + pair[bands:] + dot(outof_ref[:bands, :], low)
        for h in range(2):
            y_ref[picks[h], :] = back[:, h * lanes : (h + 1) * lanes]


def forward_kernel(src_ref, me_ref, *refs):
    tile_refs, (left_ref, right_ref, direct_ref, out_ref, high_ref, low_ref, coef_h, coef_l) = refs[:8], refs[8:]
    p = pl.program_id(0)
    slots, tile, width = left_ref.shape
    rank = width // 2
    me = me_ref[0]

    @pl.when(p == 0)
    def _():
        for i in range(8):
            count, _, lanes = tile_refs[i].shape
            block = tile_refs[i][...].reshape(count // 2, 2, 2, 8, lanes)
            parts = []
            for c in range(2):
                even, odd = block[:, 0, c], block[:, 1, c]
                low = lax.broadcasted_iota(jnp.int32, even.shape, 1) < 4
                first = jnp.where(low, even, pltpu.roll(odd, 4, 1)).reshape(count * 4, lanes)
                second = jnp.where(low, pltpu.roll(even, 4, 1), odd).reshape(count * 4, lanes)
                parts.append(jnp.concatenate([first, second], axis=1))
            h, l = split(jnp.concatenate(parts, axis=0))
            high_ref[i] = h
            low_ref[i] = l

    for s in range(slots):
        source = src_ref[p, s]
        lanes = slice(s * width, (s + 1) * width)

        @pl.when(source >= 0)
        def _():
            step = lax.rem(source // 2 - me // 2 + 4, 4)
            place = step + jnp.where(lax.rem(source, 2) == lax.rem(me, 2), 0, 4)
            right_h, right_l = split(right_ref[0, s])
            high = high_ref[place]
            pair = dot(high, jnp.concatenate([right_h, right_l], axis=1))
            products = pair[:, :width] + pair[:, width:] + dot(low_ref[place], right_h)
            h, l = split(pair_coef(products, rank))
            coef_h[:, lanes] = h
            coef_l[:, lanes] = l

        @pl.when(source < 0)
        def _():
            coef_h[:, lanes] = jnp.zeros((coef_h.shape[0], width), BF16)
            coef_l[:, lanes] = jnp.zeros((coef_l.shape[0], width), BF16)

    left_h, left_l = split(jnp.concatenate([left_ref[s] for s in range(slots)], axis=1))
    high = coef_h[...]
    result = dot(high, left_h, NT_DIMS) + dot(coef_l[...], left_h, NT_DIMS) + dot(high, left_l, NT_DIMS)
    out_ref[...] = direct_ref[...] - result.reshape(out_ref.shape)


def time_tables(count):
    times = np.arange(T_USED, dtype=np.int64)
    phase = (np.arange(count, dtype=np.int64) + FIRST_BIN)[None, :] * times[:, None] % NT
    angle = 2.0 * math.pi / NT * phase
    waves = np.stack([np.cos(angle), -np.sin(angle)], axis=2).reshape(T_USED, 2 * count)

    def parts(x):
        high = x.astype(ml_dtypes.bfloat16)
        return high, (x - high.astype(np.float64)).astype(ml_dtypes.bfloat16)

    high, low = parts(waves / math.sqrt(count))
    into = np.concatenate([high, low, high], axis=1)
    high, low = parts(waves.T / math.sqrt(NT))
    return into, np.concatenate([high, low], axis=0)


def shards(wavefield, direct, left_factors, right_factors, tile_src, onset):
    panels, slots = tile_src.shape
    tile, width = right_factors.shape[3:]
    virtual = wavefield.shape[2]
    rows = 2 * virtual
    mib = 1024 * 1024
    left = jnp.transpose(left_factors[0], (1, 0, 2))
    right = right_factors[0]
    me = lax.axis_index("panel").astype(jnp.int32)[None]
    count = lax.axis_size("freq")
    group = virtual // count

    left_spec = pl.BlockSpec((slots, tile, width), lambda p, *_: (0, p, 0))
    right_spec = pl.BlockSpec((1, slots, tile, width), lambda p, *_: (p, 0, 0, 0))
    field_spec = pl.BlockSpec((2, virtual, tile), lambda p, *_: (0, 0, p))
    sums_spec = pl.BlockSpec((4, rows, tile), lambda p, *_: (0, 0, 0))
    sums_type = jax.ShapeDtypeStruct((4, rows, tile), F32)
    own, other = pl.pallas_call(
        adjoint_kernel,
        grid_spec=pltpu.PrefetchScalarGridSpec(
            num_scalar_prefetch=2,
            grid=(panels,),
            in_specs=[field_spec, left_spec, right_spec],
            out_specs=[sums_spec, sums_spec],
        ),
        out_shape=[sums_type, sums_type],
        compiler_params=pltpu.CompilerParams(vmem_limit_bytes=20 * mib),
        name="adjoint",
    )(tile_src, me, wavefield[0], left, right)

    swap = [(i, i ^ 1) for i in range(8)]

    def shift(x, by):
        return lax.ppermute(x, "panel", [(i, (i + 2 * by) % 8) for i in range(8)])

    summed = own + lax.ppermute(other, "panel", swap)
    parts = [summed[0]] + [shift(summed[b], b) for b in range(1, 4)]
    moved = pl.pallas_call(
        sum_kernel,
        out_shape=jax.ShapeDtypeStruct((count, 4 * group, tile // 2), F32),
        compiler_params=pltpu.CompilerParams(vmem_limit_bytes=4 * mib),
        name="panel_sum",
    )(*parts)
    moved = lax.all_to_all(moved, "freq", split_axis=0, concat_axis=0, tiled=True)

    into, outof = time_tables(count)
    whole = lambda shape: pl.BlockSpec(shape, lambda i, *_: (0,) * len(shape))
    gated = pl.pallas_call(
        gate_kernel,
        grid_spec=pltpu.PrefetchScalarGridSpec(
            num_scalar_prefetch=1,
            grid=(1,),
            in_specs=[
                whole((2 * rows, tile // 2)),
                pl.BlockSpec((group, tile), lambda i, me_ref: (0, me_ref[0])),
                whole(into.shape),
                whole(outof.shape),
            ],
            out_specs=whole((2 * rows, tile // 2)),
        ),
        out_shape=jax.ShapeDtypeStruct((2 * rows, tile // 2), F32),
        compiler_params=pltpu.CompilerParams(vmem_limit_bytes=12 * mib),
        name="gate",
    )(me, moved.reshape(2 * rows, tile // 2), onset, jnp.asarray(into), jnp.asarray(outof))
    back = lax.all_to_all(gated.reshape(count, 4 * group, tile // 2), "freq", split_axis=0, concat_axis=0, tiled=True)

    tiles = [back] + [shift(back, -b) for b in range(1, 4)]
    tiles = tiles + [lax.ppermute(t, "panel", swap) for t in tiles]
    tile_spec = whole((count, 4 * group, tile // 2))
    return pl.pallas_call(
        forward_kernel,
        grid_spec=pltpu.PrefetchScalarGridSpec(
            num_scalar_prefetch=2,
            grid=(panels,),
            in_specs=[tile_spec] * 8 + [left_spec, right_spec, field_spec],
            out_specs=field_spec,
            scratch_shapes=[
                pltpu.VMEM((8, rows, tile), BF16),
                pltpu.VMEM((8, rows, tile), BF16),
                pltpu.VMEM((rows, slots * width), BF16),
                pltpu.VMEM((rows, slots * width), BF16),
            ],
        ),
        out_shape=jax.ShapeDtypeStruct(direct.shape[1:], F32),
        compiler_params=pltpu.CompilerParams(vmem_limit_bytes=24 * mib),
        name="forward",
    )(tile_src, me, *tiles, left, right, direct[0])[None]


def solution(mesh):
    in_specs = (
        P("freq", None, None, "panel"),
        P("freq", None, None, "panel"),
        P("freq", "panel", None, None),
        P("freq", "panel", None, None, None),
        P("panel", None),
        P("freq", None),
    )
    out_specs = P("freq", None, None, "panel")
    return jax.shard_map(shards, mesh=mesh, in_specs=in_specs, out_specs=out_specs, check_vma=False)
```

profile of v0, /device:TPU:1, one launch (start us, length us, event | category | flops | bytes accessed | tf_op | source)
XLA Modules:
  0.0 104.3 jit_solution(7636348213903669779)
XLA Ops:
  0.0 1.9 %copy-done = f32[1,1024,6,128]{3,1,2,0:T(8,128)S(1)} copy-done((f32[1,1024,6,128]{3,1,2,0:T(8,128)S(1)}, f32[1,1024,6,128]{3,1,2,0:T(8,128)}, u32[]{:S(2)}) %copy-start) | copy-done | bytes 3145752
  1.9 1.9 %copy-done.2 = f32[1,4,6,256,128]{4,3,2,1,0:T(8,128)S(1)} copy-done((f32[1,4,6,256,128]{4,3,2,1,0:T(8,128)S(1)}, f32[1,4,6,256,128]{4,3,2,1,0:T(8,128)}, u32[]{:S(2)}) %copy-start.2) | copy-done | bytes 3145752
  3.8 1.2 %copy-done.5 = f32[1,2,128,1024]{3,2,1,0:T(8,128)S(1)} copy-done((f32[1,2,128,1024]{3,2,1,0:T(8,128)S(1)}, f32[1,2,128,1024]{3,2,1,0:T(8,128)}, u32[]{:S(2)}) %copy-start.5) | copy-done | bytes 1048600
  5.0 0.7 copy-done.9
  5.7 10.2 %adjoint.1 = (f32[4,256,256]{2,1,0:T(8,128)S(1)}, f32[4,256,256]{2,1,0:T(8,128)S(1)}) custom-call(s32[4,6]{1,0:T(4,128)S(1)} %copy-done.9, s32[1]{0:T(128)} %bitcast.me_ref, f32[2,128,1024]{2,1,0:T(8,128)S(1)} %bitcast.25, f32[6,1024,128]{2,1,0:T(8,128)S(1)} %bitcast.18, f32[4,6,256,128]{3,2,1,0:T(8,128)S(1)} %bitcast.20), custom_call_target="tpu_custom_call" | custom-call | tf_op jit(solution)/shard_map/adjoint/pallas_call | solution.py:195
  15.9 2.1 %collective-permute-start = (f32[4,256,256]{2,1,0:T(8,128)S(1)}, f32[4,256,256]{2,1,0:T(8,128)S(1)}, u32[]{:S(2)}, u32[]{:S(2)}) collective-permute-start(f32[4,256,256]{2,1,0:T(8,128)S(1)} %get-tuple-element.8), channel_id=1, source_target_pairs={{0,1},{1,0},{2,3},{3,2},{4,5},{5,4},{6,7},{7,6},{8,9},{9,8},{10,11... | collective-permute-start | bytes 3145736 | tf_op jit(solution)/shard_map/ppermute | solution.py:213
  18.0 2.3 %collective-permute-done = f32[4,256,256]{2,1,0:T(8,128)S(1)} collective-permute-done((f32[4,256,256]{2,1,0:T(8,128)S(1)}, f32[4,256,256]{2,1,0:T(8,128)S(1)}, u32[]{:S(2)}, u32[]{:S(2)}) %collective-permute-start) | collective-permute-done | bytes 1048608 | tf_op jit(solution)/shard_map/ppermute | solution.py:213
  20.6 2.6 %collective-permute-start.3 = (f32[256,256]{1,0:T(8,128)S(1)}, f32[256,256]{1,0:T(8,128)S(1)}, u32[]{:S(2)}, u32[]{:S(2)}) collective-permute-start(f32[256,256]{1,0:T(8,128)S(1)} %get-tuple-element.9), channel_id=1, source_target_pairs={{0,6},{1,7},{2,0},{3,1},{4,2},{5,3},{6,4},{7,5},{8,14},{9,15},{10,... | collective-permute-start | bytes 786440 | tf_op jit(solution)/shard_map/ppermute | solution.py:211
  23.2 0.7 collective-permute-start.1
  23.9 10.1 %collective-permute-done.3.d_ref = f32[256,256]{1,0:T(8,128)S(1)} collective-permute-done((f32[256,256]{1,0:T(8,128)S(1)}, f32[256,256]{1,0:T(8,128)S(1)}, u32[]{:S(2)}, u32[]{:S(2)}) %collective-permute-start.3) | collective-permute-done | bytes 262176 | tf_op jit(solution)/shard_map/ppermute | solution.py:211
  34.0 4.0 %collective-permute-done.1.b_ref = f32[256,256]{1,0:T(8,128)S(1)} collective-permute-done((f32[256,256]{1,0:T(8,128)S(1)}, f32[256,256]{1,0:T(8,128)S(1)}, u32[]{:S(2)}, u32[]{:S(2)}) %collective-permute-start.1) | collective-permute-done | bytes 262176 | tf_op jit(solution)/shard_map/ppermute | solution.py:211
  38.1 22.0 %all_to_all.10 = f32[32,16,128]{2,1,0:T(8,128)S(1)} all-to-all(f32[32,16,128]{2,1,0:T(8,128)S(1)} %panel_sum.1), channel_id=1, replica_groups=mesh['freq'=32,'panel'=8] {'freq'}, dimensions={0} | all-to-all | bytes 524288 | tf_op jit(solution)/shard_map/all_to_all | solution.py:221
  60.1 1.6 %gate.1 = f32[512,128]{1,0:T(8,128)S(1)} custom-call(s32[1]{0:T(128)} %bitcast.me_ref, f32[512,128]{1,0:T(8,128)S(1)} %bitcast.23, s32[4,2048]{1,0:T(4,128)S(1)} %copy-done.8, bf16[896,192]{1,0:T(8,128)(2,1)S(1)} %copy-done.6, bf16[128,896]{1,0:T(8,128)(2,1)S(1)} %copy-done.7), custom_call_target="tpu_custom_call" | custom-call | tf_op jit(solution)/shard_map/gate/pallas_call | solution.py:225
  61.8 14.9 %all_to_all.11.refs_0_ = f32[32,16,128]{2,1,0:T(8,128)S(1)} all-to-all(f32[32,16,128]{2,1,0:T(8,128)S(1)} %bitcast.24), channel_id=1, replica_groups=mesh['freq'=32,'panel'=8] {'freq'}, dimensions={0} | all-to-all | bytes 524288 | tf_op jit(solution)/shard_map/all_to_all | solution.py:242
  76.7 0.7 collective-permute-start.5
  77.4 2.1 %collective-permute-start.4 = (f32[32,16,128]{2,1,0:T(8,128)S(1)}, f32[32,16,128]{2,1,0:T(8,128)S(1)}, u32[]{:S(2)}, u32[]{:S(2)}) collective-permute-start(f32[32,16,128]{2,1,0:T(8,128)S(1)} %all_to_all.11.refs_0_), channel_id=1, source_target_pairs={{0,6},{1,7},{2,0},{3,1},{4,2},{5,3},{6,4},{7,5},{8,14},{9,15},{10,... | collective-permute-start | bytes 786440 | tf_op jit(solution)/shard_map/ppermute | solution.py:211
  79.5 4.5 %collective-permute-start.7 = (f32[32,16,128]{2,1,0:T(8,128)S(1)}, f32[32,16,128]{2,1,0:T(8,128)S(1)}, u32[]{:S(2)}, u32[]{:S(2)}) collective-permute-start(f32[32,16,128]{2,1,0:T(8,128)S(1)} %all_to_all.11.refs_0_), channel_id=1, source_target_pairs={{0,1},{1,0},{2,3},{3,2},{4,5},{5,4},{6,7},{7,6},{8,9},{9,8},{10,11... | collective-permute-start | bytes 786440 | tf_op jit(solution)/shard_map/ppermute | solution.py:245
  84.0 2.9 %collective-permute-done.6.refs_3_ = f32[32,16,128]{2,1,0:T(8,128)S(1)} collective-permute-done((f32[32,16,128]{2,1,0:T(8,128)S(1)}, f32[32,16,128]{2,1,0:T(8,128)S(1)}, u32[]{:S(2)}, u32[]{:S(2)}) %collective-permute-start.6) | collective-permute-done | bytes 262176 | tf_op jit(solution)/shard_map/ppermute | solution.py:211
  87.0 5.3 %collective-permute-start.10 = (f32[32,16,128]{2,1,0:T(8,128)S(1)}, f32[32,16,128]{2,1,0:T(8,128)S(1)}, u32[]{:S(2)}, u32[]{:S(2)}) collective-permute-start(f32[32,16,128]{2,1,0:T(8,128)S(1)} %collective-permute-done.6.refs_3_), channel_id=1, source_target_pairs={{0,1},{1,0},{2,3},{3,2},{4,5},{5,4},{6,7},{7,6},{8,9},{9,8},{10,11... | collective-permute-start | bytes 786440 | tf_op jit(solution)/shard_map/ppermute | solution.py:245
  92.3 0.7 collective-permute-start.8
  92.9 0.5 collective-permute-done.10.refs_7_
  93.4 0.4 collective-permute-done.9.refs_6_
  93.8 0.4 collective-permute-done.8.refs_5_
  94.2 10.1 %forward.1 = f32[2,128,1024]{2,1,0:T(8,128)} custom-call(s32[4,6]{1,0:T(4,128)S(1)} %copy-done.10, s32[1]{0:T(128)} %bitcast.me_ref, f32[32,16,128]{2,1,0:T(8,128)S(1)} %all_to_all.11.refs_0_, f32[32,16,128]{2,1,0:T(8,128)S(1)} %collective-permute-done.4.refs_1_, f32[32,16,128]{2,1,0:T(8,128)S(1)} %collective-permute-done.5.refs_2_, ...), custom_call_target="tpu_custom_call" | custom-call | tf_op jit(solution)/shard_map/forward/pallas_call | solution.py:247
  (28 shorter events, 0.4 us)
Async XLA Ops:
  0.0 1.9 %copy-start = (f32[1,1024,6,128]{3,1,2,0:T(8,128)S(1)}, f32[1,1024,6,128]{3,1,2,0:T(8,128)}, u32[]{:S(2)}) copy-start(f32[1,1024,6,128]{3,1,2,0:T(8,128)} %param.10) | copy-start | bytes 9437188
  1.9 1.9 %copy-start.2 = (f32[1,4,6,256,128]{4,3,2,1,0:T(8,128)S(1)}, f32[1,4,6,256,128]{4,3,2,1,0:T(8,128)}, u32[]{:S(2)}) copy-start(f32[1,4,6,256,128]{4,3,2,1,0:T(8,128)} %param.11) | copy-start | bytes 9437188
  3.8 1.2 %copy-start.5 = (f32[1,2,128,1024]{3,2,1,0:T(8,128)S(1)}, f32[1,2,128,1024]{3,2,1,0:T(8,128)}, u32[]{:S(2)}) copy-start(f32[1,2,128,1024]{3,2,1,0:T(8,128)} %param.8) | copy-start | bytes 3145732
  5.0 0.7 copy-start.9
  15.9 4.4 %collective-permute-start = (f32[4,256,256]{2,1,0:T(8,128)S(1)}, f32[4,256,256]{2,1,0:T(8,128)S(1)}, u32[]{:S(2)}, u32[]{:S(2)}) collective-permute-start(f32[4,256,256]{2,1,0:T(8,128)S(1)} %get-tuple-element.8), channel_id=1, source_target_pairs={{0,1},{1,0},{2,3},{3,2},{4,5},{5,4},{6,7},{7,6},{8,9},{9,8},{10,11... | collective-permute-start | bytes 3145736 | tf_op jit(solution)/shard_map/ppermute | solution.py:213
  20.3 39.8 %copy-start.6 = (bf16[896,192]{1,0:T(8,128)(2,1)S(1)}, bf16[896,192]{1,0:T(8,128)(2,1)}, u32[]{:S(2)}) copy-start(bf16[896,192]{1,0:T(8,128)(2,1)} %constant.8.clone.into_ref) | copy-start | bytes 1032196
  20.3 39.8 %copy-start.7 = (bf16[128,896]{1,0:T(8,128)(2,1)S(1)}, bf16[128,896]{1,0:T(8,128)(2,1)}, u32[]{:S(2)}) copy-start(bf16[128,896]{1,0:T(8,128)(2,1)} %constant.9.clone.outof_ref) | copy-start | bytes 688132
  20.3 39.8 %copy-start.8 = (s32[4,2048]{1,0:T(4,128)S(1)}, s32[4,2048]{1,0:T(4,128)}, u32[]{:S(2)}) copy-start(s32[4,2048]{1,0:T(4,128)} %onset_ref.1) | copy-start | bytes 98308
  20.3 73.8 %copy-start.3 = (f32[1,4,6,256,128]{4,3,2,1,0:T(8,128)S(1)}, f32[1,4,6,256,128]{4,3,2,1,0:T(8,128)}, u32[]{:S(2)}) copy-start(f32[1,4,6,256,128]{4,3,2,1,0:T(8,128)} %param.11) | copy-start | bytes 9437188
  20.5 73.7 %copy-start.1 = (f32[1,1024,6,128]{3,1,2,0:T(8,128)S(1)}, f32[1,1024,6,128]{3,1,2,0:T(8,128)}, u32[]{:S(2)}) copy-start(f32[1,1024,6,128]{3,1,2,0:T(8,128)} %param.10) | copy-start | bytes 9437188
  20.5 73.6 %copy-start.4 = (f32[1,2,128,1024]{3,2,1,0:T(8,128)S(1)}, f32[1,2,128,1024]{3,2,1,0:T(8,128)}, u32[]{:S(2)}) copy-start(f32[1,2,128,1024]{3,2,1,0:T(8,128)} %param.9) | copy-start | bytes 3145732
  20.5 73.6 %copy-start.10 = (s32[4,6]{1,0:T(4,128)S(1)}, s32[4,6]{1,0:T(4,128)}, u32[]{:S(2)}) copy-start(s32[4,6]{1,0:T(4,128)} %src_ref.3) | copy-start | bytes 292
  20.6 13.4 %collective-permute-start.3 = (f32[256,256]{1,0:T(8,128)S(1)}, f32[256,256]{1,0:T(8,128)S(1)}, u32[]{:S(2)}, u32[]{:S(2)}) collective-permute-start(f32[256,256]{1,0:T(8,128)S(1)} %get-tuple-element.9), channel_id=1, source_target_pairs={{0,6},{1,7},{2,0},{3,1},{4,2},{5,3},{6,4},{7,5},{8,14},{9,15},{10,... | collective-permute-start | bytes 786440 | tf_op jit(solution)/shard_map/ppermute | solution.py:211
  23.2 10.8 %collective-permute-start.2 = (f32[256,256]{1,0:T(8,128)S(1)}, f32[256,256]{1,0:T(8,128)S(1)}, u32[]{:S(2)}, u32[]{:S(2)}) collective-permute-start(f32[256,256]{1,0:T(8,128)S(1)} %get-tuple-element.10), channel_id=1, source_target_pairs={{0,4},{1,5},{2,6},{3,7},{4,0},{5,1},{6,2},{7,3},{8,12},{9,13},{10,... | collective-permute-start | bytes 786440 | tf_op jit(solution)/shard_map/ppermute | solution.py:211
  23.2 14.7 %collective-permute-start.1 = (f32[256,256]{1,0:T(8,128)S(1)}, f32[256,256]{1,0:T(8,128)S(1)}, u32[]{:S(2)}, u32[]{:S(2)}) collective-permute-start(f32[256,256]{1,0:T(8,128)S(1)} %get-tuple-element.11), channel_id=1, source_target_pairs={{0,2},{1,3},{2,4},{3,5},{4,6},{5,7},{6,0},{7,1},{8,10},{9,11},{10,... | collective-permute-start | bytes 786440 | tf_op jit(solution)/shard_map/ppermute | solution.py:211
  76.7 10.3 %collective-permute-start.6 = (f32[32,16,128]{2,1,0:T(8,128)S(1)}, f32[32,16,128]{2,1,0:T(8,128)S(1)}, u32[]{:S(2)}, u32[]{:S(2)}) collective-permute-start(f32[32,16,128]{2,1,0:T(8,128)S(1)} %all_to_all.11.refs_0_), channel_id=1, source_target_pairs={{0,2},{1,3},{2,4},{3,5},{4,6},{5,7},{6,0},{7,1},{8,10},{9,11},{10,... | collective-permute-start | bytes 786440 | tf_op jit(solution)/shard_map/ppermute | solution.py:211
  76.7 15.6 %collective-permute-start.5 = (f32[32,16,128]{2,1,0:T(8,128)S(1)}, f32[32,16,128]{2,1,0:T(8,128)S(1)}, u32[]{:S(2)}, u32[]{:S(2)}) collective-permute-start(f32[32,16,128]{2,1,0:T(8,128)S(1)} %all_to_all.11.refs_0_), channel_id=1, source_target_pairs={{0,4},{1,5},{2,6},{3,7},{4,0},{5,1},{6,2},{7,3},{8,12},{9,13},{10,... | collective-permute-start | bytes 786440 | tf_op jit(solution)/shard_map/ppermute | solution.py:211
  77.4 14.8 %collective-permute-start.4 = (f32[32,16,128]{2,1,0:T(8,128)S(1)}, f32[32,16,128]{2,1,0:T(8,128)S(1)}, u32[]{:S(2)}, u32[]{:S(2)}) collective-permute-start(f32[32,16,128]{2,1,0:T(8,128)S(1)} %all_to_all.11.refs_0_), channel_id=1, source_target_pairs={{0,6},{1,7},{2,0},{3,1},{4,2},{5,3},{6,4},{7,5},{8,14},{9,15},{10,... | collective-permute-start | bytes 786440 | tf_op jit(solution)/shard_map/ppermute | solution.py:211
  79.5 13.4 %collective-permute-start.7 = (f32[32,16,128]{2,1,0:T(8,128)S(1)}, f32[32,16,128]{2,1,0:T(8,128)S(1)}, u32[]{:S(2)}, u32[]{:S(2)}) collective-permute-start(f32[32,16,128]{2,1,0:T(8,128)S(1)} %all_to_all.11.refs_0_), channel_id=1, source_target_pairs={{0,1},{1,0},{2,3},{3,2},{4,5},{5,4},{6,7},{7,6},{8,9},{9,8},{10,11... | collective-permute-start | bytes 786440 | tf_op jit(solution)/shard_map/ppermute | solution.py:245
  87.0 6.4 %collective-permute-start.10 = (f32[32,16,128]{2,1,0:T(8,128)S(1)}, f32[32,16,128]{2,1,0:T(8,128)S(1)}, u32[]{:S(2)}, u32[]{:S(2)}) collective-permute-start(f32[32,16,128]{2,1,0:T(8,128)S(1)} %collective-permute-done.6.refs_3_), channel_id=1, source_target_pairs={{0,1},{1,0},{2,3},{3,2},{4,5},{5,4},{6,7},{7,6},{8,9},{9,8},{10,11... | collective-permute-start | bytes 786440 | tf_op jit(solution)/shard_map/ppermute | solution.py:245
  92.3 1.5 %collective-permute-start.9 = (f32[32,16,128]{2,1,0:T(8,128)S(1)}, f32[32,16,128]{2,1,0:T(8,128)S(1)}, u32[]{:S(2)}, u32[]{:S(2)}) collective-permute-start(f32[32,16,128]{2,1,0:T(8,128)S(1)} %collective-permute-done.5.refs_2_), channel_id=1, source_target_pairs={{0,1},{1,0},{2,3},{3,2},{4,5},{5,4},{6,7},{7,6},{8,9},{9,8},{10,11... | collective-permute-start | bytes 786440 | tf_op jit(solution)/shard_map/ppermute | solution.py:245
  92.3 1.9 %collective-permute-start.8 = (f32[32,16,128]{2,1,0:T(8,128)S(1)}, f32[32,16,128]{2,1,0:T(8,128)S(1)}, u32[]{:S(2)}, u32[]{:S(2)}) collective-permute-start(f32[32,16,128]{2,1,0:T(8,128)S(1)} %collective-permute-done.4.refs_1_), channel_id=1, source_target_pairs={{0,1},{1,0},{2,3},{3,2},{4,5},{5,4},{6,7},{7,6},{8,9},{9,8},{10,11... | collective-permute-start | bytes 786440 | tf_op jit(solution)/shard_map/ppermute | solution.py:245
where the time goes:
time: 105 us; the launch traced here: 104 us
  blocking collectives  37 us (35%)
  Pallas kernels  22 us (21%)
  waiting for transfers between devices  20.6 us (20%)
  starting transfers between devices  18.7 us (18%)
  local copies, waits for them, and re-layouts  5.79 us (6%)
    all_to_all x1, blocking collectives, shards(): lax.all_to_all(moved, 'freq', split_axis=0, concat_axis=0, tiled=True)  22 us
    ppermute x6, waiting for transfers between devices, shift(): return lax.ppermute(x, 'panel', [(i, (i + 2 * by) % 8) for i in range(8)])  17 us
    all_to_all x1, blocking collectives, shards(): lax.all_to_all(gated.reshape(count, 4 * group, tile // 2), 'freq', split_...  14.9 us
    ppermute x4, starting transfers between devices, shards(): tiles = tiles + [lax.ppermute(t, 'panel', swap) for t in tiles]  10.5 us
    pallas_call x1, Pallas kernels, shards(): pl.pallas_call(adjoint_kernel, grid_spec=pltpu.PrefetchScalarGridSpec(num...  10.2 us
    pallas_call x1, Pallas kernels, shards(): pl.pallas_call(forward_kernel, grid_spec=pltpu.PrefetchScalarGridSpec(num...  10.1 us
    ppermute x6, starting transfers between devices, shift(): return lax.ppermute(x, 'panel', [(i, (i + 2 * by) % 8) for i in range(8)])  6.07 us
    unnamed x22, local copies, waits for them, and re-layouts  5.71 us
  transfers between devices with their start and end apart: 11, of which 7 were waited for; matrix products, arithmetic and copies ran while one was open for 0% of the time, Pallas kernels for 0%

commit v1 on v0

v1 whole, which is shorter than its diff:
```python
import functools
import math

import jax
import jax.numpy as jnp
import ml_dtypes
import numpy as np
from jax import lax
from jax.experimental import pallas as pl
from jax.experimental.pallas import tpu as pltpu
from jax.sharding import PartitionSpec as P

NT = 1024
FIRST_BIN = 8
T_USED = 896

F32 = jnp.float32
BF16 = jnp.bfloat16
NN = (((1,), (0,)), ((), ()))
NT_DIMS = (((1,), (1,)), ((), ()))


def split(x):
    high = x.astype(BF16)
    low = (x - high.astype(F32)).astype(BF16)
    return high, low


def dot(a, b, dims=NN):
    return lax.dot_general(a, b, dims, preferred_element_type=F32)


def pair_coef(products, rank):
    half = products.shape[0] // 2
    real, imag = products[:half], products[half:]
    lane = lax.broadcasted_iota(jnp.int32, real.shape, 1)
    sign = jnp.where(lane < rank, 1.0, -1.0).astype(F32)
    first = real + sign * pltpu.roll(imag, rank, 1)
    second = imag - sign * pltpu.roll(real, rank, 1)
    return jnp.concatenate([first, second], axis=0)


def find_slot(src_ref, panel, target, slots):
    slot, found = jnp.int32(0), jnp.int32(0)
    for s in range(slots):
        hit = src_ref[panel, s] == target
        slot = jnp.where(hit, s, slot)
        found = jnp.where(hit, 1, found)
    return slot, jnp.where(found > 0, panel * slots + slot, src_ref.shape[0] * slots)


def tile_of(me, step, other):
    return lax.rem(me // 2 + step, 4) * 2 + lax.rem(me + other, 2)


def spread(src_ref, me, other, coef_h, coef_l, right_ref, out_ref):
    width = coef_h.shape[2]
    for step in range(out_ref.shape[0]):
        target = tile_of(me, step, other)
        parts = []
        for p in range(src_ref.shape[0]):
            _, at = find_slot(src_ref, p, target, src_ref.shape[1])
            parts.append((coef_h[at], coef_l[at], right_ref[at, :, :width], right_ref[at, :, width:]))
        high, low, right_h, right_l = (jnp.concatenate(x, axis=1) for x in zip(*parts))
        out_ref[step] = dot(high, right_h, NT_DIMS) + dot(low, right_h, NT_DIMS) + dot(high, right_l, NT_DIMS)


def adjoint_kernel(
    me_ref, src_hbm, field_hbm, left_hbm, right_hbm,
    coef_h, coef_l, right_ref, left_ref, out_ref,
    src_ref, field_ref, raw_ref, sems,
):
    panels, slots, tile, width = left_ref.shape
    copies = []
    for p in range(panels):
        at = pl.ds(p * tile, tile)
        copies.append(
            (
                pltpu.make_async_copy(field_hbm.at[:, :, at], field_ref.at[p], sems.at[0, p]),
                pltpu.make_async_copy(left_hbm.at[:, at, :], left_ref.at[p], sems.at[1, p]),
            )
        )
    rights = [pltpu.make_async_copy(right_hbm.at[p], raw_ref.at[p], sems.at[2, p]) for p in range(panels)]
    names = pltpu.make_async_copy(src_hbm, src_ref, sems.at[3, 0])
    for pair in copies:
        pair[0].start()
        pair[1].start()
    for copy in rights:
        copy.start()
    names.start()
    last = panels * slots
    coef_h[last] = jnp.zeros(coef_h.shape[1:], BF16)
    coef_l[last] = jnp.zeros(coef_l.shape[1:], BF16)
    right_ref[last] = jnp.zeros(right_ref.shape[1:], BF16)
    for p in range(panels):
        copies[p][0].wait()
        copies[p][1].wait()
        field_h, field_l = split(field_ref[p].reshape(-1, tile))
        for s in range(0, slots, 2):
            left_h, left_l = split(jnp.concatenate([left_ref[p, s], left_ref[p, s + 1]], axis=1))
            both = dot(field_h, left_h) + dot(field_l, left_h) + dot(field_h, left_l)
            for k in range(2):
                high, low = split(pair_coef(both[:, k * width : (k + 1) * width], width // 2))
                coef_h[p * slots + s + k] = high
                coef_l[p * slots + s + k] = low
    for p in range(panels):
        rights[p].wait()
        for s in range(slots):
            right_ref[p * slots + s] = jnp.concatenate(split(raw_ref[p, s]), axis=1)
    names.wait()
    spread(src_ref, me_ref[0], 1, coef_h, coef_l, right_ref, out_ref)


def own_kernel(src_ref, me_ref, coef_h, coef_l, right_ref, left_ref, out_ref, left_h, left_l):
    spread(src_ref, me_ref[0], 0, coef_h, coef_l, right_ref, out_ref)
    for p in range(left_ref.shape[0]):
        for s in range(left_ref.shape[1]):
            left_h[p, s], left_l[p, s] = split(left_ref[p, s])


def sum_kernel(a_ref, b_ref, c_ref, d_ref, out_ref):
    total = (a_ref[...] + b_ref[...]) + (c_ref[...] + d_ref[...])
    rows, cols = total.shape
    lanes = cols // 2
    half = total.reshape(2, rows // 16, 8, cols)
    for c in range(2):
        left, right = half[c, :, :, :lanes], half[c, :, :, lanes:]
        low = lax.broadcasted_iota(jnp.int32, left.shape, 1) < 4
        even = jnp.where(low, left, pltpu.roll(right, 4, 1))
        odd = jnp.where(low, pltpu.roll(left, 4, 1), right)
        out_ref[:, 8 * c : 8 * c + 8, :] = jnp.stack([even, odd], axis=1).reshape(rows // 8, 8, lanes)


def gate_kernel(me_ref, x_ref, onset_ref, into_ref, outof_ref, y_ref):
    group = onset_ref.shape[0]
    lanes = x_ref.shape[1]
    bands = outof_ref.shape[0] // 2
    for v in range(group):
        picks = [pl.ds(h * group + v, bands, stride=2 * group) for h in range(2)]
        high, low = split(jnp.concatenate([x_ref[pick, :] for pick in picks], axis=1))
        traces = dot(into_ref[...], jnp.concatenate([high, high, low], axis=0))
        when = lax.broadcasted_iota(jnp.int32, traces.shape, 0)
        gated = jnp.where(when < onset_ref[v : v + 1, :], traces, 0.0)
        high, low = split(gated)
        pair = dot(outof_ref[...], high)
        back = pair[:bands] + pair[bands:] + dot(outof_ref[:bands, :], low)
        for h in range(2):
            y_ref[picks[h], :] = back[:, h * lanes : (h + 1) * lanes]


def forward_kernel(step, last, src_ref, me_ref, own_ref, other_ref, left_h, left_l, right_ref, total_ref, out_ref, *scratch):
    panels, slots, tile, width = left_h.shape
    me = me_ref[0]
    tiles = []
    for ref in (own_ref, other_ref):
        count, _, lanes = ref.shape
        block = ref[...].reshape(count // 2, 2, 2, 8, lanes)
        parts = []
        for c in range(2):
            even, odd = block[:, 0, c], block[:, 1, c]
            low = lax.broadcasted_iota(jnp.int32, even.shape, 1) < 4
            first = jnp.where(low, even, pltpu.roll(odd, 4, 1)).reshape(count * 4, lanes)
            second = jnp.where(low, pltpu.roll(even, 4, 1), odd).reshape(count * 4, lanes)
            parts.append(jnp.concatenate([first, second], axis=1))
        tiles.append(split(jnp.concatenate(parts, axis=0)))
    copies = []
    for p in range(panels):
        at = slice(p * tile, (p + 1) * tile)
        parts = []
        for i, (high, low) in enumerate(tiles):
            slot, place = find_slot(src_ref, p, tile_of(me, step, i), slots)
            right = right_ref[place]
            pair = dot(high, right)
            products = pair[:, :width] + pair[:, width:] + dot(low, right[:, :width])
            parts.append(split(pair_coef(products, width // 2)) + (left_h[p, slot], left_l[p, slot]))
        high, low, there_h, there_l = (jnp.concatenate(x, axis=1) for x in zip(*parts))
        result = dot(high, there_h, NT_DIMS) + dot(low, there_h, NT_DIMS) + dot(high, there_l, NT_DIMS)
        result = total_ref[:, :, at] - result.reshape(total_ref.shape[0], total_ref.shape[1], tile)
        if last:
            kept, sems = scratch
            kept[p] = result
            copies.append(pltpu.make_async_copy(kept.at[p], out_ref.at[:, :, pl.ds(p * tile, tile)], sems.at[p]))
            copies[p].start()
        else:
            out_ref[:, :, at] = result
    for copy in copies:
        copy.wait()


def time_tables(count):
    times = np.arange(T_USED, dtype=np.int64)
    phase = (np.arange(count, dtype=np.int64) + FIRST_BIN)[None, :] * times[:, None] % NT
    angle = 2.0 * math.pi / NT * phase
    waves = np.stack([np.cos(angle), -np.sin(angle)], axis=2).reshape(T_USED, 2 * count)

    def parts(x):
        high = x.astype(ml_dtypes.bfloat16)
        return high, (x - high.astype(np.float64)).astype(ml_dtypes.bfloat16)

    high, low = parts(waves / math.sqrt(count))
    into = np.concatenate([high, low, high], axis=1)
    high, low = parts(waves.T / math.sqrt(NT))
    return into, np.concatenate([high, low], axis=0)


def shards(wavefield, direct, left_factors, right_factors, tile_src, onset):
    panels, slots = tile_src.shape
    tile, width = right_factors.shape[3:]
    virtual = wavefield.shape[2]
    rows = 2 * virtual
    mib = 1024 * 1024
    left = jnp.transpose(left_factors[0], (1, 0, 2))
    right = right_factors[0]
    me = lax.axis_index("panel").astype(jnp.int32)[None]
    count = lax.axis_size("freq")
    group = virtual // count

    in_vmem = pl.BlockSpec(memory_space=pltpu.VMEM)
    in_smem = pl.BlockSpec(memory_space=pltpu.SMEM)
    in_hbm = pl.BlockSpec(memory_space=pltpu.HBM)
    hbm = lambda x: pltpu.with_memory_space_constraint(x, pltpu.HBM)
    sums_type = jax.ShapeDtypeStruct((4, rows, tile), F32)
    places = panels * slots + 1
    cost = pl.CostEstimate(flops=3_000_000_000, bytes_accessed=8_000_000, transcendentals=0)
    coef_type = jax.ShapeDtypeStruct((places, rows, width), BF16)
    left_shape = (panels, slots, tile, width)
    coef_h, coef_l, right_kept, left_kept, other = pl.pallas_call(
        adjoint_kernel,
        in_specs=[in_smem] + [in_hbm] * 4,
        out_specs=[in_vmem] * 5,
        out_shape=[
            coef_type,
            coef_type,
            jax.ShapeDtypeStruct((places, tile, 2 * width), BF16),
            jax.ShapeDtypeStruct(left_shape, F32),
            sums_type,
        ],
        scratch_shapes=[
            pltpu.SMEM(tile_src.shape, jnp.int32),
            pltpu.VMEM((panels, 2, virtual, tile), F32),
            pltpu.VMEM((panels, slots, tile, width), F32),
            pltpu.SemaphoreType.DMA((4, panels)),
        ],
        compiler_params=pltpu.CompilerParams(vmem_limit_bytes=28 * mib),
        name="adjoint",
    )(me, hbm(tile_src), hbm(wavefield[0]), hbm(left), hbm(right))
    own, left_h, left_l = pl.pallas_call(
        own_kernel,
        in_specs=[in_smem, in_smem] + [in_vmem] * 4,
        out_specs=[in_vmem] * 3,
        out_shape=[sums_type, jax.ShapeDtypeStruct(left_shape, BF16), jax.ShapeDtypeStruct(left_shape, BF16)],
        compiler_params=pltpu.CompilerParams(vmem_limit_bytes=24 * mib),
        cost_estimate=cost,
        name="own",
    )(tile_src, me, coef_h, coef_l, right_kept, left_kept)

    swap = [(i, i ^ 1) for i in range(8)]

    def shift(x, by):
        return lax.ppermute(x, "panel", [(i, (i + 2 * by) % 8) for i in range(8)])

    summed = own + lax.ppermute(other, "panel", swap)
    parts = [summed[0]] + [shift(summed[b], b) for b in range(1, 4)]
    moved = pl.pallas_call(
        sum_kernel,
        out_shape=jax.ShapeDtypeStruct((count, 4 * group, tile // 2), F32),
        compiler_params=pltpu.CompilerParams(vmem_limit_bytes=4 * mib),
        name="panel_sum",
    )(*parts)
    moved = lax.all_to_all(moved, "freq", split_axis=0, concat_axis=0, tiled=True)

    into, outof = time_tables(count)
    whole = lambda shape: pl.BlockSpec(shape, lambda i, *_: (0,) * len(shape))
    gated = pl.pallas_call(
        gate_kernel,
        grid_spec=pltpu.PrefetchScalarGridSpec(
            num_scalar_prefetch=1,
            grid=(1,),
            in_specs=[
                whole((2 * rows, tile // 2)),
                pl.BlockSpec((group, tile), lambda i, me_ref: (0, me_ref[0])),
                whole(into.shape),
                whole(outof.shape),
            ],
            out_specs=whole((2 * rows, tile // 2)),
        ),
        out_shape=jax.ShapeDtypeStruct((2 * rows, tile // 2), F32),
        compiler_params=pltpu.CompilerParams(vmem_limit_bytes=12 * mib),
        name="gate",
    )(me, moved.reshape(2 * rows, tile // 2), onset, jnp.asarray(into), jnp.asarray(outof))
    back = lax.all_to_all(gated.reshape(count, 4 * group, tile // 2), "freq", split_axis=0, concat_axis=0, tiled=True)

    def exchange(x):
        return lax.ppermute(x, "panel", swap)

    def forward(step, mine, theirs, total, last=False):
        return pl.pallas_call(
            functools.partial(forward_kernel, step, last),
            in_specs=[in_smem, in_smem] + [in_vmem] * 6,
            out_specs=in_hbm if last else in_vmem,
            out_shape=jax.ShapeDtypeStruct(total.shape, F32),
            scratch_shapes=[pltpu.VMEM((panels, 2, virtual, tile), F32), pltpu.SemaphoreType.DMA((panels,))] if last else [],
            compiler_params=pltpu.CompilerParams(vmem_limit_bytes=22 * mib),
            cost_estimate=cost,
            name=f"forward_{step}",
        )(tile_src, me, mine, theirs, left_h, left_l, right_kept, total)

    mine = {step: shift(back, -step) for step in (1, 3, 2)}
    total = forward(0, back, exchange(back), direct[0])
    mine[1], mine[3], total = lax.optimization_barrier((mine[1], mine[3], total))
    theirs = {step: exchange(mine[step]) for step in (1, 3)}
    total = forward(1, mine[1], theirs[1], total)
    mine[2], total = lax.optimization_barrier((mine[2], total))
    theirs[2] = exchange(mine[2])
    total = forward(3, mine[3], theirs[3], total)
    return forward(2, mine[2], theirs[2], total, last=True)[None]


def solution(mesh):
    in_specs = (
        P("freq", None, None, "panel"),
        P("freq", None, None, "panel"),
        P("freq", "panel", None, None),
        P("freq", "panel", None, None, None),
        P("panel", None),
        P("freq", None),
    )
    out_specs = P("freq", None, None, "panel")
    return jax.shard_map(shards, mesh=mesh, in_specs=in_specs, out_specs=out_specs, check_vma=False)
```

time: 105 us -> 96.8 us (0.922)
  local copies, waits for them, and re-layouts: 5.79 us -> 0.1 us
  starting transfers between devices: 18.7 us -> 14.8 us
  waiting for transfers between devices: 20.6 us -> 23.8 us
  Pallas kernels: 22 us -> 20.5 us
    ppermute x6, waiting for transfers between devices: 17 us -> 23.4 us  [shift(): return lax.ppermute(x, 'panel', [(i, (i + 2 * by) % 8) for i in range(8)])]
    unnamed x22 -> x10, local copies, waits for them, and re-layouts: 5.71 us -> 0.02 us
    ppermute x4, starting transfers between devices: 10.5 us -> 5.55 us  [exchange(): return lax.ppermute(x, 'panel', swap)]
    ppermute x1, waiting for transfers between devices: 2.29 us -> 0.32 us  [shards(): summed = own + lax.ppermute(other, 'panel', swap)]
    pallas_call x2 -> x6, Pallas kernels: 20.3 us -> 18.8 us  [the longest x4 11.4 us: forward(): pl.pallas_call(functools.partial(forward_kernel, step, last), in_specs=[i...]
    ppermute x4, waiting for transfers between devices: 1.25 us -> 0.01 us  [exchange(): return lax.ppermute(x, 'panel', swap)]
    ppermute x1, starting transfers between devices: 2.11 us -> 3.32 us  [shards(): summed = own + lax.ppermute(other, 'panel', swap)]
  transfers between devices with their start and end apart: 11 -> 11, of which waited for: 7 -> 6; matrix products, arithmetic and copies ran while one was open for 0% -> 0% of each run, Pallas kernels for 0% -> 10%
where the time goes in v1:
time: 96.8 us; the launch traced here: 96.7 us
  blocking collectives  37.1 us (38%)
  waiting for transfers between devices  23.8 us (25%)
  Pallas kernels  20.5 us (21%)
  starting transfers between devices  14.8 us (15%)
    ppermute x6, waiting for transfers between devices, shift(): return lax.ppermute(x, 'panel', [(i, (i + 2 * by) % 8) for i in range(8)])  23.4 us
    all_to_all x1, blocking collectives, shards(): lax.all_to_all(moved, 'freq', split_axis=0, concat_axis=0, tiled=True)  22.3 us
    all_to_all x1, blocking collectives, shards(): lax.all_to_all(gated.reshape(count, 4 * group, tile // 2), 'freq', split_...  14.8 us
    pallas_call x4, Pallas kernels, forward(): pl.pallas_call(functools.partial(forward_kernel, step, last), in_specs=[i...  11.4 us
    ppermute x6, starting transfers between devices, shift(): return lax.ppermute(x, 'panel', [(i, (i + 2 * by) % 8) for i in range(8)])  5.98 us
    ppermute x4, starting transfers between devices, exchange(): return lax.ppermute(x, 'panel', swap)  5.55 us
    pallas_call x1, Pallas kernels, shards(): pl.pallas_call(adjoint_kernel, in_specs=[in_smem] + [in_hbm] * 4, out_spe...  5.54 us
    ppermute x1, starting transfers between devices, shards(): summed = own + lax.ppermute(other, 'panel', swap)  3.32 us
  transfers between devices with their start and end apart: 11, of which 6 were waited for; matrix products, arithmetic and copies ran while one was open for 0% of the time, Pallas kernels for 10%

profile of v1, /device:TPU:1, one launch (start us, length us, event | category | flops | bytes accessed | tf_op | source)
XLA Modules:
  0.0 96.7 jit_solution(11786620227683827511)
XLA Ops:
  0.0 5.5 %adjoint.1 = (bf16[25,256,128]{2,1,0:T(8,128)(2,1)S(1)}, bf16[25,256,128]{2,1,0:T(8,128)(2,1)S(1)}, bf16[25,256,256]{2,1,0:T(8,128)(2,1)S(1)}, f32[4,6,256,128]{3,2,1,0:T(8,128)S(1)}, f32[4,256,256]{2,1,0:T(8,128)S(1)}) custom-call(s32[1]{0:T(128)} %bitcast.me_ref, s32[4,6]{1,0:T(4,128)} %src_ref.9, f32[2,128,1024]{2,1,0:T(8,128)} %bitcast.23, ...), custom_call_target="tpu_custom_call" | custom-call | tf_op jit(solution)/shard_map/adjoint/pallas_call | solution.py:227
  5.5 3.3 %collective-permute-start = (f32[4,256,256]{2,1,0:T(8,128)S(1)}, f32[4,256,256]{2,1,0:T(8,128)S(1)}, u32[]{:S(2)}, u32[]{:S(2)}) collective-permute-start(f32[4,256,256]{2,1,0:T(8,128)S(1)} %get-tuple-element.23), channel_id=1, source_target_pairs={{0,1},{1,0},{2,3},{3,2},{4,5},{5,4},{6,7},{7,6},{8,9},{9,8},{10,11... | collective-permute-start | bytes 3145736 | tf_op jit(solution)/shard_map/ppermute | solution.py:262
  8.9 2.0 %own.1 = (f32[4,256,256]{2,1,0:T(8,128)S(1)}, bf16[4,6,256,128]{3,2,1,0:T(8,128)(2,1)S(1)}, bf16[4,6,256,128]{3,2,1,0:T(8,128)(2,1)S(1)}) custom-call(s32[4,6]{1,0:T(4,128)S(1)} %copy-done.3, s32[1]{0:T(128)} %bitcast.me_ref, bf16[25,256,128]{2,1,0:T(8,128)(2,1)S(1)} %get-tuple-element.18.coef_h, bf16[25,256,128]{2,1,0:T(8,128)(2,1)S(1)} %get-tuple-element.19.coef_l, ...), custom_call_target="tpu_custom_call" | custom-call | flops 3000000000 | bytes 8000000 | tf_op jit(solution)/shard_map/own/pallas_call | solution.py:247
  10.8 0.3 collective-permute-done
  11.4 1.1 %collective-permute-start.3 = (f32[256,256]{1,0:T(8,128)S(1)}, f32[256,256]{1,0:T(8,128)S(1)}, u32[]{:S(2)}, u32[]{:S(2)}) collective-permute-start(f32[256,256]{1,0:T(8,128)S(1)} %get-tuple-element.31), channel_id=1, source_target_pairs={{0,6},{1,7},{2,0},{3,1},{4,2},{5,3},{6,4},{7,5},{8,14},{9,15},{10,... | collective-permute-start | bytes 786440 | tf_op jit(solution)/shard_map/ppermute | solution.py:260
  12.5 0.3 collective-permute-start.2
  12.8 0.7 collective-permute-start.1
  13.5 5.5 %collective-permute-done.3.d_ref = f32[256,256]{1,0:T(8,128)S(1)} collective-permute-done((f32[256,256]{1,0:T(8,128)S(1)}, f32[256,256]{1,0:T(8,128)S(1)}, u32[]{:S(2)}, u32[]{:S(2)}) %collective-permute-start.3) | collective-permute-done | bytes 262176 | tf_op jit(solution)/shard_map/ppermute | solution.py:260
  19.0 2.2 %collective-permute-done.2.c_ref = f32[256,256]{1,0:T(8,128)S(1)} collective-permute-done((f32[256,256]{1,0:T(8,128)S(1)}, f32[256,256]{1,0:T(8,128)S(1)}, u32[]{:S(2)}, u32[]{:S(2)}) %collective-permute-start.2) | collective-permute-done | bytes 262176 | tf_op jit(solution)/shard_map/ppermute | solution.py:260
  21.2 6.6 %collective-permute-done.1.b_ref = f32[256,256]{1,0:T(8,128)S(1)} collective-permute-done((f32[256,256]{1,0:T(8,128)S(1)}, f32[256,256]{1,0:T(8,128)S(1)}, u32[]{:S(2)}, u32[]{:S(2)}) %collective-permute-start.1) | collective-permute-done | bytes 262176 | tf_op jit(solution)/shard_map/ppermute | solution.py:260
  27.9 22.3 %all_to_all.10 = f32[32,16,128]{2,1,0:T(8,128)S(1)} all-to-all(f32[32,16,128]{2,1,0:T(8,128)S(1)} %panel_sum.1), channel_id=1, replica_groups=mesh['freq'=32,'panel'=8] {'freq'}, dimensions={0} | all-to-all | bytes 524288 | tf_op jit(solution)/shard_map/all_to_all | solution.py:270
  50.2 1.6 %gate.1 = f32[512,128]{1,0:T(8,128)S(1)} custom-call(s32[1]{0:T(128)} %bitcast.me_ref, f32[512,128]{1,0:T(8,128)S(1)} %bitcast.18, s32[4,2048]{1,0:T(4,128)S(1)} %copy-done.2, bf16[896,192]{1,0:T(8,128)(2,1)S(1)} %copy-done, bf16[128,896]{1,0:T(8,128)(2,1)S(1)} %copy-done.1), custom_call_target="tpu_custom_call" | custom-call | tf_op jit(solution)/shard_map/gate/pallas_call | solution.py:274
  51.8 14.8 %all_to_all.11.own_ref = f32[32,16,128]{2,1,0:T(8,128)S(1)} all-to-all(f32[32,16,128]{2,1,0:T(8,128)S(1)} %bitcast.19), channel_id=1, replica_groups=mesh['freq'=32,'panel'=8] {'freq'}, dimensions={0} | all-to-all | bytes 524288 | tf_op jit(solution)/shard_map/all_to_all | solution.py:291
  66.6 3.7 %collective-permute-start.7 = (f32[32,16,128]{2,1,0:T(8,128)S(1)}, f32[32,16,128]{2,1,0:T(8,128)S(1)}, u32[]{:S(2)}, u32[]{:S(2)}) collective-permute-start(f32[32,16,128]{2,1,0:T(8,128)S(1)} %all_to_all.11.own_ref), channel_id=1, source_target_pairs={{0,1},{1,0},{2,3},{3,2},{4,5},{5,4},{6,7},{7,6},{8,9},{9,8},{10,11... | collective-permute-start | bytes 786440 | tf_op jit(solution)/shard_map/ppermute | solution.py:294
  70.3 2.7 %collective-permute-start.5 = (f32[32,16,128]{2,1,0:T(8,128)S(1)}, f32[32,16,128]{2,1,0:T(8,128)S(1)}, u32[]{:S(2)}, u32[]{:S(2)}) collective-permute-start(f32[32,16,128]{2,1,0:T(8,128)S(1)} %all_to_all.11.own_ref), channel_id=1, source_target_pairs={{0,6},{1,7},{2,0},{3,1},{4,2},{5,3},{6,4},{7,5},{8,14},{9,15},{10,... | collective-permute-start | bytes 786440 | tf_op jit(solution)/shard_map/ppermute | solution.py:260
  73.0 2.6 %forward_0.1.total_ref = f32[2,128,1024]{2,1,0:T(8,128)S(1)} custom-call(s32[4,6]{1,0:T(4,128)S(1)} %copy-done.3, s32[1]{0:T(128)} %bitcast.me_ref, f32[32,16,128]{2,1,0:T(8,128)S(1)} %all_to_all.11.own_ref, f32[32,16,128]{2,1,0:T(8,128)S(1)} %collective-permute-done.7.other_ref, bf16[4,6,256,128]{3,2,1,0:T(8,128)(2,1)S(1)} %get-tuple-element.24.left_h, ...), custom_call_target="tpu_custom_call" | custom-call | flops 3000000000 | bytes 8000000 | tf_op jit(solution)/shard_map/forward_0/pallas_call | solution.py:297
  75.6 3.8 %collective-permute-done.6.own_ref = f32[32,16,128]{2,1,0:T(8,128)S(1)} collective-permute-done((f32[32,16,128]{2,1,0:T(8,128)S(1)}, f32[32,16,128]{2,1,0:T(8,128)S(1)}, u32[]{:S(2)}, u32[]{:S(2)}) %collective-permute-start.6) | collective-permute-done | bytes 262176 | tf_op jit(solution)/shard_map/ppermute | solution.py:260
  79.4 0.8 collective-permute-start.8
  80.2 1.2 %collective-permute-start.4 = (f32[32,16,128]{2,1,0:T(8,128)S(1)}, f32[32,16,128]{2,1,0:T(8,128)S(1)}, u32[]{:S(2)}, u32[]{:S(2)}) collective-permute-start(f32[32,16,128]{2,1,0:T(8,128)S(1)} %all_to_all.11.own_ref), channel_id=1, source_target_pairs={{0,4},{1,5},{2,6},{3,7},{4,0},{5,1},{6,2},{7,3},{8,12},{9,13},{10,... | collective-permute-start | bytes 786440 | tf_op jit(solution)/shard_map/ppermute | solution.py:260
  81.7 2.7 %forward_1.1.total_ref = f32[2,128,1024]{2,1,0:T(8,128)S(1)} custom-call(s32[4,6]{1,0:T(4,128)S(1)} %copy-done.3, s32[1]{0:T(128)} %bitcast.me_ref, f32[32,16,128]{2,1,0:T(8,128)S(1)} %collective-permute-done.5.own_ref, f32[32,16,128]{2,1,0:T(8,128)S(1)} %collective-permute-done.8.other_ref, bf16[4,6,256,128]{3,2,1,0:T(8,128)(2,1)S(1)} %get-tuple-element.24.left_h, ...), custom_call_target="tpu_custom_call" | custom-call | flops 3000000000 | bytes 8000000 | tf_op jit(solution)/shard_map/forward_1/pallas_call | solution.py:297
  84.3 5.3 %collective-permute-done.4.own_ref = f32[32,16,128]{2,1,0:T(8,128)S(1)} collective-permute-done((f32[32,16,128]{2,1,0:T(8,128)S(1)}, f32[32,16,128]{2,1,0:T(8,128)S(1)}, u32[]{:S(2)}, u32[]{:S(2)}) %collective-permute-start.4) | collective-permute-done | bytes 262176 | tf_op jit(solution)/shard_map/ppermute | solution.py:260
  89.7 0.8 collective-permute-start.9
  90.4 2.7 %forward_3.1.total_ref = f32[2,128,1024]{2,1,0:T(8,128)S(1)} custom-call(s32[4,6]{1,0:T(4,128)S(1)} %copy-done.3, s32[1]{0:T(128)} %bitcast.me_ref, f32[32,16,128]{2,1,0:T(8,128)S(1)} %collective-permute-done.6.own_ref, f32[32,16,128]{2,1,0:T(8,128)S(1)} %collective-permute-done.10.other_ref, bf16[4,6,256,128]{3,2,1,0:T(8,128)(2,1)S(1)} %get-tuple-element.24.left_h, ...), custom_call_target="tpu_custom_call" | custom-call | flops 3000000000 | bytes 8000000 | tf_op jit(solution)/shard_map/forward_3/pallas_call | solution.py:297
  93.1 3.4 %forward_2.1 = f32[2,128,1024]{2,1,0:T(8,128)} custom-call(s32[4,6]{1,0:T(4,128)S(1)} %copy-done.3, s32[1]{0:T(128)} %bitcast.me_ref, f32[32,16,128]{2,1,0:T(8,128)S(1)} %collective-permute-done.4.own_ref, f32[32,16,128]{2,1,0:T(8,128)S(1)} %collective-permute-done.9.other_ref, bf16[4,6,256,128]{3,2,1,0:T(8,128)(2,1)S(1)} %get-tuple-element.24.left_h, ...), custom_call_target="tpu_custom_call" | custom-call | flops 3000000000 | bytes 8000000 | tf_op jit(solution)/shard_map/forward_2/pallas_call | solution.py:297
  (20 shorter events, 0.6 us)
Async XLA Ops:
  0.0 8.9 %copy-start.3 = (s32[4,6]{1,0:T(4,128)S(1)}, s32[4,6]{1,0:T(4,128)}, u32[]{:S(2)}) copy-start(s32[4,6]{1,0:T(4,128)} %src_ref.9) | copy-start | bytes 292
  5.5 5.6 %collective-permute-start = (f32[4,256,256]{2,1,0:T(8,128)S(1)}, f32[4,256,256]{2,1,0:T(8,128)S(1)}, u32[]{:S(2)}, u32[]{:S(2)}) collective-permute-start(f32[4,256,256]{2,1,0:T(8,128)S(1)} %get-tuple-element.23), channel_id=1, source_target_pairs={{0,1},{1,0},{2,3},{3,2},{4,5},{5,4},{6,7},{7,6},{8,9},{9,8},{10,11... | collective-permute-start | bytes 3145736 | tf_op jit(solution)/shard_map/ppermute | solution.py:262
  11.2 39.0 %copy-start = (bf16[896,192]{1,0:T(8,128)(2,1)S(1)}, bf16[896,192]{1,0:T(8,128)(2,1)}, u32[]{:S(2)}) copy-start(bf16[896,192]{1,0:T(8,128)(2,1)} %constant.8.clone.into_ref) | copy-start | bytes 1032196
  11.2 39.0 %copy-start.1 = (bf16[128,896]{1,0:T(8,128)(2,1)S(1)}, bf16[128,896]{1,0:T(8,128)(2,1)}, u32[]{:S(2)}) copy-start(bf16[128,896]{1,0:T(8,128)(2,1)} %constant.9.clone.outof_ref) | copy-start | bytes 688132
  11.2 39.0 %copy-start.2 = (s32[4,2048]{1,0:T(4,128)S(1)}, s32[4,2048]{1,0:T(4,128)}, u32[]{:S(2)}) copy-start(s32[4,2048]{1,0:T(4,128)} %onset_ref.1) | copy-start | bytes 98308
  11.3 61.7 %copy-start.4 = (f32[1,2,128,1024]{3,2,1,0:T(8,128)S(1)}, f32[1,2,128,1024]{3,2,1,0:T(8,128)}, u32[]{:S(2)}) copy-start(f32[1,2,128,1024]{3,2,1,0:T(8,128)} %param.9) | copy-start | bytes 3145732
  11.4 7.6 %collective-permute-start.3 = (f32[256,256]{1,0:T(8,128)S(1)}, f32[256,256]{1,0:T(8,128)S(1)}, u32[]{:S(2)}, u32[]{:S(2)}) collective-permute-start(f32[256,256]{1,0:T(8,128)S(1)} %get-tuple-element.31), channel_id=1, source_target_pairs={{0,6},{1,7},{2,0},{3,1},{4,2},{5,3},{6,4},{7,5},{8,14},{9,15},{10,... | collective-permute-start | bytes 786440 | tf_op jit(solution)/shard_map/ppermute | solution.py:260
  12.5 8.7 %collective-permute-start.2 = (f32[256,256]{1,0:T(8,128)S(1)}, f32[256,256]{1,0:T(8,128)S(1)}, u32[]{:S(2)}, u32[]{:S(2)}) collective-permute-start(f32[256,256]{1,0:T(8,128)S(1)} %get-tuple-element.32), channel_id=1, source_target_pairs={{0,4},{1,5},{2,6},{3,7},{4,0},{5,1},{6,2},{7,3},{8,12},{9,13},{10,... | collective-permute-start | bytes 786440 | tf_op jit(solution)/shard_map/ppermute | solution.py:260
  12.8 15.0 %collective-permute-start.1 = (f32[256,256]{1,0:T(8,128)S(1)}, f32[256,256]{1,0:T(8,128)S(1)}, u32[]{:S(2)}, u32[]{:S(2)}) collective-permute-start(f32[256,256]{1,0:T(8,128)S(1)} %get-tuple-element.33), channel_id=1, source_target_pairs={{0,2},{1,3},{2,4},{3,5},{4,6},{5,7},{6,0},{7,1},{8,10},{9,11},{10,... | collective-permute-start | bytes 786440 | tf_op jit(solution)/shard_map/ppermute | solution.py:260
  66.6 6.4 %collective-permute-start.7 = (f32[32,16,128]{2,1,0:T(8,128)S(1)}, f32[32,16,128]{2,1,0:T(8,128)S(1)}, u32[]{:S(2)}, u32[]{:S(2)}) collective-permute-start(f32[32,16,128]{2,1,0:T(8,128)S(1)} %all_to_all.11.own_ref), channel_id=1, source_target_pairs={{0,1},{1,0},{2,3},{3,2},{4,5},{5,4},{6,7},{7,6},{8,9},{9,8},{10,11... | collective-permute-start | bytes 786440 | tf_op jit(solution)/shard_map/ppermute | solution.py:294
  70.3 9.1 %collective-permute-start.6 = (f32[32,16,128]{2,1,0:T(8,128)S(1)}, f32[32,16,128]{2,1,0:T(8,128)S(1)}, u32[]{:S(2)}, u32[]{:S(2)}) collective-permute-start(f32[32,16,128]{2,1,0:T(8,128)S(1)} %all_to_all.11.own_ref), channel_id=1, source_target_pairs={{0,2},{1,3},{2,4},{3,5},{4,6},{5,7},{6,0},{7,1},{8,10},{9,11},{10,... | collective-permute-start | bytes 786440 | tf_op jit(solution)/shard_map/ppermute | solution.py:260
  70.3 9.1 %collective-permute-start.5 = (f32[32,16,128]{2,1,0:T(8,128)S(1)}, f32[32,16,128]{2,1,0:T(8,128)S(1)}, u32[]{:S(2)}, u32[]{:S(2)}) collective-permute-start(f32[32,16,128]{2,1,0:T(8,128)S(1)} %all_to_all.11.own_ref), channel_id=1, source_target_pairs={{0,6},{1,7},{2,0},{3,1},{4,2},{5,3},{6,4},{7,5},{8,14},{9,15},{10,... | collective-permute-start | bytes 786440 | tf_op jit(solution)/shard_map/ppermute | solution.py:260
  79.4 2.3 %collective-permute-start.8 = (f32[32,16,128]{2,1,0:T(8,128)S(1)}, f32[32,16,128]{2,1,0:T(8,128)S(1)}, u32[]{:S(2)}, u32[]{:S(2)}) collective-permute-start(f32[32,16,128]{2,1,0:T(8,128)S(1)} %collective-permute-done.5.own_ref), channel_id=1, source_target_pairs={{0,1},{1,0},{2,3},{3,2},{4,5},{5,4},{6,7},{7,6},{8,9},{9,8},{10,11... | collective-permute-start | bytes 786440 | tf_op jit(solution)/shard_map/ppermute | solution.py:294
  80.2 9.4 %collective-permute-start.4 = (f32[32,16,128]{2,1,0:T(8,128)S(1)}, f32[32,16,128]{2,1,0:T(8,128)S(1)}, u32[]{:S(2)}, u32[]{:S(2)}) collective-permute-start(f32[32,16,128]{2,1,0:T(8,128)S(1)} %all_to_all.11.own_ref), channel_id=1, source_target_pairs={{0,4},{1,5},{2,6},{3,7},{4,0},{5,1},{6,2},{7,3},{8,12},{9,13},{10,... | collective-permute-start | bytes 786440 | tf_op jit(solution)/shard_map/ppermute | solution.py:260
  81.4 9.0 %collective-permute-start.10 = (f32[32,16,128]{2,1,0:T(8,128)S(1)}, f32[32,16,128]{2,1,0:T(8,128)S(1)}, u32[]{:S(2)}, u32[]{:S(2)}) collective-permute-start(f32[32,16,128]{2,1,0:T(8,128)S(1)} %collective-permute-done.6.own_ref), channel_id=1, source_target_pairs={{0,1},{1,0},{2,3},{3,2},{4,5},{5,4},{6,7},{7,6},{8,9},{9,8},{10,11... | collective-permute-start | bytes 786440 | tf_op jit(solution)/shard_map/ppermute | solution.py:294
  89.7 3.5 %collective-permute-start.9 = (f32[32,16,128]{2,1,0:T(8,128)S(1)}, f32[32,16,128]{2,1,0:T(8,128)S(1)}, u32[]{:S(2)}, u32[]{:S(2)}) collective-permute-start(f32[32,16,128]{2,1,0:T(8,128)S(1)} %collective-permute-done.4.own_ref), channel_id=1, source_target_pairs={{0,1},{1,0},{2,3},{3,2},{4,5},{5,4},{6,7},{7,6},{8,9},{9,8},{10,11... | collective-permute-start | bytes 786440 | tf_op jit(solution)/shard_map/ppermute | solution.py:294

commit v2 on v1

--- a/solution.py
+++ b/solution.py
@@ -18,6 +18,7 @@
 BF16 = jnp.bfloat16
 NN = (((1,), (0,)), ((), ()))
 NT_DIMS = (((1,), (1,)), ((), ()))
+AWAY = (2, 1, 3)
 
 
 def split(x):
@@ -53,16 +54,16 @@
     return lax.rem(me // 2 + step, 4) * 2 + lax.rem(me + other, 2)
 
 
-def spread(src_ref, me, other, coef_h, coef_l, right_ref, out_ref):
+def spread(src_ref, me, targets, coef_h, coef_l, right_ref, out_ref):
     width = coef_h.shape[2]
-    for step in range(out_ref.shape[0]):
+    for i, (step, other) in enumerate(targets):
         target = tile_of(me, step, other)
         parts = []
         for p in range(src_ref.shape[0]):
             _, at = find_slot(src_ref, p, target, src_ref.shape[1])
             parts.append((coef_h[at], coef_l[at], right_ref[at, :, :width], right_ref[at, :, width:]))
         high, low, right_h, right_l = (jnp.concatenate(x, axis=1) for x in zip(*parts))
-        out_ref[step] = dot(high, right_h, NT_DIMS) + dot(low, right_h, NT_DIMS) + dot(high, right_l, NT_DIMS)
+        out_ref[i] = dot(high, right_h, NT_DIMS) + dot(low, right_h, NT_DIMS) + dot(high, right_l, NT_DIMS)
 
 
 def adjoint_kernel(
@@ -82,12 +83,9 @@
         )
     rights = [pltpu.make_async_copy(right_hbm.at[p], raw_ref.at[p], sems.at[2, p]) for p in range(panels)]
     names = pltpu.make_async_copy(src_hbm, src_ref, sems.at[3, 0])
-    for pair in copies:
+    for pair in copies[:2]:
         pair[0].start()
         pair[1].start()
-    for copy in rights:
-        copy.start()
-    names.start()
     last = panels * slots
     coef_h[last] = jnp.zeros(coef_h.shape[1:], BF16)
     coef_l[last] = jnp.zeros(coef_l.shape[1:], BF16)
@@ -95,6 +93,13 @@
     for p in range(panels):
         copies[p][0].wait()
         copies[p][1].wait()
+        if p + 2 < panels:
+            copies[p + 2][0].start()
+            copies[p + 2][1].start()
+        elif p + 2 == panels:
+            names.start()
+            for copy in rights:
+                copy.start()
         field_h, field_l = split(field_ref[p].reshape(-1, tile))
         for s in range(0, slots, 2):
             left_h, left_l = split(jnp.concatenate([left_ref[p, s], left_ref[p, s + 1]], axis=1))
@@ -108,39 +113,64 @@
         for s in range(slots):
             right_ref[p * slots + s] = jnp.concatenate(split(raw_ref[p, s]), axis=1)
     names.wait()
-    spread(src_ref, me_ref[0], 1, coef_h, coef_l, right_ref, out_ref)
-
-
-def own_kernel(src_ref, me_ref, coef_h, coef_l, right_ref, left_ref, out_ref, left_h, left_l):
-    spread(src_ref, me_ref[0], 0, coef_h, coef_l, right_ref, out_ref)
+    spread(src_ref, me_ref[0], [(step, 1) for step in AWAY], coef_h, coef_l, right_ref, out_ref)
+
+
+def own_kernel(src_ref, me_ref, coef_h, coef_l, right_ref, out_ref):
+    spread(src_ref, me_ref[0], [(step, 0) for step in AWAY], coef_h, coef_l, right_ref, out_ref)
+
+
+def here_kernel(src_ref, me_ref, coef_h, coef_l, right_ref, left_ref, _, out_ref, left_h, left_l):
+    spread(src_ref, me_ref[0], [(0, 1), (0, 0)], coef_h, coef_l, right_ref, out_ref)
     for p in range(left_ref.shape[0]):
         for s in range(left_ref.shape[1]):
             left_h[p, s], left_l[p, s] = split(left_ref[p, s])
 
 
-def sum_kernel(a_ref, b_ref, c_ref, d_ref, out_ref):
-    total = (a_ref[...] + b_ref[...]) + (c_ref[...] + d_ref[...])
-    rows, cols = total.shape
-    lanes = cols // 2
-    half = total.reshape(2, rows // 16, 8, cols)
-    for c in range(2):
-        left, right = half[c, :, :, :lanes], half[c, :, :, lanes:]
+def chip_sum_kernel(own_ref, swapped_ref, up_ref, down_ref, up_half, down_half):
+    half = up_half.shape[0]
+    up_ref[0] = own_ref[0, :half] + swapped_ref[0, :half]
+    down_ref[0] = own_ref[0, half:] + swapped_ref[0, half:]
+    up_half[...] = own_ref[1, :half] + swapped_ref[1, :half]
+    up_ref[1] = own_ref[1, half:] + swapped_ref[1, half:]
+    down_ref[1] = own_ref[2, :half] + swapped_ref[2, :half]
+    down_half[...] = own_ref[2, half:] + swapped_ref[2, half:]
+
+
+def relay_kernel(up_half, from_below, down_half, from_above, up_ref, down_ref):
+    up_ref[...] = up_half[...] + from_below[0]
+    down_ref[...] = down_half[...] + from_above[0]
+
+
+def sum_kernel(here_ref, swapped_ref, below, above, relayed_below, relayed_above, out_ref):
+    totals = (
+        (here_ref[1, : relayed_below.shape[0]] + swapped_ref[: relayed_below.shape[0]])
+        + (relayed_below[...] + above[1]),
+        (here_ref[1, relayed_below.shape[0] :] + swapped_ref[relayed_below.shape[0] :])
+        + (relayed_above[...] + below[1]),
+    )
+    for c, total in enumerate(totals):
+        rows, cols = total.shape
+        lanes = cols // 2
+        block = total.reshape(rows // 8, 8, cols)
+        left, right = block[:, :, :lanes], block[:, :, lanes:]
         low = lax.broadcasted_iota(jnp.int32, left.shape, 1) < 4
         even = jnp.where(low, left, pltpu.roll(right, 4, 1))
         odd = jnp.where(low, pltpu.roll(left, 4, 1), right)
-        out_ref[:, 8 * c : 8 * c + 8, :] = jnp.stack([even, odd], axis=1).reshape(rows // 8, 8, lanes)
-
-
-def gate_kernel(me_ref, x_ref, onset_ref, into_ref, outof_ref, y_ref):
+        out_ref[:, 8 * c : 8 * c + 8, :] = jnp.stack([even, odd], axis=1).reshape(rows // 4, 8, lanes)
+
+
+def gate_kernel(_, me_ref, x_ref, onset_ref, into_ref, outof_ref, y_ref):
     group = onset_ref.shape[0]
     lanes = x_ref.shape[1]
+    here = pl.ds(pl.multiple_of(me_ref[0] * (2 * lanes), 2 * lanes), 2 * lanes)
     bands = outof_ref.shape[0] // 2
     for v in range(group):
         picks = [pl.ds(h * group + v, bands, stride=2 * group) for h in range(2)]
         high, low = split(jnp.concatenate([x_ref[pick, :] for pick in picks], axis=1))
         traces = dot(into_ref[...], jnp.concatenate([high, high, low], axis=0))
         when = lax.broadcasted_iota(jnp.int32, traces.shape, 0)
-        gated = jnp.where(when < onset_ref[v : v + 1, :], traces, 0.0)
+        gated = jnp.where(when < onset_ref[v : v + 1, here], traces, 0.0)
         high, low = split(gated)
         pair = dot(outof_ref[...], high)
         back = pair[:bands] + pair[bands:] + dot(outof_ref[:bands, :], low)
@@ -148,13 +178,16 @@
             y_ref[picks[h], :] = back[:, h * lanes : (h + 1) * lanes]
 
 
-def forward_kernel(step, last, src_ref, me_ref, own_ref, other_ref, left_h, left_l, right_ref, total_ref, out_ref, *scratch):
+def forward_kernel(steps, last, pieces, src_ref, me_ref, *refs):
+    number = 2 * len(steps)
+    left_h, left_l, right_ref, total_ref, out_ref, *scratch = refs[number * pieces :]
     panels, slots, tile, width = left_h.shape
     me = me_ref[0]
     tiles = []
-    for ref in (own_ref, other_ref):
-        count, _, lanes = ref.shape
-        block = ref[...].reshape(count // 2, 2, 2, 8, lanes)
+    for i in range(number):
+        got = jnp.concatenate([ref[...] for ref in refs[i * pieces : (i + 1) * pieces]], axis=0)
+        count, _, lanes = got.shape
+        block = got.reshape(count // 2, 2, 2, 8, lanes)
         parts = []
         for c in range(2):
             even, odd = block[:, 0, c], block[:, 1, c]
@@ -168,7 +201,7 @@
         at = slice(p * tile, (p + 1) * tile)
         parts = []
         for i, (high, low) in enumerate(tiles):
-            slot, place = find_slot(src_ref, p, tile_of(me, step, i), slots)
+            slot, place = find_slot(src_ref, p, tile_of(me, steps[i // 2], i % 2), slots)
             right = right_ref[place]
             pair = dot(high, right)
             products = pair[:, :width] + pair[:, width:] + dot(low, right[:, :width])
@@ -219,7 +252,7 @@
     in_smem = pl.BlockSpec(memory_space=pltpu.SMEM)
     in_hbm = pl.BlockSpec(memory_space=pltpu.HBM)
     hbm = lambda x: pltpu.with_memory_space_constraint(x, pltpu.HBM)
-    sums_type = jax.ShapeDtypeStruct((4, rows, tile), F32)
+    sums_type = jax.ShapeDtypeStruct((3, rows, tile), F32)
     places = panels * slots + 1
     cost = pl.CostEstimate(flops=3_000_000_000, bytes_accessed=8_000_000, transcendentals=0)
     coef_type = jax.ShapeDtypeStruct((places, rows, width), BF16)
@@ -244,76 +277,80 @@
         compiler_params=pltpu.CompilerParams(vmem_limit_bytes=28 * mib),
         name="adjoint",
     )(me, hbm(tile_src), hbm(wavefield[0]), hbm(left), hbm(right))
-    own, left_h, left_l = pl.pallas_call(
-        own_kernel,
-        in_specs=[in_smem, in_smem] + [in_vmem] * 4,
-        out_specs=[in_vmem] * 3,
-        out_shape=[sums_type, jax.ShapeDtypeStruct(left_shape, BF16), jax.ShapeDtypeStruct(left_shape, BF16)],
-        compiler_params=pltpu.CompilerParams(vmem_limit_bytes=24 * mib),
-        cost_estimate=cost,
-        name="own",
-    )(tile_src, me, coef_h, coef_l, right_kept, left_kept)
+    def local(kernel, outs, *args, scalars=True, limit=4):
+        return pl.pallas_call(
+            kernel,
+            in_specs=[in_smem] * (2 * scalars) + [in_vmem] * (len(args) - 2 * scalars),
+            out_specs=[in_vmem] * len(outs),
+            out_shape=[jax.ShapeDtypeStruct(shape, dtype) for shape, dtype in outs],
+            compiler_params=pltpu.CompilerParams(vmem_limit_bytes=limit * mib),
+            cost_estimate=cost if scalars else None,
+            name=kernel.__name__,
+        )(*args)
 
     swap = [(i, i ^ 1) for i in range(8)]
+
+    def exchange(x):
+        return lax.ppermute(x, "panel", swap)
 
     def shift(x, by):
         return lax.ppermute(x, "panel", [(i, (i + 2 * by) % 8) for i in range(8)])
 
-    summed = own + lax.ppermute(other, "panel", swap)
-    parts = [summed[0]] + [shift(summed[b], b) for b in range(1, 4)]
-    moved = pl.pallas_call(
+    half = rows // 2
+    swapped = exchange(other)
+    (own,) = local(own_kernel, [((3, rows, tile), F32)], tile_src, me, coef_h, coef_l, right_kept, limit=16)
+    up, down, up_half, down_half = local(
+        chip_sum_kernel, [((2, half, tile), F32)] * 2 + [((half, tile), F32)] * 2, own, swapped, scalars=False
+    )
+    below, above = shift(up, 1), shift(down, -1)
+    after = exchange(up[0, :8, :width])
+    here, left_h, left_l = local(
+        here_kernel,
+        [((2, rows, tile), F32), (left_shape, BF16), (left_shape, BF16)],
+        tile_src, me, coef_h, coef_l, right_kept, left_kept, after, limit=20,
+    )
+    swapped = exchange(here[0])
+    below, above, swapped = lax.optimization_barrier((below, above, swapped))
+    up, down = local(relay_kernel, [((half, tile), F32)] * 2, up_half, below, down_half, above, scalars=False)
+    (moved,) = local(
         sum_kernel,
-        out_shape=jax.ShapeDtypeStruct((count, 4 * group, tile // 2), F32),
-        compiler_params=pltpu.CompilerParams(vmem_limit_bytes=4 * mib),
-        name="panel_sum",
-    )(*parts)
+        [((count, 4 * group, tile // 2), F32)],
+        here, swapped, below, above, shift(up, 1), shift(down, -1), scalars=False,
+    )
     moved = lax.all_to_all(moved, "freq", split_axis=0, concat_axis=0, tiled=True)
 
     into, outof = time_tables(count)
-    whole = lambda shape: pl.BlockSpec(shape, lambda i, *_: (0,) * len(shape))
-    gated = pl.pallas_call(
+    (gated,) = local(
         gate_kernel,
-        grid_spec=pltpu.PrefetchScalarGridSpec(
-            num_scalar_prefetch=1,
-            grid=(1,),
-            in_specs=[
-                whole((2 * rows, tile // 2)),
-                pl.BlockSpec((group, tile), lambda i, me_ref: (0, me_ref[0])),
-                whole(into.shape),
-                whole(outof.shape),
-            ],
-            out_specs=whole((2 * rows, tile // 2)),
-        ),
-        out_shape=jax.ShapeDtypeStruct((2 * rows, tile // 2), F32),
-        compiler_params=pltpu.CompilerParams(vmem_limit_bytes=12 * mib),
-        name="gate",
-    )(me, moved.reshape(2 * rows, tile // 2), onset, jnp.asarray(into), jnp.asarray(outof))
+        [((2 * rows, tile // 2), F32)],
+        tile_src, me, moved.reshape(2 * rows, tile // 2), onset, jnp.asarray(into), jnp.asarray(outof), limit=12,
+    )
     back = lax.all_to_all(gated.reshape(count, 4 * group, tile // 2), "freq", split_axis=0, concat_axis=0, tiled=True)
 
-    def exchange(x):
-        return lax.ppermute(x, "panel", swap)
-
-    def forward(step, mine, theirs, total, last=False):
+    def forward(steps, tiles, total, last=False):
+        number = len(tiles)
         return pl.pallas_call(
-            functools.partial(forward_kernel, step, last),
-            in_specs=[in_smem, in_smem] + [in_vmem] * 6,
+            functools.partial(forward_kernel, steps, last, number // (2 * len(steps))),
+            in_specs=[in_smem, in_smem] + [in_vmem] * (number + 4),
             out_specs=in_hbm if last else in_vmem,
             out_shape=jax.ShapeDtypeStruct(total.shape, F32),
             scratch_shapes=[pltpu.VMEM((panels, 2, virtual, tile), F32), pltpu.SemaphoreType.DMA((panels,))] if last else [],
-            compiler_params=pltpu.CompilerParams(vmem_limit_bytes=22 * mib),
+            compiler_params=pltpu.CompilerParams(vmem_limit_bytes=24 * mib),
             cost_estimate=cost,
-            name=f"forward_{step}",
-        )(tile_src, me, mine, theirs, left_h, left_l, right_kept, total)
-
-    mine = {step: shift(back, -step) for step in (1, 3, 2)}
-    total = forward(0, back, exchange(back), direct[0])
-    mine[1], mine[3], total = lax.optimization_barrier((mine[1], mine[3], total))
-    theirs = {step: exchange(mine[step]) for step in (1, 3)}
-    total = forward(1, mine[1], theirs[1], total)
-    mine[2], total = lax.optimization_barrier((mine[2], total))
-    theirs[2] = exchange(mine[2])
-    total = forward(3, mine[3], theirs[3], total)
-    return forward(2, mine[2], theirs[2], total, last=True)[None]
+            name="forward_" + "_".join(str(step) for step in steps),
+        )(tile_src, me, *tiles, left_h, left_l, right_kept, total)
+
+    above, below = shift(back, -1), shift(back, 1)
+    total = forward((0,), [back, exchange(back)], direct[0])
+    above, below, total = lax.optimization_barrier((above, below, total))
+    cut = count // 2
+    far = [shift(above[:cut], -1), shift(below[cut:], 1)]
+    above_other, below_other = exchange(above), exchange(below)
+    total = forward((1,), [above, above_other], total)
+    *far, total = lax.optimization_barrier((*far, total))
+    far = far + [exchange(part) for part in far]
+    total = forward((3,), [below, below_other], total)
+    return forward((2,), far, total, last=True)[None]
 
 
 def solution(mesh):

time: 96.8 us -> 90.2 us (0.932)
  waiting for transfers between devices: 23.8 us -> 11 us
  starting transfers between devices: 14.8 us -> 22.4 us
  blocking collectives: 37.1 us -> 33.7 us
  Pallas kernels: 20.5 us -> 22.5 us
    ppermute x6 -> x8, waiting for transfers between devices: 23.4 us -> 10.5 us  [shift(): return lax.ppermute(x, 'panel', [(i, (i + 2 * by) % 8) for i in range(8)])]
    ppermute x4 -> x8, starting transfers between devices: 5.55 us -> 11.5 us  [exchange(): return lax.ppermute(x, 'panel', swap)]
    ppermute x6 -> x8, starting transfers between devices: 5.98 us -> 10.9 us  [shift(): return lax.ppermute(x, 'panel', [(i, (i + 2 * by) % 8) for i in range(8)])]
    ppermute x1 -> x0, starting transfers between devices: 3.32 us -> none  [shards(): summed = own + lax.ppermute(other, 'panel', swap)]
    all_to_all x1, blocking collectives: 22.3 us -> 19.7 us  [shards(): lax.all_to_all(moved, 'freq', split_axis=0, concat_axis=0, tiled=True)]
    pallas_call x7 -> x10, Pallas kernels: 14.9 us -> 16.7 us  [the longest x4 11.3 us: forward(): pl.pallas_call(functools.partial(forward_kernel, steps, last, number // (...]
  transfers between devices with their start and end apart: 11 -> 16, of which waited for: 6 -> 6; matrix products, arithmetic and copies ran while one was open for 0% -> 0% of each run, Pallas kernels for 10% -> 12%
where the time goes in v2:
time: 90.2 us; the launch traced here: 90 us
  blocking collectives  33.7 us (37%)
  Pallas kernels  22.5 us (25%)
  starting transfers between devices  22.4 us (25%)
  waiting for transfers between devices  11 us (12%)
    all_to_all x1, blocking collectives, shards(): lax.all_to_all(moved, 'freq', split_axis=0, concat_axis=0, tiled=True)  19.7 us
    all_to_all x1, blocking collectives, shards(): lax.all_to_all(gated.reshape(count, 4 * group, tile // 2), 'freq', split_...  14 us
    ppermute x8, starting transfers between devices, exchange(): return lax.ppermute(x, 'panel', swap)  11.5 us
    pallas_call x4, Pallas kernels, forward(): pl.pallas_call(functools.partial(forward_kernel, steps, last, number // (...  11.3 us
    ppermute x8, starting transfers between devices, shift(): return lax.ppermute(x, 'panel', [(i, (i + 2 * by) % 8) for i in range(8)])  10.9 us
    ppermute x8, waiting for transfers between devices, shift(): return lax.ppermute(x, 'panel', [(i, (i + 2 * by) % 8) for i in range(8)])  10.5 us
    pallas_call x1, Pallas kernels, shards(): pl.pallas_call(adjoint_kernel, in_specs=[in_smem] + [in_hbm] * 4, out_spe...  5.79 us
    pallas_call x6, Pallas kernels, local(): pl.pallas_call(kernel, in_specs=[in_smem] * (2 * scalars) + [in_vmem] * (...  5.35 us
  transfers between devices with their start and end apart: 16, of which 6 were waited for; matrix products, arithmetic and copies ran while one was open for 0% of the time, Pallas kernels for 12%

profile of v2, /device:TPU:1, one launch (start us, length us, event | category | flops | bytes accessed | tf_op | source)
XLA Modules:
  0.0 90.0 jit_solution(6180824744149730308)
XLA Ops:
  0.0 5.8 %adjoint.1 = (bf16[25,256,128]{2,1,0:T(8,128)(2,1)S(1)}, bf16[25,256,128]{2,1,0:T(8,128)(2,1)S(1)}, bf16[25,256,256]{2,1,0:T(8,128)(2,1)S(1)}, f32[4,6,256,128]{3,2,1,0:T(8,128)S(1)}, f32[3,256,256]{2,1,0:T(8,128)S(1)}) custom-call(s32[1]{0:T(128)} %bitcast.me_ref, s32[4,6]{1,0:T(4,128)} %src_ref.11, f32[2,128,1024]{2,1,0:T(8,128)} %bitcast.19, ...), custom_call_target="tpu_custom_call" | custom-call | tf_op jit(solution)/shard_map/adjoint/pallas_call | solution.py:260
  5.8 3.3 %collective-permute-start = (f32[3,256,256]{2,1,0:T(8,128)S(1)}, f32[3,256,256]{2,1,0:T(8,128)S(1)}, u32[]{:S(2)}, u32[]{:S(2)}) collective-permute-start(f32[3,256,256]{2,1,0:T(8,128)S(1)} %get-tuple-element.32), channel_id=1, source_target_pairs={{0,1},{1,0},{2,3},{3,2},{4,5},{5,4},{6,7},{7,6},{8,9},{9,8},{10,11... | collective-permute-start | bytes 2359304 | tf_op jit(solution)/shard_map/ppermute | solution.py:294
  9.1 1.4 %own_kernel.1.own_ref = f32[3,256,256]{2,1,0:T(8,128)S(1)} custom-call(s32[4,6]{1,0:T(4,128)S(1)} %copy-done, s32[1]{0:T(128)} %bitcast.me_ref, bf16[25,256,128]{2,1,0:T(8,128)(2,1)S(1)} %get-tuple-element.28.coef_h, bf16[25,256,128]{2,1,0:T(8,128)(2,1)S(1)} %get-tuple-element.29.coef_l, bf16[25,256,256]{2,1,0:T(8,128)(2,1)S(1)} %get-tuple-element.30.right_ref.refs_4_.refs_6_), custom_call_target="tpu_custom_call" | custom-call | flops 3000000000 | bytes 8000000 | tf_op jit(solution)/shard_map/own_kernel/pallas_call | solution.py:281
  11.6 2.7 %collective-permute-start.3 = (f32[2,128,256]{2,1,0:T(8,128)S(1)}, f32[2,128,256]{2,1,0:T(8,128)S(1)}, u32[]{:S(2)}, u32[]{:S(2)}) collective-permute-start(f32[2,128,256]{2,1,0:T(8,128)S(1)} %get-tuple-element.35), channel_id=1, source_target_pairs={{0,6},{1,7},{2,0},{3,1},{4,2},{5,3},{6,4},{7,5},{8,14},{9,15},{10,... | collective-permute-start | bytes 786440 | tf_op jit(solution)/shard_map/ppermute | solution.py:297
  14.3 1.6 %here_kernel.1 = (f32[2,256,256]{2,1,0:T(8,128)S(1)}, bf16[4,6,256,128]{3,2,1,0:T(8,128)(2,1)S(1)}, bf16[4,6,256,128]{3,2,1,0:T(8,128)(2,1)S(1)}) custom-call(s32[4,6]{1,0:T(4,128)S(1)} %copy-done, s32[1]{0:T(128)} %bitcast.me_ref, bf16[25,256,128]{2,1,0:T(8,128)(2,1)S(1)} %get-tuple-element.28.coef_h, bf16[25,256,128]{2,1,0:T(8,128)(2,1)S(1)} %get-tuple-element.29.coef_l, ...), custom_call_target="tpu_custom_call" | custom-call | flops 3000000000 | bytes 8000000 | tf_op jit(solution)/shard_map/here_kernel/pallas_call | solution.py:281
  15.9 0.8 collective-permute-start.4
  16.7 2.8 %collective-permute-done.3.from_above.above = f32[2,128,256]{2,1,0:T(8,128)S(1)} collective-permute-done((f32[2,128,256]{2,1,0:T(8,128)S(1)}, f32[2,128,256]{2,1,0:T(8,128)S(1)}, u32[]{:S(2)}, u32[]{:S(2)}) %collective-permute-start.3) | collective-permute-done | bytes 262176 | tf_op jit(solution)/shard_map/ppermute | solution.py:297
  19.5 1.1 %collective-permute-done.2.from_below.below = f32[2,128,256]{2,1,0:T(8,128)S(1)} collective-permute-done((f32[2,128,256]{2,1,0:T(8,128)S(1)}, f32[2,128,256]{2,1,0:T(8,128)S(1)}, u32[]{:S(2)}, u32[]{:S(2)}) %collective-permute-start.2) | collective-permute-done | bytes 262176 | tf_op jit(solution)/shard_map/ppermute | solution.py:297
  20.7 2.7 %collective-permute-start.6 = (f32[128,256]{1,0:T(8,128)S(1)}, f32[128,256]{1,0:T(8,128)S(1)}, u32[]{:S(2)}, u32[]{:S(2)}) collective-permute-start(f32[128,256]{1,0:T(8,128)S(1)} %get-tuple-element.42), channel_id=1, source_target_pairs={{0,6},{1,7},{2,0},{3,1},{4,2},{5,3},{6,4},{7,5},{8,14},{9,15},{10,... | collective-permute-start | bytes 393224 | tf_op jit(solution)/shard_map/ppermute | solution.py:297
  23.4 2.4 %collective-permute-done.5.relayed_below = f32[128,256]{1,0:T(8,128)S(1)} collective-permute-done((f32[128,256]{1,0:T(8,128)S(1)}, f32[128,256]{1,0:T(8,128)S(1)}, u32[]{:S(2)}, u32[]{:S(2)}) %collective-permute-start.5) | collective-permute-done | bytes 131104 | tf_op jit(solution)/shard_map/ppermute | solution.py:297
  25.8 19.7 %all_to_all.10 = f32[32,16,128]{2,1,0:T(8,128)S(1)} all-to-all(f32[32,16,128]{2,1,0:T(8,128)S(1)} %sum_kernel.1), channel_id=1, replica_groups=mesh['freq'=32,'panel'=8] {'freq'}, dimensions={0} | all-to-all | bytes 524288 | tf_op jit(solution)/shard_map/all_to_all | solution.py:320
  45.5 2.2 %gate_kernel.1 = f32[512,128]{1,0:T(8,128)S(1)} custom-call(s32[4,6]{1,0:T(4,128)S(1)} %copy-done, s32[1]{0:T(128)} %bitcast.me_ref, f32[512,128]{1,0:T(8,128)S(1)} %bitcast.14, s32[4,2048]{1,0:T(4,128)S(1)} %copy-done.2, bf16[896,192]{1,0:T(8,128)(2,1)S(1)} %copy-done.3, bf16[128,896]{1,0:T(8,128)(2,1)S(1)} %copy-done.4), custom_call_target="tpu_custom_call" | custom-call | flops 3000000000 | bytes 8000000 | tf_op jit(solution)/shard_map/gate_kernel/pallas_call | solution.py:281
  47.8 14.0 %all_to_all.11.refs_0_ = f32[32,16,128]{2,1,0:T(8,128)S(1)} all-to-all(f32[32,16,128]{2,1,0:T(8,128)S(1)} %bitcast.15), channel_id=1, replica_groups=mesh['freq'=32,'panel'=8] {'freq'}, dimensions={0} | all-to-all | bytes 524288 | tf_op jit(solution)/shard_map/all_to_all | solution.py:328
  61.8 4.7 %collective-permute-start.9 = (f32[32,16,128]{2,1,0:T(8,128)S(1)}, f32[32,16,128]{2,1,0:T(8,128)S(1)}, u32[]{:S(2)}, u32[]{:S(2)}) collective-permute-start(f32[32,16,128]{2,1,0:T(8,128)S(1)} %all_to_all.11.refs_0_), channel_id=1, source_target_pairs={{0,1},{1,0},{2,3},{3,2},{4,5},{5,4},{6,7},{7,6},{8,9},{9,8},{10,11... | collective-permute-start | bytes 786440 | tf_op jit(solution)/shard_map/ppermute | solution.py:294
  66.5 1.0 %collective-permute-start.8 = (f32[32,16,128]{2,1,0:T(8,128)S(1)}, f32[32,16,128]{2,1,0:T(8,128)S(1)}, u32[]{:S(2)}, u32[]{:S(2)}) collective-permute-start(f32[32,16,128]{2,1,0:T(8,128)S(1)} %all_to_all.11.refs_0_), channel_id=1, source_target_pairs={{0,2},{1,3},{2,4},{3,5},{4,6},{5,7},{6,0},{7,1},{8,10},{9,11},{10,... | collective-permute-start | bytes 786440 | tf_op jit(solution)/shard_map/ppermute | solution.py:297
  67.5 1.7 %collective-permute-start.7 = (f32[32,16,128]{2,1,0:T(8,128)S(1)}, f32[32,16,128]{2,1,0:T(8,128)S(1)}, u32[]{:S(2)}, u32[]{:S(2)}) collective-permute-start(f32[32,16,128]{2,1,0:T(8,128)S(1)} %all_to_all.11.refs_0_), channel_id=1, source_target_pairs={{0,6},{1,7},{2,0},{3,1},{4,2},{5,3},{6,4},{7,5},{8,14},{9,15},{10,... | collective-permute-start | bytes 786440 | tf_op jit(solution)/shard_map/ppermute | solution.py:297
  69.2 2.6 %forward_0.1.refs_5_ = f32[2,128,1024]{2,1,0:T(8,128)S(1)} custom-call(s32[4,6]{1,0:T(4,128)S(1)} %copy-done, s32[1]{0:T(128)} %bitcast.me_ref, f32[32,16,128]{2,1,0:T(8,128)S(1)} %all_to_all.11.refs_0_, f32[32,16,128]{2,1,0:T(8,128)S(1)} %collective-permute-done.9.refs_1_, bf16[4,6,256,128]{3,2,1,0:T(8,128)(2,1)S(1)} %get-tuple-element.43.refs_2_.refs_4_, ...), custom_call_target="tpu_custom_call" | custom-call | flops 3000000000 | bytes 8000000 | tf_op jit(solution)/shard_map/forward_0/pallas_call | solution.py:332
  71.9 3.8 %collective-permute-done.8.refs_0_ = f32[32,16,128]{2,1,0:T(8,128)S(1)} collective-permute-done((f32[32,16,128]{2,1,0:T(8,128)S(1)}, f32[32,16,128]{2,1,0:T(8,128)S(1)}, u32[]{:S(2)}, u32[]{:S(2)}) %collective-permute-start.8) | collective-permute-done | bytes 262176 | tf_op jit(solution)/shard_map/ppermute | solution.py:297
  76.6 1.1 %collective-permute-start.11 = (f32[16,16,128]{2,1,0:T(8,128)S(1)}, f32[16,16,128]{2,1,0:T(8,128)S(1)}, u32[]{:S(2)}, u32[]{:S(2)}) collective-permute-start(f32[16,16,128]{2,1,0:T(8,128)S(1)} %slice.15), channel_id=1, source_target_pairs={{0,2},{1,3},{2,4},{3,5},{4,6},{5,7},{6,0},{7,1},{8,10},{9,11},{10,... | collective-permute-start | bytes 393224 | tf_op jit(solution)/shard_map/ppermute | solution.py:297
  77.7 1.8 %collective-permute-start.10 = (f32[16,16,128]{2,1,0:T(8,128)S(1)}, f32[16,16,128]{2,1,0:T(8,128)S(1)}, u32[]{:S(2)}, u32[]{:S(2)}) collective-permute-start(f32[16,16,128]{2,1,0:T(8,128)S(1)} %slice.14), channel_id=1, source_target_pairs={{0,6},{1,7},{2,0},{3,1},{4,2},{5,3},{6,4},{7,5},{8,14},{9,15},{10,... | collective-permute-start | bytes 393224 | tf_op jit(solution)/shard_map/ppermute | solution.py:297
  79.4 2.6 %forward_1.1.refs_5_ = f32[2,128,1024]{2,1,0:T(8,128)S(1)} custom-call(s32[4,6]{1,0:T(4,128)S(1)} %copy-done, s32[1]{0:T(128)} %bitcast.me_ref, f32[32,16,128]{2,1,0:T(8,128)S(1)} %collective-permute-done.7.refs_0_, f32[32,16,128]{2,1,0:T(8,128)S(1)} %collective-permute-done.12.refs_1_, bf16[4,6,256,128]{3,2,1,0:T(8,128)(2,1)S(1)} %get-tuple-element.43.refs_2_.refs_4_, ...), custom_call_target="tpu_custom_call" | custom-call | flops 3000000000 | bytes 8000000 | tf_op jit(solution)/shard_map/forward_1/pallas_call | solution.py:332
  82.5 1.3 %collective-permute-start.13 = (f32[16,16,128]{2,1,0:T(8,128)S(1)}, f32[16,16,128]{2,1,0:T(8,128)S(1)}, u32[]{:S(2)}, u32[]{:S(2)}) collective-permute-start(f32[16,16,128]{2,1,0:T(8,128)S(1)} %collective-permute-done.10.refs_0_), channel_id=1, source_target_pairs={{0,1},{1,0},{2,3},{3,2},{4,5},{5,4},{6,7},{7,6},{8,9},{9,8},{10,11... | collective-permute-start | bytes 393224 | tf_op jit(solution)/shard_map/ppermute | solution.py:294
  83.8 2.6 %forward_3.1.refs_7_ = f32[2,128,1024]{2,1,0:T(8,128)S(1)} custom-call(s32[4,6]{1,0:T(4,128)S(1)} %copy-done, s32[1]{0:T(128)} %bitcast.me_ref, f32[32,16,128]{2,1,0:T(8,128)S(1)} %collective-permute-done.8.refs_0_, f32[32,16,128]{2,1,0:T(8,128)S(1)} %collective-permute-done.15.refs_1_, bf16[4,6,256,128]{3,2,1,0:T(8,128)(2,1)S(1)} %get-tuple-element.43.refs_2_.refs_4_, ...), custom_call_target="tpu_custom_call" | custom-call | flops 3000000000 | bytes 8000000 | tf_op jit(solution)/shard_map/forward_3/pallas_call | solution.py:332
  86.5 3.4 %forward_2.1 = f32[2,128,1024]{2,1,0:T(8,128)} custom-call(s32[4,6]{1,0:T(4,128)S(1)} %copy-done, s32[1]{0:T(128)} %bitcast.me_ref, f32[16,16,128]{2,1,0:T(8,128)S(1)} %collective-permute-done.10.refs_0_, f32[16,16,128]{2,1,0:T(8,128)S(1)} %collective-permute-done.11.refs_1_, f32[16,16,128]{2,1,0:T(8,128)S(1)} %collective-permute-done.13.refs_2_, ...), custom_call_target="tpu_custom_call" | custom-call | flops 3000000000 | bytes 8000000 | tf_op jit(solution)/shard_map/forward_2/pallas_call | solution.py:332
  (35 shorter events, 2.7 us)
Async XLA Ops:
  0.0 9.1 %copy-start = (s32[4,6]{1,0:T(4,128)S(1)}, s32[4,6]{1,0:T(4,128)}, u32[]{:S(2)}) copy-start(s32[4,6]{1,0:T(4,128)} %src_ref.11) | copy-start | bytes 292
  5.8 5.2 %collective-permute-start = (f32[3,256,256]{2,1,0:T(8,128)S(1)}, f32[3,256,256]{2,1,0:T(8,128)S(1)}, u32[]{:S(2)}, u32[]{:S(2)}) collective-permute-start(f32[3,256,256]{2,1,0:T(8,128)S(1)} %get-tuple-element.32), channel_id=1, source_target_pairs={{0,1},{1,0},{2,3},{3,2},{4,5},{5,4},{6,7},{7,6},{8,9},{9,8},{10,11... | collective-permute-start | bytes 2359304 | tf_op jit(solution)/shard_map/ppermute | solution.py:294
  11.1 3.1 %collective-permute-start.1 = (f32[8,128]{1,0:T(8,128)S(1)}, f32[8,128]{1,0:T(8,128)S(1)}, u32[]{:S(2)}, u32[]{:S(2)}) collective-permute-start(f32[8,128]{1,0:T(8,128)S(1)} %slice_bitcast_fusion.1), channel_id=1, source_target_pairs={{0,1},{1,0},{2,3},{3,2},{4,5},{5,4},{6,7},{7,6},{8,9},{9,8},{10,11... | collective-permute-start | bytes 12296 | tf_op jit(solution)/shard_map/ppermute | solution.py:294
  11.6 9.0 %collective-permute-start.2 = (f32[2,128,256]{2,1,0:T(8,128)S(1)}, f32[2,128,256]{2,1,0:T(8,128)S(1)}, u32[]{:S(2)}, u32[]{:S(2)}) collective-permute-start(f32[2,128,256]{2,1,0:T(8,128)S(1)} %get-tuple-element.33), channel_id=1, source_target_pairs={{0,2},{1,3},{2,4},{3,5},{4,6},{5,7},{6,0},{7,1},{8,10},{9,11},{10,... | collective-permute-start | bytes 786440 | tf_op jit(solution)/shard_map/ppermute | solution.py:297
  11.6 7.9 %collective-permute-start.3 = (f32[2,128,256]{2,1,0:T(8,128)S(1)}, f32[2,128,256]{2,1,0:T(8,128)S(1)}, u32[]{:S(2)}, u32[]{:S(2)}) collective-permute-start(f32[2,128,256]{2,1,0:T(8,128)S(1)} %get-tuple-element.35), channel_id=1, source_target_pairs={{0,6},{1,7},{2,0},{3,1},{4,2},{5,3},{6,4},{7,5},{8,14},{9,15},{10,... | collective-permute-start | bytes 786440 | tf_op jit(solution)/shard_map/ppermute | solution.py:297
  15.8 29.7 %copy-start.2 = (s32[4,2048]{1,0:T(4,128)S(1)}, s32[4,2048]{1,0:T(4,128)}, u32[]{:S(2)}) copy-start(s32[4,2048]{1,0:T(4,128)} %onset_ref.1) | copy-start | bytes 98308
  15.8 29.7 %copy-start.3 = (bf16[896,192]{1,0:T(8,128)(2,1)S(1)}, bf16[896,192]{1,0:T(8,128)(2,1)}, u32[]{:S(2)}) copy-start(bf16[896,192]{1,0:T(8,128)(2,1)} %constant.8.clone.into_ref) | copy-start | bytes 1032196
  15.9 29.7 %copy-start.4 = (bf16[128,896]{1,0:T(8,128)(2,1)S(1)}, bf16[128,896]{1,0:T(8,128)(2,1)}, u32[]{:S(2)}) copy-start(bf16[128,896]{1,0:T(8,128)(2,1)} %constant.9.clone.outof_ref) | copy-start | bytes 688132
  15.9 4.7 %collective-permute-start.4 = (f32[256,256]{1,0:T(8,128)S(1)}, f32[256,256]{1,0:T(8,128)S(1)}, u32[]{:S(2)}, u32[]{:S(2)}) collective-permute-start(f32[256,256]{1,0:T(8,128)S(1)} %slice_bitcast_fusion), channel_id=1, source_target_pairs={{0,1},{1,0},{2,3},{3,2},{4,5},{5,4},{6,7},{7,6},{8,9},{9,8},{10,11... | collective-permute-start | bytes 786440 | tf_op jit(solution)/shard_map/ppermute | solution.py:294
  20.6 5.1 %collective-permute-start.5 = (f32[128,256]{1,0:T(8,128)S(1)}, f32[128,256]{1,0:T(8,128)S(1)}, u32[]{:S(2)}, u32[]{:S(2)}) collective-permute-start(f32[128,256]{1,0:T(8,128)S(1)} %get-tuple-element.41), channel_id=1, source_target_pairs={{0,2},{1,3},{2,4},{3,5},{4,6},{5,7},{6,0},{7,1},{8,10},{9,11},{10,... | collective-permute-start | bytes 393224 | tf_op jit(solution)/shard_map/ppermute | solution.py:297
  20.7 5.0 %collective-permute-start.6 = (f32[128,256]{1,0:T(8,128)S(1)}, f32[128,256]{1,0:T(8,128)S(1)}, u32[]{:S(2)}, u32[]{:S(2)}) collective-permute-start(f32[128,256]{1,0:T(8,128)S(1)} %get-tuple-element.42), channel_id=1, source_target_pairs={{0,6},{1,7},{2,0},{3,1},{4,2},{5,3},{6,4},{7,5},{8,14},{9,15},{10,... | collective-permute-start | bytes 393224 | tf_op jit(solution)/shard_map/ppermute | solution.py:297
  45.5 23.7 %copy-start.1 = (f32[1,2,128,1024]{3,2,1,0:T(8,128)S(1)}, f32[1,2,128,1024]{3,2,1,0:T(8,128)}, u32[]{:S(2)}) copy-start(f32[1,2,128,1024]{3,2,1,0:T(8,128)} %param.9) | copy-start | bytes 3145732
  61.8 7.4 %collective-permute-start.9 = (f32[32,16,128]{2,1,0:T(8,128)S(1)}, f32[32,16,128]{2,1,0:T(8,128)S(1)}, u32[]{:S(2)}, u32[]{:S(2)}) collective-permute-start(f32[32,16,128]{2,1,0:T(8,128)S(1)} %all_to_all.11.refs_0_), channel_id=1, source_target_pairs={{0,1},{1,0},{2,3},{3,2},{4,5},{5,4},{6,7},{7,6},{8,9},{9,8},{10,11... | collective-permute-start | bytes 786440 | tf_op jit(solution)/shard_map/ppermute | solution.py:294
  66.5 9.1 %collective-permute-start.8 = (f32[32,16,128]{2,1,0:T(8,128)S(1)}, f32[32,16,128]{2,1,0:T(8,128)S(1)}, u32[]{:S(2)}, u32[]{:S(2)}) collective-permute-start(f32[32,16,128]{2,1,0:T(8,128)S(1)} %all_to_all.11.refs_0_), channel_id=1, source_target_pairs={{0,2},{1,3},{2,4},{3,5},{4,6},{5,7},{6,0},{7,1},{8,10},{9,11},{10,... | collective-permute-start | bytes 786440 | tf_op jit(solution)/shard_map/ppermute | solution.py:297
  67.5 8.1 %collective-permute-start.7 = (f32[32,16,128]{2,1,0:T(8,128)S(1)}, f32[32,16,128]{2,1,0:T(8,128)S(1)}, u32[]{:S(2)}, u32[]{:S(2)}) collective-permute-start(f32[32,16,128]{2,1,0:T(8,128)S(1)} %all_to_all.11.refs_0_), channel_id=1, source_target_pairs={{0,6},{1,7},{2,0},{3,1},{4,2},{5,3},{6,4},{7,5},{8,14},{9,15},{10,... | collective-permute-start | bytes 786440 | tf_op jit(solution)/shard_map/ppermute | solution.py:297
  75.7 3.8 %collective-permute-start.12 = (f32[32,16,128]{2,1,0:T(8,128)S(1)}, f32[32,16,128]{2,1,0:T(8,128)S(1)}, u32[]{:S(2)}, u32[]{:S(2)}) collective-permute-start(f32[32,16,128]{2,1,0:T(8,128)S(1)} %collective-permute-done.7.refs_0_), channel_id=1, source_target_pairs={{0,1},{1,0},{2,3},{3,2},{4,5},{5,4},{6,7},{7,6},{8,9},{9,8},{10,11... | collective-permute-start | bytes 786440 | tf_op jit(solution)/shard_map/ppermute | solution.py:294
  76.5 7.3 %collective-permute-start.15 = (f32[32,16,128]{2,1,0:T(8,128)S(1)}, f32[32,16,128]{2,1,0:T(8,128)S(1)}, u32[]{:S(2)}, u32[]{:S(2)}) collective-permute-start(f32[32,16,128]{2,1,0:T(8,128)S(1)} %collective-permute-done.8.refs_0_), channel_id=1, source_target_pairs={{0,1},{1,0},{2,3},{3,2},{4,5},{5,4},{6,7},{7,6},{8,9},{9,8},{10,11... | collective-permute-start | bytes 786440 | tf_op jit(solution)/shard_map/ppermute | solution.py:294
  76.6 6.0 %collective-permute-start.11 = (f32[16,16,128]{2,1,0:T(8,128)S(1)}, f32[16,16,128]{2,1,0:T(8,128)S(1)}, u32[]{:S(2)}, u32[]{:S(2)}) collective-permute-start(f32[16,16,128]{2,1,0:T(8,128)S(1)} %slice.15), channel_id=1, source_target_pairs={{0,2},{1,3},{2,4},{3,5},{4,6},{5,7},{6,0},{7,1},{8,10},{9,11},{10,... | collective-permute-start | bytes 393224 | tf_op jit(solution)/shard_map/ppermute | solution.py:297
  77.7 4.9 %collective-permute-start.10 = (f32[16,16,128]{2,1,0:T(8,128)S(1)}, f32[16,16,128]{2,1,0:T(8,128)S(1)}, u32[]{:S(2)}, u32[]{:S(2)}) collective-permute-start(f32[16,16,128]{2,1,0:T(8,128)S(1)} %slice.14), channel_id=1, source_target_pairs={{0,6},{1,7},{2,0},{3,1},{4,2},{5,3},{6,4},{7,5},{8,14},{9,15},{10,... | collective-permute-start | bytes 393224 | tf_op jit(solution)/shard_map/ppermute | solution.py:297
  82.5 3.9 %collective-permute-start.13 = (f32[16,16,128]{2,1,0:T(8,128)S(1)}, f32[16,16,128]{2,1,0:T(8,128)S(1)}, u32[]{:S(2)}, u32[]{:S(2)}) collective-permute-start(f32[16,16,128]{2,1,0:T(8,128)S(1)} %collective-permute-done.10.refs_0_), channel_id=1, source_target_pairs={{0,1},{1,0},{2,3},{3,2},{4,5},{5,4},{6,7},{7,6},{8,9},{9,8},{10,11... | collective-permute-start | bytes 393224 | tf_op jit(solution)/shard_map/ppermute | solution.py:294
  83.8 2.7 %collective-permute-start.14 = (f32[16,16,128]{2,1,0:T(8,128)S(1)}, f32[16,16,128]{2,1,0:T(8,128)S(1)}, u32[]{:S(2)}, u32[]{:S(2)}) collective-permute-start(f32[16,16,128]{2,1,0:T(8,128)S(1)} %collective-permute-done.11.refs_1_), channel_id=1, source_target_pairs={{0,1},{1,0},{2,3},{3,2},{4,5},{5,4},{6,7},{7,6},{8,9},{9,8},{10,11... | collective-permute-start | bytes 393224 | tf_op jit(solution)/shard_map/ppermute | solution.py:294

commit v3 on v2

--- a/solution.py
+++ b/solution.py
@@ -83,9 +83,12 @@
         )
     rights = [pltpu.make_async_copy(right_hbm.at[p], raw_ref.at[p], sems.at[2, p]) for p in range(panels)]
     names = pltpu.make_async_copy(src_hbm, src_ref, sems.at[3, 0])
-    for pair in copies[:2]:
+    for pair in copies:
         pair[0].start()
         pair[1].start()
+    for copy in rights:
+        copy.start()
+    names.start()
     last = panels * slots
     coef_h[last] = jnp.zeros(coef_h.shape[1:], BF16)
     coef_l[last] = jnp.zeros(coef_l.shape[1:], BF16)
@@ -93,13 +96,6 @@
     for p in range(panels):
         copies[p][0].wait()
         copies[p][1].wait()
-        if p + 2 < panels:
-            copies[p + 2][0].start()
-            copies[p + 2][1].start()
-        elif p + 2 == panels:
-            names.start()
-            for copy in rights:
-                copy.start()
         field_h, field_l = split(field_ref[p].reshape(-1, tile))
         for s in range(0, slots, 2):
             left_h, left_l = split(jnp.concatenate([left_ref[p, s], left_ref[p, s + 1]], axis=1))
@@ -160,17 +156,16 @@
         out_ref[:, 8 * c : 8 * c + 8, :] = jnp.stack([even, odd], axis=1).reshape(rows // 4, 8, lanes)
 
 
-def gate_kernel(_, me_ref, x_ref, onset_ref, into_ref, outof_ref, y_ref):
+def gate_kernel(me_ref, x_ref, onset_ref, into_ref, outof_ref, y_ref):
     group = onset_ref.shape[0]
     lanes = x_ref.shape[1]
-    here = pl.ds(pl.multiple_of(me_ref[0] * (2 * lanes), 2 * lanes), 2 * lanes)
     bands = outof_ref.shape[0] // 2
     for v in range(group):
         picks = [pl.ds(h * group + v, bands, stride=2 * group) for h in range(2)]
         high, low = split(jnp.concatenate([x_ref[pick, :] for pick in picks], axis=1))
         traces = dot(into_ref[...], jnp.concatenate([high, high, low], axis=0))
         when = lax.broadcasted_iota(jnp.int32, traces.shape, 0)
-        gated = jnp.where(when < onset_ref[v : v + 1, here], traces, 0.0)
+        gated = jnp.where(when < onset_ref[v : v + 1, :], traces, 0.0)
         high, low = split(gated)
         pair = dot(outof_ref[...], high)
         back = pair[:bands] + pair[bands:] + dot(outof_ref[:bands, :], low)
@@ -196,9 +191,8 @@
             second = jnp.where(low, pltpu.roll(even, 4, 1), odd).reshape(count * 4, lanes)
             parts.append(jnp.concatenate([first, second], axis=1))
         tiles.append(split(jnp.concatenate(parts, axis=0)))
-    copies = []
-    for p in range(panels):
-        at = slice(p * tile, (p + 1) * tile)
+    found = []
+    for p in range(panels):
         parts = []
         for i, (high, low) in enumerate(tiles):
             slot, place = find_slot(src_ref, p, tile_of(me, steps[i // 2], i % 2), slots)
@@ -206,7 +200,11 @@
             pair = dot(high, right)
             products = pair[:, :width] + pair[:, width:] + dot(low, right[:, :width])
             parts.append(split(pair_coef(products, width // 2)) + (left_h[p, slot], left_l[p, slot]))
-        high, low, there_h, there_l = (jnp.concatenate(x, axis=1) for x in zip(*parts))
+        found.append(parts)
+    copies = []
+    for p in range(panels):
+        at = slice(p * tile, (p + 1) * tile)
+        high, low, there_h, there_l = (jnp.concatenate(x, axis=1) for x in zip(*found[p]))
         result = dot(high, there_h, NT_DIMS) + dot(low, there_h, NT_DIMS) + dot(high, there_l, NT_DIMS)
         result = total_ref[:, :, at] - result.reshape(total_ref.shape[0], total_ref.shape[1], tile)
         if last:
@@ -320,11 +318,24 @@
     moved = lax.all_to_all(moved, "freq", split_axis=0, concat_axis=0, tiled=True)
 
     into, outof = time_tables(count)
-    (gated,) = local(
+    whole = lambda shape: pl.BlockSpec(shape, lambda i, *_: (0,) * len(shape))
+    gated = pl.pallas_call(
         gate_kernel,
-        [((2 * rows, tile // 2), F32)],
-        tile_src, me, moved.reshape(2 * rows, tile // 2), onset, jnp.asarray(into), jnp.asarray(outof), limit=12,
-    )
+        grid_spec=pltpu.PrefetchScalarGridSpec(
+            num_scalar_prefetch=1,
+            grid=(1,),
+            in_specs=[
+                whole((2 * rows, tile // 2)),
+                pl.BlockSpec((group, tile), lambda i, me_ref: (0, me_ref[0])),
+                whole(into.shape),
+                whole(outof.shape),
+            ],
+            out_specs=whole((2 * rows, tile // 2)),
+        ),
+        out_shape=jax.ShapeDtypeStruct((2 * rows, tile // 2), F32),
+        compiler_params=pltpu.CompilerParams(vmem_limit_bytes=12 * mib),
+        name="gate",
+    )(me, moved.reshape(2 * rows, tile // 2), onset, jnp.asarray(into), jnp.asarray(outof))
     back = lax.all_to_all(gated.reshape(count, 4 * group, tile // 2), "freq", split_axis=0, concat_axis=0, tiled=True)
 
     def forward(steps, tiles, total, last=False):

time: 90.2 us -> 87.6 us (0.971)
  Pallas kernels: 22.5 us -> 18.1 us
  waiting for transfers between devices: 11 us -> 12.8 us
    pallas_call x4, Pallas kernels: 11.3 us -> 7.85 us  [forward(): pl.pallas_call(functools.partial(forward_kernel, steps, last, number // (...]
    pallas_call x6 -> x5, Pallas kernels: 5.35 us -> 3.14 us  [local(): pl.pallas_call(kernel, in_specs=[in_smem] * (2 * scalars) + [in_vmem] * (...]
    ppermute x8, waiting for transfers between devices: 10.5 us -> 12.3 us  [shift(): return lax.ppermute(x, 'panel', [(i, (i + 2 * by) % 8) for i in range(8)])]
    pallas_call x0 -> x1, Pallas kernels: none -> 1.63 us  [shards(): pl.pallas_call(gate_kernel, grid_spec=pltpu.PrefetchScalarGridSpec(num_sc...]
  transfers between devices with their start and end apart: 16 -> 16, of which waited for: 6 -> 6; matrix products, arithmetic and copies ran while one was open for 0% -> 0% of each run, Pallas kernels for 12% -> 9%
where the time goes in v3:
time: 87.6 us; the launch traced here: 87.4 us
  blocking collectives  33.7 us (38%)
  starting transfers between devices  22.4 us (26%)
  Pallas kernels  18.1 us (21%)
  waiting for transfers between devices  12.8 us (15%)
    all_to_all x1, blocking collectives, shards(): lax.all_to_all(moved, 'freq', split_axis=0, concat_axis=0, tiled=True)  19.7 us
    all_to_all x1, blocking collectives, shards(): lax.all_to_all(gated.reshape(count, 4 * group, tile // 2), 'freq', split_...  14 us
    ppermute x8, waiting for transfers between devices, shift(): return lax.ppermute(x, 'panel', [(i, (i + 2 * by) % 8) for i in range(8)])  12.3 us
    ppermute x8, starting transfers between devices, exchange(): return lax.ppermute(x, 'panel', swap)  11.5 us
    ppermute x8, starting transfers between devices, shift(): return lax.ppermute(x, 'panel', [(i, (i + 2 * by) % 8) for i in range(8)])  10.9 us
    pallas_call x4, Pallas kernels, forward(): pl.pallas_call(functools.partial(forward_kernel, steps, last, number // (...  7.85 us
    pallas_call x1, Pallas kernels, shards(): pl.pallas_call(adjoint_kernel, in_specs=[in_smem] + [in_hbm] * 4, out_spe...  5.5 us
    pallas_call x5, Pallas kernels, local(): pl.pallas_call(kernel, in_specs=[in_smem] * (2 * scalars) + [in_vmem] * (...  3.14 us
  transfers between devices with their start and end apart: 16, of which 6 were waited for; matrix products, arithmetic and copies ran while one was open for 0% of the time, Pallas kernels for 9%

profile of v3, /device:TPU:1, one launch (start us, length us, event | category | flops | bytes accessed | tf_op | source)
XLA Modules:
  0.0 87.4 jit_solution(6506708820735950363)
XLA Ops:
  0.0 5.5 %adjoint.1 = (bf16[25,256,128]{2,1,0:T(8,128)(2,1)S(1)}, bf16[25,256,128]{2,1,0:T(8,128)(2,1)S(1)}, bf16[25,256,256]{2,1,0:T(8,128)(2,1)S(1)}, f32[4,6,256,128]{3,2,1,0:T(8,128)S(1)}, f32[3,256,256]{2,1,0:T(8,128)S(1)}) custom-call(s32[1]{0:T(128)} %bitcast.me_ref, s32[4,6]{1,0:T(4,128)} %src_ref.11, f32[2,128,1024]{2,1,0:T(8,128)} %bitcast.19, ...), custom_call_target="tpu_custom_call" | custom-call | tf_op jit(solution)/shard_map/adjoint/pallas_call | solution.py:258
  5.5 3.3 %collective-permute-start = (f32[3,256,256]{2,1,0:T(8,128)S(1)}, f32[3,256,256]{2,1,0:T(8,128)S(1)}, u32[]{:S(2)}, u32[]{:S(2)}) collective-permute-start(f32[3,256,256]{2,1,0:T(8,128)S(1)} %get-tuple-element.32), channel_id=1, source_target_pairs={{0,1},{1,0},{2,3},{3,2},{4,5},{5,4},{6,7},{7,6},{8,9},{9,8},{10,11... | collective-permute-start | bytes 2359304 | tf_op jit(solution)/shard_map/ppermute | solution.py:292
  8.8 1.4 %own_kernel.1.own_ref = f32[3,256,256]{2,1,0:T(8,128)S(1)} custom-call(s32[4,6]{1,0:T(4,128)S(1)} %copy-done.3, s32[1]{0:T(128)} %bitcast.me_ref, bf16[25,256,128]{2,1,0:T(8,128)(2,1)S(1)} %get-tuple-element.28.coef_h, bf16[25,256,128]{2,1,0:T(8,128)(2,1)S(1)} %get-tuple-element.29.coef_l, bf16[25,256,256]{2,1,0:T(8,128)(2,1)S(1)} %get-tuple-element.30.right_ref.refs_4_.refs_6_), custom_call_target="tpu_custom_call" | custom-call | flops 3000000000 | bytes 8000000 | tf_op jit(solution)/shard_map/own_kernel/pallas_call | solution.py:279
  11.3 2.7 %collective-permute-start.3 = (f32[2,128,256]{2,1,0:T(8,128)S(1)}, f32[2,128,256]{2,1,0:T(8,128)S(1)}, u32[]{:S(2)}, u32[]{:S(2)}) collective-permute-start(f32[2,128,256]{2,1,0:T(8,128)S(1)} %get-tuple-element.35), channel_id=1, source_target_pairs={{0,6},{1,7},{2,0},{3,1},{4,2},{5,3},{6,4},{7,5},{8,14},{9,15},{10,... | collective-permute-start | bytes 786440 | tf_op jit(solution)/shard_map/ppermute | solution.py:295
  14.0 1.6 %here_kernel.1 = (f32[2,256,256]{2,1,0:T(8,128)S(1)}, bf16[4,6,256,128]{3,2,1,0:T(8,128)(2,1)S(1)}, bf16[4,6,256,128]{3,2,1,0:T(8,128)(2,1)S(1)}) custom-call(s32[4,6]{1,0:T(4,128)S(1)} %copy-done.3, s32[1]{0:T(128)} %bitcast.me_ref, bf16[25,256,128]{2,1,0:T(8,128)(2,1)S(1)} %get-tuple-element.28.coef_h, bf16[25,256,128]{2,1,0:T(8,128)(2,1)S(1)} %get-tuple-element.29.coef_l, ...), custom_call_target="tpu_custom_call" | custom-call | flops 3000000000 | bytes 8000000 | tf_op jit(solution)/shard_map/here_kernel/pallas_call | solution.py:279
  16.4 2.8 %collective-permute-done.3.from_above.above = f32[2,128,256]{2,1,0:T(8,128)S(1)} collective-permute-done((f32[2,128,256]{2,1,0:T(8,128)S(1)}, f32[2,128,256]{2,1,0:T(8,128)S(1)}, u32[]{:S(2)}, u32[]{:S(2)}) %collective-permute-start.3) | collective-permute-done | bytes 262176 | tf_op jit(solution)/shard_map/ppermute | solution.py:295
  19.2 1.1 %collective-permute-done.2.from_below.below = f32[2,128,256]{2,1,0:T(8,128)S(1)} collective-permute-done((f32[2,128,256]{2,1,0:T(8,128)S(1)}, f32[2,128,256]{2,1,0:T(8,128)S(1)}, u32[]{:S(2)}, u32[]{:S(2)}) %collective-permute-start.2) | collective-permute-done | bytes 262176 | tf_op jit(solution)/shard_map/ppermute | solution.py:295
  20.4 2.7 %collective-permute-start.6 = (f32[128,256]{1,0:T(8,128)S(1)}, f32[128,256]{1,0:T(8,128)S(1)}, u32[]{:S(2)}, u32[]{:S(2)}) collective-permute-start(f32[128,256]{1,0:T(8,128)S(1)} %get-tuple-element.42), channel_id=1, source_target_pairs={{0,6},{1,7},{2,0},{3,1},{4,2},{5,3},{6,4},{7,5},{8,14},{9,15},{10,... | collective-permute-start | bytes 393224 | tf_op jit(solution)/shard_map/ppermute | solution.py:295
  23.1 2.4 %collective-permute-done.5.relayed_below = f32[128,256]{1,0:T(8,128)S(1)} collective-permute-done((f32[128,256]{1,0:T(8,128)S(1)}, f32[128,256]{1,0:T(8,128)S(1)}, u32[]{:S(2)}, u32[]{:S(2)}) %collective-permute-start.5) | collective-permute-done | bytes 131104 | tf_op jit(solution)/shard_map/ppermute | solution.py:295
  25.5 19.7 %all_to_all.10 = f32[32,16,128]{2,1,0:T(8,128)S(1)} all-to-all(f32[32,16,128]{2,1,0:T(8,128)S(1)} %sum_kernel.1), channel_id=1, replica_groups=mesh['freq'=32,'panel'=8] {'freq'}, dimensions={0} | all-to-all | bytes 524288 | tf_op jit(solution)/shard_map/all_to_all | solution.py:318
  45.2 1.6 %gate.1 = f32[512,128]{1,0:T(8,128)S(1)} custom-call(s32[1]{0:T(128)} %bitcast.me_ref, f32[512,128]{1,0:T(8,128)S(1)} %bitcast.14, s32[4,2048]{1,0:T(4,128)S(1)} %copy-done.2, bf16[896,192]{1,0:T(8,128)(2,1)S(1)} %copy-done, bf16[128,896]{1,0:T(8,128)(2,1)S(1)} %copy-done.1), custom_call_target="tpu_custom_call" | custom-call | tf_op jit(solution)/shard_map/gate/pallas_call | solution.py:322
  46.9 14.0 %all_to_all.11.refs_0_ = f32[32,16,128]{2,1,0:T(8,128)S(1)} all-to-all(f32[32,16,128]{2,1,0:T(8,128)S(1)} %bitcast.15), channel_id=1, replica_groups=mesh['freq'=32,'panel'=8] {'freq'}, dimensions={0} | all-to-all | bytes 524288 | tf_op jit(solution)/shard_map/all_to_all | solution.py:339
  60.9 4.7 %collective-permute-start.9 = (f32[32,16,128]{2,1,0:T(8,128)S(1)}, f32[32,16,128]{2,1,0:T(8,128)S(1)}, u32[]{:S(2)}, u32[]{:S(2)}) collective-permute-start(f32[32,16,128]{2,1,0:T(8,128)S(1)} %all_to_all.11.refs_0_), channel_id=1, source_target_pairs={{0,1},{1,0},{2,3},{3,2},{4,5},{5,4},{6,7},{7,6},{8,9},{9,8},{10,11... | collective-permute-start | bytes 786440 | tf_op jit(solution)/shard_map/ppermute | solution.py:292
  65.6 1.0 %collective-permute-start.8 = (f32[32,16,128]{2,1,0:T(8,128)S(1)}, f32[32,16,128]{2,1,0:T(8,128)S(1)}, u32[]{:S(2)}, u32[]{:S(2)}) collective-permute-start(f32[32,16,128]{2,1,0:T(8,128)S(1)} %all_to_all.11.refs_0_), channel_id=1, source_target_pairs={{0,2},{1,3},{2,4},{3,5},{4,6},{5,7},{6,0},{7,1},{8,10},{9,11},{10,... | collective-permute-start | bytes 786440 | tf_op jit(solution)/shard_map/ppermute | solution.py:295
  66.6 1.7 %collective-permute-start.7 = (f32[32,16,128]{2,1,0:T(8,128)S(1)}, f32[32,16,128]{2,1,0:T(8,128)S(1)}, u32[]{:S(2)}, u32[]{:S(2)}) collective-permute-start(f32[32,16,128]{2,1,0:T(8,128)S(1)} %all_to_all.11.refs_0_), channel_id=1, source_target_pairs={{0,6},{1,7},{2,0},{3,1},{4,2},{5,3},{6,4},{7,5},{8,14},{9,15},{10,... | collective-permute-start | bytes 786440 | tf_op jit(solution)/shard_map/ppermute | solution.py:295
  68.3 1.8 %forward_0.1.refs_5_ = f32[2,128,1024]{2,1,0:T(8,128)S(1)} custom-call(s32[4,6]{1,0:T(4,128)S(1)} %copy-done.3, s32[1]{0:T(128)} %bitcast.me_ref, f32[32,16,128]{2,1,0:T(8,128)S(1)} %all_to_all.11.refs_0_, f32[32,16,128]{2,1,0:T(8,128)S(1)} %collective-permute-done.9.refs_1_, bf16[4,6,256,128]{3,2,1,0:T(8,128)(2,1)S(1)} %get-tuple-element.43.refs_2_.refs_4_, ...), custom_call_target="tpu_custom_call" | custom-call | flops 3000000000 | bytes 8000000 | tf_op jit(solution)/shard_map/forward_0/pallas_call | solution.py:343
  70.1 4.7 %collective-permute-done.8.refs_0_ = f32[32,16,128]{2,1,0:T(8,128)S(1)} collective-permute-done((f32[32,16,128]{2,1,0:T(8,128)S(1)}, f32[32,16,128]{2,1,0:T(8,128)S(1)}, u32[]{:S(2)}, u32[]{:S(2)}) %collective-permute-start.8) | collective-permute-done | bytes 262176 | tf_op jit(solution)/shard_map/ppermute | solution.py:295
  75.7 1.1 %collective-permute-start.11 = (f32[16,16,128]{2,1,0:T(8,128)S(1)}, f32[16,16,128]{2,1,0:T(8,128)S(1)}, u32[]{:S(2)}, u32[]{:S(2)}) collective-permute-start(f32[16,16,128]{2,1,0:T(8,128)S(1)} %slice.15), channel_id=1, source_target_pairs={{0,2},{1,3},{2,4},{3,5},{4,6},{5,7},{6,0},{7,1},{8,10},{9,11},{10,... | collective-permute-start | bytes 393224 | tf_op jit(solution)/shard_map/ppermute | solution.py:295
  76.8 1.8 %collective-permute-start.10 = (f32[16,16,128]{2,1,0:T(8,128)S(1)}, f32[16,16,128]{2,1,0:T(8,128)S(1)}, u32[]{:S(2)}, u32[]{:S(2)}) collective-permute-start(f32[16,16,128]{2,1,0:T(8,128)S(1)} %slice.14), channel_id=1, source_target_pairs={{0,6},{1,7},{2,0},{3,1},{4,2},{5,3},{6,4},{7,5},{8,14},{9,15},{10,... | collective-permute-start | bytes 393224 | tf_op jit(solution)/shard_map/ppermute | solution.py:295
  78.6 1.8 %forward_1.1.refs_5_ = f32[2,128,1024]{2,1,0:T(8,128)S(1)} custom-call(s32[4,6]{1,0:T(4,128)S(1)} %copy-done.3, s32[1]{0:T(128)} %bitcast.me_ref, f32[32,16,128]{2,1,0:T(8,128)S(1)} %collective-permute-done.7.refs_0_, f32[32,16,128]{2,1,0:T(8,128)S(1)} %collective-permute-done.12.refs_1_, bf16[4,6,256,128]{3,2,1,0:T(8,128)(2,1)S(1)} %get-tuple-element.43.refs_2_.refs_4_, ...), custom_call_target="tpu_custom_call" | custom-call | flops 3000000000 | bytes 8000000 | tf_op jit(solution)/shard_map/forward_1/pallas_call | solution.py:343
  80.3 1.3 %collective-permute-done.11.refs_1_ = f32[16,16,128]{2,1,0:T(8,128)S(1)} collective-permute-done((f32[16,16,128]{2,1,0:T(8,128)S(1)}, f32[16,16,128]{2,1,0:T(8,128)S(1)}, u32[]{:S(2)}, u32[]{:S(2)}) %collective-permute-start.11) | collective-permute-done | bytes 131104 | tf_op jit(solution)/shard_map/ppermute | solution.py:295
  81.7 1.3 %collective-permute-start.13 = (f32[16,16,128]{2,1,0:T(8,128)S(1)}, f32[16,16,128]{2,1,0:T(8,128)S(1)}, u32[]{:S(2)}, u32[]{:S(2)}) collective-permute-start(f32[16,16,128]{2,1,0:T(8,128)S(1)} %collective-permute-done.10.refs_0_), channel_id=1, source_target_pairs={{0,1},{1,0},{2,3},{3,2},{4,5},{5,4},{6,7},{7,6},{8,9},{9,8},{10,11... | collective-permute-start | bytes 393224 | tf_op jit(solution)/shard_map/ppermute | solution.py:292
  82.9 1.8 %forward_3.1.refs_7_ = f32[2,128,1024]{2,1,0:T(8,128)S(1)} custom-call(s32[4,6]{1,0:T(4,128)S(1)} %copy-done.3, s32[1]{0:T(128)} %bitcast.me_ref, f32[32,16,128]{2,1,0:T(8,128)S(1)} %collective-permute-done.8.refs_0_, f32[32,16,128]{2,1,0:T(8,128)S(1)} %collective-permute-done.15.refs_1_, bf16[4,6,256,128]{3,2,1,0:T(8,128)(2,1)S(1)} %get-tuple-element.43.refs_2_.refs_4_, ...), custom_call_target="tpu_custom_call" | custom-call | flops 3000000000 | bytes 8000000 | tf_op jit(solution)/shard_map/forward_3/pallas_call | solution.py:343
  84.7 2.6 %forward_2.1 = f32[2,128,1024]{2,1,0:T(8,128)} custom-call(s32[4,6]{1,0:T(4,128)S(1)} %copy-done.3, s32[1]{0:T(128)} %bitcast.me_ref, f32[16,16,128]{2,1,0:T(8,128)S(1)} %collective-permute-done.10.refs_0_, f32[16,16,128]{2,1,0:T(8,128)S(1)} %collective-permute-done.11.refs_1_, f32[16,16,128]{2,1,0:T(8,128)S(1)} %collective-permute-done.13.refs_2_, ...), custom_call_target="tpu_custom_call" | custom-call | flops 3000000000 | bytes 8000000 | tf_op jit(solution)/shard_map/forward_2/pallas_call | solution.py:343
  (35 shorter events, 3.0 us)
Async XLA Ops:
  0.0 8.8 %copy-start.3 = (s32[4,6]{1,0:T(4,128)S(1)}, s32[4,6]{1,0:T(4,128)}, u32[]{:S(2)}) copy-start(s32[4,6]{1,0:T(4,128)} %src_ref.11) | copy-start | bytes 292
  5.5 5.2 %collective-permute-start = (f32[3,256,256]{2,1,0:T(8,128)S(1)}, f32[3,256,256]{2,1,0:T(8,128)S(1)}, u32[]{:S(2)}, u32[]{:S(2)}) collective-permute-start(f32[3,256,256]{2,1,0:T(8,128)S(1)} %get-tuple-element.32), channel_id=1, source_target_pairs={{0,1},{1,0},{2,3},{3,2},{4,5},{5,4},{6,7},{7,6},{8,9},{9,8},{10,11... | collective-permute-start | bytes 2359304 | tf_op jit(solution)/shard_map/ppermute | solution.py:292
  10.8 3.1 %collective-permute-start.1 = (f32[8,128]{1,0:T(8,128)S(1)}, f32[8,128]{1,0:T(8,128)S(1)}, u32[]{:S(2)}, u32[]{:S(2)}) collective-permute-start(f32[8,128]{1,0:T(8,128)S(1)} %slice_bitcast_fusion.1), channel_id=1, source_target_pairs={{0,1},{1,0},{2,3},{3,2},{4,5},{5,4},{6,7},{7,6},{8,9},{9,8},{10,11... | collective-permute-start | bytes 12296 | tf_op jit(solution)/shard_map/ppermute | solution.py:292
  11.3 9.0 %collective-permute-start.2 = (f32[2,128,256]{2,1,0:T(8,128)S(1)}, f32[2,128,256]{2,1,0:T(8,128)S(1)}, u32[]{:S(2)}, u32[]{:S(2)}) collective-permute-start(f32[2,128,256]{2,1,0:T(8,128)S(1)} %get-tuple-element.33), channel_id=1, source_target_pairs={{0,2},{1,3},{2,4},{3,5},{4,6},{5,7},{6,0},{7,1},{8,10},{9,11},{10,... | collective-permute-start | bytes 786440 | tf_op jit(solution)/shard_map/ppermute | solution.py:295
  11.3 7.9 %collective-permute-start.3 = (f32[2,128,256]{2,1,0:T(8,128)S(1)}, f32[2,128,256]{2,1,0:T(8,128)S(1)}, u32[]{:S(2)}, u32[]{:S(2)}) collective-permute-start(f32[2,128,256]{2,1,0:T(8,128)S(1)} %get-tuple-element.35), channel_id=1, source_target_pairs={{0,6},{1,7},{2,0},{3,1},{4,2},{5,3},{6,4},{7,5},{8,14},{9,15},{10,... | collective-permute-start | bytes 786440 | tf_op jit(solution)/shard_map/ppermute | solution.py:295
  15.5 29.7 %copy-start = (bf16[896,192]{1,0:T(8,128)(2,1)S(1)}, bf16[896,192]{1,0:T(8,128)(2,1)}, u32[]{:S(2)}) copy-start(bf16[896,192]{1,0:T(8,128)(2,1)} %constant.8.clone.into_ref) | copy-start | bytes 1032196
  15.6 29.7 %copy-start.1 = (bf16[128,896]{1,0:T(8,128)(2,1)S(1)}, bf16[128,896]{1,0:T(8,128)(2,1)}, u32[]{:S(2)}) copy-start(bf16[128,896]{1,0:T(8,128)(2,1)} %constant.9.clone.outof_ref) | copy-start | bytes 688132
  15.6 29.7 %copy-start.2 = (s32[4,2048]{1,0:T(4,128)S(1)}, s32[4,2048]{1,0:T(4,128)}, u32[]{:S(2)}) copy-start(s32[4,2048]{1,0:T(4,128)} %onset_ref.1) | copy-start | bytes 98308
  15.6 52.7 %copy-start.4 = (f32[1,2,128,1024]{3,2,1,0:T(8,128)S(1)}, f32[1,2,128,1024]{3,2,1,0:T(8,128)}, u32[]{:S(2)}) copy-start(f32[1,2,128,1024]{3,2,1,0:T(8,128)} %param.9) | copy-start | bytes 3145732
  15.6 4.7 %collective-permute-start.4 = (f32[256,256]{1,0:T(8,128)S(1)}, f32[256,256]{1,0:T(8,128)S(1)}, u32[]{:S(2)}, u32[]{:S(2)}) collective-permute-start(f32[256,256]{1,0:T(8,128)S(1)} %slice_bitcast_fusion), channel_id=1, source_target_pairs={{0,1},{1,0},{2,3},{3,2},{4,5},{5,4},{6,7},{7,6},{8,9},{9,8},{10,11... | collective-permute-start | bytes 786440 | tf_op jit(solution)/shard_map/ppermute | solution.py:292
  20.3 5.1 %collective-permute-start.5 = (f32[128,256]{1,0:T(8,128)S(1)}, f32[128,256]{1,0:T(8,128)S(1)}, u32[]{:S(2)}, u32[]{:S(2)}) collective-permute-start(f32[128,256]{1,0:T(8,128)S(1)} %get-tuple-element.41), channel_id=1, source_target_pairs={{0,2},{1,3},{2,4},{3,5},{4,6},{5,7},{6,0},{7,1},{8,10},{9,11},{10,... | collective-permute-start | bytes 393224 | tf_op jit(solution)/shard_map/ppermute | solution.py:295
  20.4 5.0 %collective-permute-start.6 = (f32[128,256]{1,0:T(8,128)S(1)}, f32[128,256]{1,0:T(8,128)S(1)}, u32[]{:S(2)}, u32[]{:S(2)}) collective-permute-start(f32[128,256]{1,0:T(8,128)S(1)} %get-tuple-element.42), channel_id=1, source_target_pairs={{0,6},{1,7},{2,0},{3,1},{4,2},{5,3},{6,4},{7,5},{8,14},{9,15},{10,... | collective-permute-start | bytes 393224 | tf_op jit(solution)/shard_map/ppermute | solution.py:295
  60.9 7.4 %collective-permute-start.9 = (f32[32,16,128]{2,1,0:T(8,128)S(1)}, f32[32,16,128]{2,1,0:T(8,128)S(1)}, u32[]{:S(2)}, u32[]{:S(2)}) collective-permute-start(f32[32,16,128]{2,1,0:T(8,128)S(1)} %all_to_all.11.refs_0_), channel_id=1, source_target_pairs={{0,1},{1,0},{2,3},{3,2},{4,5},{5,4},{6,7},{7,6},{8,9},{9,8},{10,11... | collective-permute-start | bytes 786440 | tf_op jit(solution)/shard_map/ppermute | solution.py:292
  65.6 9.1 %collective-permute-start.8 = (f32[32,16,128]{2,1,0:T(8,128)S(1)}, f32[32,16,128]{2,1,0:T(8,128)S(1)}, u32[]{:S(2)}, u32[]{:S(2)}) collective-permute-start(f32[32,16,128]{2,1,0:T(8,128)S(1)} %all_to_all.11.refs_0_), channel_id=1, source_target_pairs={{0,2},{1,3},{2,4},{3,5},{4,6},{5,7},{6,0},{7,1},{8,10},{9,11},{10,... | collective-permute-start | bytes 786440 | tf_op jit(solution)/shard_map/ppermute | solution.py:295
  66.6 8.1 %collective-permute-start.7 = (f32[32,16,128]{2,1,0:T(8,128)S(1)}, f32[32,16,128]{2,1,0:T(8,128)S(1)}, u32[]{:S(2)}, u32[]{:S(2)}) collective-permute-start(f32[32,16,128]{2,1,0:T(8,128)S(1)} %all_to_all.11.refs_0_), channel_id=1, source_target_pairs={{0,6},{1,7},{2,0},{3,1},{4,2},{5,3},{6,4},{7,5},{8,14},{9,15},{10,... | collective-permute-start | bytes 786440 | tf_op jit(solution)/shard_map/ppermute | solution.py:295
  74.8 3.8 %collective-permute-start.12 = (f32[32,16,128]{2,1,0:T(8,128)S(1)}, f32[32,16,128]{2,1,0:T(8,128)S(1)}, u32[]{:S(2)}, u32[]{:S(2)}) collective-permute-start(f32[32,16,128]{2,1,0:T(8,128)S(1)} %collective-permute-done.7.refs_0_), channel_id=1, source_target_pairs={{0,1},{1,0},{2,3},{3,2},{4,5},{5,4},{6,7},{7,6},{8,9},{9,8},{10,11... | collective-permute-start | bytes 786440 | tf_op jit(solution)/shard_map/ppermute | solution.py:292
  75.6 7.3 %collective-permute-start.15 = (f32[32,16,128]{2,1,0:T(8,128)S(1)}, f32[32,16,128]{2,1,0:T(8,128)S(1)}, u32[]{:S(2)}, u32[]{:S(2)}) collective-permute-start(f32[32,16,128]{2,1,0:T(8,128)S(1)} %collective-permute-done.8.refs_0_), channel_id=1, source_target_pairs={{0,1},{1,0},{2,3},{3,2},{4,5},{5,4},{6,7},{7,6},{8,9},{9,8},{10,11... | collective-permute-start | bytes 786440 | tf_op jit(solution)/shard_map/ppermute | solution.py:292
  75.7 6.0 %collective-permute-start.11 = (f32[16,16,128]{2,1,0:T(8,128)S(1)}, f32[16,16,128]{2,1,0:T(8,128)S(1)}, u32[]{:S(2)}, u32[]{:S(2)}) collective-permute-start(f32[16,16,128]{2,1,0:T(8,128)S(1)} %slice.15), channel_id=1, source_target_pairs={{0,2},{1,3},{2,4},{3,5},{4,6},{5,7},{6,0},{7,1},{8,10},{9,11},{10,... | collective-permute-start | bytes 393224 | tf_op jit(solution)/shard_map/ppermute | solution.py:295
  76.8 4.9 %collective-permute-start.10 = (f32[16,16,128]{2,1,0:T(8,128)S(1)}, f32[16,16,128]{2,1,0:T(8,128)S(1)}, u32[]{:S(2)}, u32[]{:S(2)}) collective-permute-start(f32[16,16,128]{2,1,0:T(8,128)S(1)} %slice.14), channel_id=1, source_target_pairs={{0,6},{1,7},{2,0},{3,1},{4,2},{5,3},{6,4},{7,5},{8,14},{9,15},{10,... | collective-permute-start | bytes 393224 | tf_op jit(solution)/shard_map/ppermute | solution.py:295
  81.7 3.0 %collective-permute-start.13 = (f32[16,16,128]{2,1,0:T(8,128)S(1)}, f32[16,16,128]{2,1,0:T(8,128)S(1)}, u32[]{:S(2)}, u32[]{:S(2)}) collective-permute-start(f32[16,16,128]{2,1,0:T(8,128)S(1)} %collective-permute-done.10.refs_0_), channel_id=1, source_target_pairs={{0,1},{1,0},{2,3},{3,2},{4,5},{5,4},{6,7},{7,6},{8,9},{9,8},{10,11... | collective-permute-start | bytes 393224 | tf_op jit(solution)/shard_map/ppermute | solution.py:292
  82.9 1.8 %collective-permute-start.14 = (f32[16,16,128]{2,1,0:T(8,128)S(1)}, f32[16,16,128]{2,1,0:T(8,128)S(1)}, u32[]{:S(2)}, u32[]{:S(2)}) collective-permute-start(f32[16,16,128]{2,1,0:T(8,128)S(1)} %collective-permute-done.11.refs_1_), channel_id=1, source_target_pairs={{0,1},{1,0},{2,3},{3,2},{4,5},{5,4},{6,7},{7,6},{8,9},{9,8},{10,11... | collective-permute-start | bytes 393224 | tf_op jit(solution)/shard_map/ppermute | solution.py:292

commit v4 on v3

--- a/solution.py
+++ b/solution.py
@@ -351,17 +351,12 @@
             name="forward_" + "_".join(str(step) for step in steps),
         )(tile_src, me, *tiles, left_h, left_l, right_kept, total)
 
-    above, below = shift(back, -1), shift(back, 1)
+    there = [shift(back, -step) for step in (1, 3, 2)]
     total = forward((0,), [back, exchange(back)], direct[0])
-    above, below, total = lax.optimization_barrier((above, below, total))
-    cut = count // 2
-    far = [shift(above[:cut], -1), shift(below[cut:], 1)]
-    above_other, below_other = exchange(above), exchange(below)
-    total = forward((1,), [above, above_other], total)
-    *far, total = lax.optimization_barrier((*far, total))
-    far = far + [exchange(part) for part in far]
-    total = forward((3,), [below, below_other], total)
-    return forward((2,), far, total, last=True)[None]
+    *there, total = lax.optimization_barrier((*there, total))
+    for step, mine in zip((1, 3, 2), there):
+        total = forward((step,), [mine, exchange(mine)], total, last=step == 2)
+    return total[None]
 
 
 def solution(mesh):

time: 87.6 us -> 89.3 us (1.019)
  waiting for transfers between devices: 12.8 us -> 15.8 us
  starting transfers between devices: 22.4 us -> 21.2 us
    ppermute x8 -> x7, waiting for transfers between devices: 12.3 us -> 14.6 us  [shift(): return lax.ppermute(x, 'panel', [(i, (i + 2 * by) % 8) for i in range(8)])]
    ppermute x8 -> x7, starting transfers between devices: 11.5 us -> 10.5 us  [exchange(): return lax.ppermute(x, 'panel', swap)]
    ppermute x8 -> x7, starting transfers between devices: 10.9 us -> 10.6 us  [shift(): return lax.ppermute(x, 'panel', [(i, (i + 2 * by) % 8) for i in range(8)])]
  transfers between devices with their start and end apart: 16 -> 14, of which waited for: 6 -> 7; matrix products, arithmetic and copies ran while one was open for 0% -> 0% of each run, Pallas kernels for 9% -> 9%
where the time goes in v4:
time: 89.3 us; the launch traced here: 89.2 us
  blocking collectives  33.7 us (38%)
  starting transfers between devices  21.2 us (24%)
  Pallas kernels  18.1 us (20%)
  waiting for transfers between devices  15.8 us (18%)
    all_to_all x1, blocking collectives, shards(): lax.all_to_all(moved, 'freq', split_axis=0, concat_axis=0, tiled=True)  19.7 us
    ppermute x7, waiting for transfers between devices, shift(): return lax.ppermute(x, 'panel', [(i, (i + 2 * by) % 8) for i in range(8)])  14.6 us
    all_to_all x1, blocking collectives, shards(): lax.all_to_all(gated.reshape(count, 4 * group, tile // 2), 'freq', split_...  14 us
    ppermute x7, starting transfers between devices, shift(): return lax.ppermute(x, 'panel', [(i, (i + 2 * by) % 8) for i in range(8)])  10.6 us
    ppermute x7, starting transfers between devices, exchange(): return lax.ppermute(x, 'panel', swap)  10.5 us
    pallas_call x4, Pallas kernels, forward(): pl.pallas_call(functools.partial(forward_kernel, steps, last, number // (...  7.85 us
    pallas_call x1, Pallas kernels, shards(): pl.pallas_call(adjoint_kernel, in_specs=[in_smem] + [in_hbm] * 4, out_spe...  5.5 us
    pallas_call x5, Pallas kernels, local(): pl.pallas_call(kernel, in_specs=[in_smem] * (2 * scalars) + [in_vmem] * (...  3.14 us
  transfers between devices with their start and end apart: 14, of which 7 were waited for; matrix products, arithmetic and copies ran while one was open for 0% of the time, Pallas kernels for 9%

profile of v4, /device:TPU:1, one launch (start us, length us, event | category | flops | bytes accessed | tf_op | source)
XLA Modules:
  0.0 89.2 jit_solution(9508069434270714549)
XLA Ops:
  0.0 5.5 %adjoint.1 = (bf16[25,256,128]{2,1,0:T(8,128)(2,1)S(1)}, bf16[25,256,128]{2,1,0:T(8,128)(2,1)S(1)}, bf16[25,256,256]{2,1,0:T(8,128)(2,1)S(1)}, f32[4,6,256,128]{3,2,1,0:T(8,128)S(1)}, f32[3,256,256]{2,1,0:T(8,128)S(1)}) custom-call(s32[1]{0:T(128)} %bitcast.me_ref, s32[4,6]{1,0:T(4,128)} %src_ref.11, f32[2,128,1024]{2,1,0:T(8,128)} %bitcast.19, ...), custom_call_target="tpu_custom_call" | custom-call | tf_op jit(solution)/shard_map/adjoint/pallas_call | solution.py:258
  5.5 3.3 %collective-permute-start = (f32[3,256,256]{2,1,0:T(8,128)S(1)}, f32[3,256,256]{2,1,0:T(8,128)S(1)}, u32[]{:S(2)}, u32[]{:S(2)}) collective-permute-start(f32[3,256,256]{2,1,0:T(8,128)S(1)} %get-tuple-element.30), channel_id=1, source_target_pairs={{0,1},{1,0},{2,3},{3,2},{4,5},{5,4},{6,7},{7,6},{8,9},{9,8},{10,11... | collective-permute-start | bytes 2359304 | tf_op jit(solution)/shard_map/ppermute | solution.py:292
  8.8 1.4 %own_kernel.1.own_ref = f32[3,256,256]{2,1,0:T(8,128)S(1)} custom-call(s32[4,6]{1,0:T(4,128)S(1)} %copy-done.3, s32[1]{0:T(128)} %bitcast.me_ref, bf16[25,256,128]{2,1,0:T(8,128)(2,1)S(1)} %get-tuple-element.26.coef_h, bf16[25,256,128]{2,1,0:T(8,128)(2,1)S(1)} %get-tuple-element.27.coef_l, bf16[25,256,256]{2,1,0:T(8,128)(2,1)S(1)} %get-tuple-element.28.right_ref.refs_4_), custom_call_target="tpu_custom_call" | custom-call | flops 3000000000 | bytes 8000000 | tf_op jit(solution)/shard_map/own_kernel/pallas_call | solution.py:279
  11.3 2.7 %collective-permute-start.3 = (f32[2,128,256]{2,1,0:T(8,128)S(1)}, f32[2,128,256]{2,1,0:T(8,128)S(1)}, u32[]{:S(2)}, u32[]{:S(2)}) collective-permute-start(f32[2,128,256]{2,1,0:T(8,128)S(1)} %get-tuple-element.33), channel_id=1, source_target_pairs={{0,6},{1,7},{2,0},{3,1},{4,2},{5,3},{6,4},{7,5},{8,14},{9,15},{10,... | collective-permute-start | bytes 786440 | tf_op jit(solution)/shard_map/ppermute | solution.py:295
  14.0 1.6 %here_kernel.1 = (f32[2,256,256]{2,1,0:T(8,128)S(1)}, bf16[4,6,256,128]{3,2,1,0:T(8,128)(2,1)S(1)}, bf16[4,6,256,128]{3,2,1,0:T(8,128)(2,1)S(1)}) custom-call(s32[4,6]{1,0:T(4,128)S(1)} %copy-done.3, s32[1]{0:T(128)} %bitcast.me_ref, bf16[25,256,128]{2,1,0:T(8,128)(2,1)S(1)} %get-tuple-element.26.coef_h, bf16[25,256,128]{2,1,0:T(8,128)(2,1)S(1)} %get-tuple-element.27.coef_l, ...), custom_call_target="tpu_custom_call" | custom-call | flops 3000000000 | bytes 8000000 | tf_op jit(solution)/shard_map/here_kernel/pallas_call | solution.py:279
  15.6 0.8 collective-permute-start.4
  16.4 2.8 %collective-permute-done.3.from_above.above = f32[2,128,256]{2,1,0:T(8,128)S(1)} collective-permute-done((f32[2,128,256]{2,1,0:T(8,128)S(1)}, f32[2,128,256]{2,1,0:T(8,128)S(1)}, u32[]{:S(2)}, u32[]{:S(2)}) %collective-permute-start.3) | collective-permute-done | bytes 262176 | tf_op jit(solution)/shard_map/ppermute | solution.py:295
  19.2 1.1 %collective-permute-done.2.from_below.below = f32[2,128,256]{2,1,0:T(8,128)S(1)} collective-permute-done((f32[2,128,256]{2,1,0:T(8,128)S(1)}, f32[2,128,256]{2,1,0:T(8,128)S(1)}, u32[]{:S(2)}, u32[]{:S(2)}) %collective-permute-start.2) | collective-permute-done | bytes 262176 | tf_op jit(solution)/shard_map/ppermute | solution.py:295
  20.4 2.7 %collective-permute-start.6 = (f32[128,256]{1,0:T(8,128)S(1)}, f32[128,256]{1,0:T(8,128)S(1)}, u32[]{:S(2)}, u32[]{:S(2)}) collective-permute-start(f32[128,256]{1,0:T(8,128)S(1)} %get-tuple-element.40), channel_id=1, source_target_pairs={{0,6},{1,7},{2,0},{3,1},{4,2},{5,3},{6,4},{7,5},{8,14},{9,15},{10,... | collective-permute-start | bytes 393224 | tf_op jit(solution)/shard_map/ppermute | solution.py:295
  23.1 2.4 %collective-permute-done.5.relayed_below = f32[128,256]{1,0:T(8,128)S(1)} collective-permute-done((f32[128,256]{1,0:T(8,128)S(1)}, f32[128,256]{1,0:T(8,128)S(1)}, u32[]{:S(2)}, u32[]{:S(2)}) %collective-permute-start.5) | collective-permute-done | bytes 131104 | tf_op jit(solution)/shard_map/ppermute | solution.py:295
  25.5 19.7 %all_to_all.10 = f32[32,16,128]{2,1,0:T(8,128)S(1)} all-to-all(f32[32,16,128]{2,1,0:T(8,128)S(1)} %sum_kernel.1), channel_id=1, replica_groups=mesh['freq'=32,'panel'=8] {'freq'}, dimensions={0} | all-to-all | bytes 524288 | tf_op jit(solution)/shard_map/all_to_all | solution.py:318
  45.2 1.6 %gate.1 = f32[512,128]{1,0:T(8,128)S(1)} custom-call(s32[1]{0:T(128)} %bitcast.me_ref, f32[512,128]{1,0:T(8,128)S(1)} %bitcast.14, s32[4,2048]{1,0:T(4,128)S(1)} %copy-done.2, bf16[896,192]{1,0:T(8,128)(2,1)S(1)} %copy-done, bf16[128,896]{1,0:T(8,128)(2,1)S(1)} %copy-done.1), custom_call_target="tpu_custom_call" | custom-call | tf_op jit(solution)/shard_map/gate/pallas_call | solution.py:322
  46.9 14.0 %all_to_all.11.refs_0_ = f32[32,16,128]{2,1,0:T(8,128)S(1)} all-to-all(f32[32,16,128]{2,1,0:T(8,128)S(1)} %bitcast.15), channel_id=1, replica_groups=mesh['freq'=32,'panel'=8] {'freq'}, dimensions={0} | all-to-all | bytes 524288 | tf_op jit(solution)/shard_map/all_to_all | solution.py:339
  60.9 4.7 %collective-permute-start.10 = (f32[32,16,128]{2,1,0:T(8,128)S(1)}, f32[32,16,128]{2,1,0:T(8,128)S(1)}, u32[]{:S(2)}, u32[]{:S(2)}) collective-permute-start(f32[32,16,128]{2,1,0:T(8,128)S(1)} %all_to_all.11.refs_0_), channel_id=1, source_target_pairs={{0,1},{1,0},{2,3},{3,2},{4,5},{5,4},{6,7},{7,6},{8,9},{9,8},{10,11... | collective-permute-start | bytes 786440 | tf_op jit(solution)/shard_map/ppermute | solution.py:292
  65.6 2.5 %collective-permute-start.9 = (f32[32,16,128]{2,1,0:T(8,128)S(1)}, f32[32,16,128]{2,1,0:T(8,128)S(1)}, u32[]{:S(2)}, u32[]{:S(2)}) collective-permute-start(f32[32,16,128]{2,1,0:T(8,128)S(1)} %all_to_all.11.refs_0_), channel_id=1, source_target_pairs={{0,4},{1,5},{2,6},{3,7},{4,0},{5,1},{6,2},{7,3},{8,12},{9,13},{10,... | collective-permute-start | bytes 786440 | tf_op jit(solution)/shard_map/ppermute | solution.py:295
  68.8 2.0 %collective-permute-start.7 = (f32[32,16,128]{2,1,0:T(8,128)S(1)}, f32[32,16,128]{2,1,0:T(8,128)S(1)}, u32[]{:S(2)}, u32[]{:S(2)}) collective-permute-start(f32[32,16,128]{2,1,0:T(8,128)S(1)} %all_to_all.11.refs_0_), channel_id=1, source_target_pairs={{0,6},{1,7},{2,0},{3,1},{4,2},{5,3},{6,4},{7,5},{8,14},{9,15},{10,... | collective-permute-start | bytes 786440 | tf_op jit(solution)/shard_map/ppermute | solution.py:295
  70.9 1.8 %forward_0.1.refs_5_ = f32[2,128,1024]{2,1,0:T(8,128)S(1)} custom-call(s32[4,6]{1,0:T(4,128)S(1)} %copy-done.3, s32[1]{0:T(128)} %bitcast.me_ref, f32[32,16,128]{2,1,0:T(8,128)S(1)} %all_to_all.11.refs_0_, f32[32,16,128]{2,1,0:T(8,128)S(1)} %collective-permute-done.10.refs_1_, bf16[4,6,256,128]{3,2,1,0:T(8,128)(2,1)S(1)} %get-tuple-element.41.refs_2_, ...), custom_call_target="tpu_custom_call" | custom-call | flops 3000000000 | bytes 8000000 | tf_op jit(solution)/shard_map/forward_0/pallas_call | solution.py:343
  72.6 2.5 %collective-permute-done.9.refs_0_ = f32[32,16,128]{2,1,0:T(8,128)S(1)} collective-permute-done((f32[32,16,128]{2,1,0:T(8,128)S(1)}, f32[32,16,128]{2,1,0:T(8,128)S(1)}, u32[]{:S(2)}, u32[]{:S(2)}) %collective-permute-start.9) | collective-permute-done | bytes 262176 | tf_op jit(solution)/shard_map/ppermute | solution.py:295
  75.1 5.9 %collective-permute-done.8.refs_0_ = f32[32,16,128]{2,1,0:T(8,128)S(1)} collective-permute-done((f32[32,16,128]{2,1,0:T(8,128)S(1)}, f32[32,16,128]{2,1,0:T(8,128)S(1)}, u32[]{:S(2)}, u32[]{:S(2)}) %collective-permute-start.8) | collective-permute-done | bytes 262176 | tf_op jit(solution)/shard_map/ppermute | solution.py:295
  81.0 0.7 collective-permute-start.13
  82.2 0.7 collective-permute-done.13.refs_1_
  82.9 1.7 %forward_1.1.refs_5_ = f32[2,128,1024]{2,1,0:T(8,128)S(1)} custom-call(s32[4,6]{1,0:T(4,128)S(1)} %copy-done.3, s32[1]{0:T(128)} %bitcast.me_ref, f32[32,16,128]{2,1,0:T(8,128)S(1)} %collective-permute-done.7.refs_0_, f32[32,16,128]{2,1,0:T(8,128)S(1)} %collective-permute-done.13.refs_1_, bf16[4,6,256,128]{3,2,1,0:T(8,128)(2,1)S(1)} %get-tuple-element.41.refs_2_, ...), custom_call_target="tpu_custom_call" | custom-call | flops 3000000000 | bytes 8000000 | tf_op jit(solution)/shard_map/forward_1/pallas_call | solution.py:343
  84.7 1.7 %forward_3.1.refs_5_ = f32[2,128,1024]{2,1,0:T(8,128)S(1)} custom-call(s32[4,6]{1,0:T(4,128)S(1)} %copy-done.3, s32[1]{0:T(128)} %bitcast.me_ref, f32[32,16,128]{2,1,0:T(8,128)S(1)} %collective-permute-done.8.refs_0_, f32[32,16,128]{2,1,0:T(8,128)S(1)} %collective-permute-done.12.refs_1_, bf16[4,6,256,128]{3,2,1,0:T(8,128)(2,1)S(1)} %get-tuple-element.41.refs_2_, ...), custom_call_target="tpu_custom_call" | custom-call | flops 3000000000 | bytes 8000000 | tf_op jit(solution)/shard_map/forward_3/pallas_call | solution.py:343
  86.4 2.6 %forward_2.1 = f32[2,128,1024]{2,1,0:T(8,128)} custom-call(s32[4,6]{1,0:T(4,128)S(1)} %copy-done.3, s32[1]{0:T(128)} %bitcast.me_ref, f32[32,16,128]{2,1,0:T(8,128)S(1)} %collective-permute-done.9.refs_0_, f32[32,16,128]{2,1,0:T(8,128)S(1)} %collective-permute-done.11.refs_1_, bf16[4,6,256,128]{3,2,1,0:T(8,128)(2,1)S(1)} %get-tuple-element.41.refs_2_, ...), custom_call_target="tpu_custom_call" | custom-call | flops 3000000000 | bytes 8000000 | tf_op jit(solution)/shard_map/forward_2/pallas_call | solution.py:343
  (29 shorter events, 2.4 us)
Async XLA Ops:
  0.0 8.8 %copy-start.3 = (s32[4,6]{1,0:T(4,128)S(1)}, s32[4,6]{1,0:T(4,128)}, u32[]{:S(2)}) copy-start(s32[4,6]{1,0:T(4,128)} %src_ref.11) | copy-start | bytes 292
  5.5 5.2 %collective-permute-start = (f32[3,256,256]{2,1,0:T(8,128)S(1)}, f32[3,256,256]{2,1,0:T(8,128)S(1)}, u32[]{:S(2)}, u32[]{:S(2)}) collective-permute-start(f32[3,256,256]{2,1,0:T(8,128)S(1)} %get-tuple-element.30), channel_id=1, source_target_pairs={{0,1},{1,0},{2,3},{3,2},{4,5},{5,4},{6,7},{7,6},{8,9},{9,8},{10,11... | collective-permute-start | bytes 2359304 | tf_op jit(solution)/shard_map/ppermute | solution.py:292
  10.8 3.1 %collective-permute-start.1 = (f32[8,128]{1,0:T(8,128)S(1)}, f32[8,128]{1,0:T(8,128)S(1)}, u32[]{:S(2)}, u32[]{:S(2)}) collective-permute-start(f32[8,128]{1,0:T(8,128)S(1)} %slice_bitcast_fusion.1), channel_id=1, source_target_pairs={{0,1},{1,0},{2,3},{3,2},{4,5},{5,4},{6,7},{7,6},{8,9},{9,8},{10,11... | collective-permute-start | bytes 12296 | tf_op jit(solution)/shard_map/ppermute | solution.py:292
  11.3 9.0 %collective-permute-start.2 = (f32[2,128,256]{2,1,0:T(8,128)S(1)}, f32[2,128,256]{2,1,0:T(8,128)S(1)}, u32[]{:S(2)}, u32[]{:S(2)}) collective-permute-start(f32[2,128,256]{2,1,0:T(8,128)S(1)} %get-tuple-element.31), channel_id=1, source_target_pairs={{0,2},{1,3},{2,4},{3,5},{4,6},{5,7},{6,0},{7,1},{8,10},{9,11},{10,... | collective-permute-start | bytes 786440 | tf_op jit(solution)/shard_map/ppermute | solution.py:295
  11.3 7.9 %collective-permute-start.3 = (f32[2,128,256]{2,1,0:T(8,128)S(1)}, f32[2,128,256]{2,1,0:T(8,128)S(1)}, u32[]{:S(2)}, u32[]{:S(2)}) collective-permute-start(f32[2,128,256]{2,1,0:T(8,128)S(1)} %get-tuple-element.33), channel_id=1, source_target_pairs={{0,6},{1,7},{2,0},{3,1},{4,2},{5,3},{6,4},{7,5},{8,14},{9,15},{10,... | collective-permute-start | bytes 786440 | tf_op jit(solution)/shard_map/ppermute | solution.py:295
  15.5 29.7 %copy-start = (bf16[896,192]{1,0:T(8,128)(2,1)S(1)}, bf16[896,192]{1,0:T(8,128)(2,1)}, u32[]{:S(2)}) copy-start(bf16[896,192]{1,0:T(8,128)(2,1)} %constant.8.clone.into_ref) | copy-start | bytes 1032196
  15.6 29.7 %copy-start.1 = (bf16[128,896]{1,0:T(8,128)(2,1)S(1)}, bf16[128,896]{1,0:T(8,128)(2,1)}, u32[]{:S(2)}) copy-start(bf16[128,896]{1,0:T(8,128)(2,1)} %constant.9.clone.outof_ref) | copy-start | bytes 688132
  15.6 29.7 %copy-start.2 = (s32[4,2048]{1,0:T(4,128)S(1)}, s32[4,2048]{1,0:T(4,128)}, u32[]{:S(2)}) copy-start(s32[4,2048]{1,0:T(4,128)} %onset_ref.1) | copy-start | bytes 98308
  15.6 55.3 %copy-start.4 = (f32[1,2,128,1024]{3,2,1,0:T(8,128)S(1)}, f32[1,2,128,1024]{3,2,1,0:T(8,128)}, u32[]{:S(2)}) copy-start(f32[1,2,128,1024]{3,2,1,0:T(8,128)} %param.9) | copy-start | bytes 3145732
  15.6 4.7 %collective-permute-start.4 = (f32[256,256]{1,0:T(8,128)S(1)}, f32[256,256]{1,0:T(8,128)S(1)}, u32[]{:S(2)}, u32[]{:S(2)}) collective-permute-start(f32[256,256]{1,0:T(8,128)S(1)} %slice_bitcast_fusion), channel_id=1, source_target_pairs={{0,1},{1,0},{2,3},{3,2},{4,5},{5,4},{6,7},{7,6},{8,9},{9,8},{10,11... | collective-permute-start | bytes 786440 | tf_op jit(solution)/shard_map/ppermute | solution.py:292
  20.3 5.1 %collective-permute-start.5 = (f32[128,256]{1,0:T(8,128)S(1)}, f32[128,256]{1,0:T(8,128)S(1)}, u32[]{:S(2)}, u32[]{:S(2)}) collective-permute-start(f32[128,256]{1,0:T(8,128)S(1)} %get-tuple-element.39), channel_id=1, source_target_pairs={{0,2},{1,3},{2,4},{3,5},{4,6},{5,7},{6,0},{7,1},{8,10},{9,11},{10,... | collective-permute-start | bytes 393224 | tf_op jit(solution)/shard_map/ppermute | solution.py:295
  20.4 5.0 %collective-permute-start.6 = (f32[128,256]{1,0:T(8,128)S(1)}, f32[128,256]{1,0:T(8,128)S(1)}, u32[]{:S(2)}, u32[]{:S(2)}) collective-permute-start(f32[128,256]{1,0:T(8,128)S(1)} %get-tuple-element.40), channel_id=1, source_target_pairs={{0,6},{1,7},{2,0},{3,1},{4,2},{5,3},{6,4},{7,5},{8,14},{9,15},{10,... | collective-permute-start | bytes 393224 | tf_op jit(solution)/shard_map/ppermute | solution.py:295
  60.9 10.0 %collective-permute-start.10 = (f32[32,16,128]{2,1,0:T(8,128)S(1)}, f32[32,16,128]{2,1,0:T(8,128)S(1)}, u32[]{:S(2)}, u32[]{:S(2)}) collective-permute-start(f32[32,16,128]{2,1,0:T(8,128)S(1)} %all_to_all.11.refs_0_), channel_id=1, source_target_pairs={{0,1},{1,0},{2,3},{3,2},{4,5},{5,4},{6,7},{7,6},{8,9},{9,8},{10,11... | collective-permute-start | bytes 786440 | tf_op jit(solution)/shard_map/ppermute | solution.py:292
  65.6 9.5 %collective-permute-start.9 = (f32[32,16,128]{2,1,0:T(8,128)S(1)}, f32[32,16,128]{2,1,0:T(8,128)S(1)}, u32[]{:S(2)}, u32[]{:S(2)}) collective-permute-start(f32[32,16,128]{2,1,0:T(8,128)S(1)} %all_to_all.11.refs_0_), channel_id=1, source_target_pairs={{0,4},{1,5},{2,6},{3,7},{4,0},{5,1},{6,2},{7,3},{8,12},{9,13},{10,... | collective-permute-start | bytes 786440 | tf_op jit(solution)/shard_map/ppermute | solution.py:295
  68.2 12.8 %collective-permute-start.8 = (f32[32,16,128]{2,1,0:T(8,128)S(1)}, f32[32,16,128]{2,1,0:T(8,128)S(1)}, u32[]{:S(2)}, u32[]{:S(2)}) collective-permute-start(f32[32,16,128]{2,1,0:T(8,128)S(1)} %all_to_all.11.refs_0_), channel_id=1, source_target_pairs={{0,2},{1,3},{2,4},{3,5},{4,6},{5,7},{6,0},{7,1},{8,10},{9,11},{10,... | collective-permute-start | bytes 786440 | tf_op jit(solution)/shard_map/ppermute | solution.py:295
  68.8 12.2 %collective-permute-start.7 = (f32[32,16,128]{2,1,0:T(8,128)S(1)}, f32[32,16,128]{2,1,0:T(8,128)S(1)}, u32[]{:S(2)}, u32[]{:S(2)}) collective-permute-start(f32[32,16,128]{2,1,0:T(8,128)S(1)} %all_to_all.11.refs_0_), channel_id=1, source_target_pairs={{0,6},{1,7},{2,0},{3,1},{4,2},{5,3},{6,4},{7,5},{8,14},{9,15},{10,... | collective-permute-start | bytes 786440 | tf_op jit(solution)/shard_map/ppermute | solution.py:295
  81.0 1.9 %collective-permute-start.13 = (f32[32,16,128]{2,1,0:T(8,128)S(1)}, f32[32,16,128]{2,1,0:T(8,128)S(1)}, u32[]{:S(2)}, u32[]{:S(2)}) collective-permute-start(f32[32,16,128]{2,1,0:T(8,128)S(1)} %collective-permute-done.7.refs_0_), channel_id=1, source_target_pairs={{0,1},{1,0},{2,3},{3,2},{4,5},{5,4},{6,7},{7,6},{8,9},{9,8},{10,11... | collective-permute-start | bytes 786440 | tf_op jit(solution)/shard_map/ppermute | solution.py:292
  81.7 4.7 %collective-permute-start.11 = (f32[32,16,128]{2,1,0:T(8,128)S(1)}, f32[32,16,128]{2,1,0:T(8,128)S(1)}, u32[]{:S(2)}, u32[]{:S(2)}) collective-permute-start(f32[32,16,128]{2,1,0:T(8,128)S(1)} %collective-permute-done.9.refs_0_), channel_id=1, source_target_pairs={{0,1},{1,0},{2,3},{3,2},{4,5},{5,4},{6,7},{7,6},{8,9},{9,8},{10,11... | collective-permute-start | bytes 786440 | tf_op jit(solution)/shard_map/ppermute | solution.py:292
  81.7 2.9 %collective-permute-start.12 = (f32[32,16,128]{2,1,0:T(8,128)S(1)}, f32[32,16,128]{2,1,0:T(8,128)S(1)}, u32[]{:S(2)}, u32[]{:S(2)}) collective-permute-start(f32[32,16,128]{2,1,0:T(8,128)S(1)} %collective-permute-done.8.refs_0_), channel_id=1, source_target_pairs={{0,1},{1,0},{2,3},{3,2},{4,5},{5,4},{6,7},{7,6},{8,9},{9,8},{10,11... | collective-permute-start | bytes 786440 | tf_op jit(solution)/shard_map/ppermute | solution.py:292

commit v5 on v3

--- a/solution.py
+++ b/solution.py
@@ -18,7 +18,7 @@
 BF16 = jnp.bfloat16
 NN = (((1,), (0,)), ((), ()))
 NT_DIMS = (((1,), (1,)), ((), ()))
-AWAY = (2, 1, 3)
+FAR, NEAR = (2,), (1, 3)
 
 
 def split(x):
@@ -68,7 +68,7 @@
 
 def adjoint_kernel(
     me_ref, src_hbm, field_hbm, left_hbm, right_hbm,
-    coef_h, coef_l, right_ref, left_ref, out_ref,
+    coef_h, coef_l, right_ref, left_ref, far_ref, near_ref,
     src_ref, field_ref, raw_ref, sems,
 ):
     panels, slots, tile, width = left_ref.shape
@@ -109,11 +109,16 @@
         for s in range(slots):
             right_ref[p * slots + s] = jnp.concatenate(split(raw_ref[p, s]), axis=1)
     names.wait()
-    spread(src_ref, me_ref[0], [(step, 1) for step in AWAY], coef_h, coef_l, right_ref, out_ref)
-
-
-def own_kernel(src_ref, me_ref, coef_h, coef_l, right_ref, out_ref):
-    spread(src_ref, me_ref[0], [(step, 0) for step in AWAY], coef_h, coef_l, right_ref, out_ref)
+    spread(src_ref, me_ref[0], [(step, 1) for step in FAR], coef_h, coef_l, right_ref, far_ref)
+    spread(src_ref, me_ref[0], [(step, 1) for step in NEAR], coef_h, coef_l, right_ref, near_ref)
+
+
+def far_kernel(src_ref, me_ref, coef_h, coef_l, right_ref, out_ref):
+    spread(src_ref, me_ref[0], [(step, 0) for step in FAR], coef_h, coef_l, right_ref, out_ref)
+
+
+def near_kernel(src_ref, me_ref, coef_h, coef_l, right_ref, _, out_ref):
+    spread(src_ref, me_ref[0], [(step, 0) for step in NEAR], coef_h, coef_l, right_ref, out_ref)
 
 
 def here_kernel(src_ref, me_ref, coef_h, coef_l, right_ref, left_ref, _, out_ref, left_h, left_l):
@@ -123,28 +128,24 @@
             left_h[p, s], left_l[p, s] = split(left_ref[p, s])
 
 
-def chip_sum_kernel(own_ref, swapped_ref, up_ref, down_ref, up_half, down_half):
-    half = up_half.shape[0]
-    up_ref[0] = own_ref[0, :half] + swapped_ref[0, :half]
-    down_ref[0] = own_ref[0, half:] + swapped_ref[0, half:]
-    up_half[...] = own_ref[1, :half] + swapped_ref[1, :half]
-    up_ref[1] = own_ref[1, half:] + swapped_ref[1, half:]
-    down_ref[1] = own_ref[2, :half] + swapped_ref[2, :half]
-    down_half[...] = own_ref[2, half:] + swapped_ref[2, half:]
-
-
-def relay_kernel(up_half, from_below, down_half, from_above, up_ref, down_ref):
-    up_ref[...] = up_half[...] + from_below[0]
-    down_ref[...] = down_half[...] + from_above[0]
-
-
-def sum_kernel(here_ref, swapped_ref, below, above, relayed_below, relayed_above, out_ref):
-    totals = (
-        (here_ref[1, : relayed_below.shape[0]] + swapped_ref[: relayed_below.shape[0]])
-        + (relayed_below[...] + above[1]),
-        (here_ref[1, relayed_below.shape[0] :] + swapped_ref[relayed_below.shape[0] :])
-        + (relayed_above[...] + below[1]),
-    )
+def far_sum_kernel(own_ref, swapped_ref, up_ref, down_ref):
+    half = up_ref.shape[0]
+    up_ref[...] = own_ref[0, :half] + swapped_ref[0, :half]
+    down_ref[...] = own_ref[0, half:] + swapped_ref[0, half:]
+
+
+def near_sum_kernel(own_ref, swapped_ref, from_below, from_above, up_ref, down_ref):
+    half = from_below.shape[0]
+    up_ref[:half] = (own_ref[0, :half] + swapped_ref[0, :half]) + from_below[...]
+    up_ref[half:] = own_ref[0, half:] + swapped_ref[0, half:]
+    down_ref[:half] = own_ref[1, :half] + swapped_ref[1, :half]
+    down_ref[half:] = (own_ref[1, half:] + swapped_ref[1, half:]) + from_above[...]
+
+
+def sum_kernel(here_ref, swapped_ref, below, above, out_ref):
+    all_parts = (here_ref[1] + swapped_ref[...]) + (below[...] + above[...])
+    half = all_parts.shape[0] // 2
+    totals = (all_parts[:half], all_parts[half:])
     for c, total in enumerate(totals):
         rows, cols = total.shape
         lanes = cols // 2
@@ -250,21 +251,21 @@
     in_smem = pl.BlockSpec(memory_space=pltpu.SMEM)
     in_hbm = pl.BlockSpec(memory_space=pltpu.HBM)
     hbm = lambda x: pltpu.with_memory_space_constraint(x, pltpu.HBM)
-    sums_type = jax.ShapeDtypeStruct((3, rows, tile), F32)
     places = panels * slots + 1
     cost = pl.CostEstimate(flops=3_000_000_000, bytes_accessed=8_000_000, transcendentals=0)
     coef_type = jax.ShapeDtypeStruct((places, rows, width), BF16)
     left_shape = (panels, slots, tile, width)
-    coef_h, coef_l, right_kept, left_kept, other = pl.pallas_call(
+    coef_h, coef_l, right_kept, left_kept, far, near = pl.pallas_call(
         adjoint_kernel,
         in_specs=[in_smem] + [in_hbm] * 4,
-        out_specs=[in_vmem] * 5,
+        out_specs=[in_vmem] * 6,
         out_shape=[
             coef_type,
             coef_type,
             jax.ShapeDtypeStruct((places, tile, 2 * width), BF16),
             jax.ShapeDtypeStruct(left_shape, F32),
-            sums_type,
+            jax.ShapeDtypeStruct((len(FAR), rows, tile), F32),
+            jax.ShapeDtypeStruct((len(NEAR), rows, tile), F32),
         ],
         scratch_shapes=[
             pltpu.SMEM(tile_src.shape, jnp.int32),
@@ -275,14 +276,14 @@
         compiler_params=pltpu.CompilerParams(vmem_limit_bytes=28 * mib),
         name="adjoint",
     )(me, hbm(tile_src), hbm(wavefield[0]), hbm(left), hbm(right))
-    def local(kernel, outs, *args, scalars=True, limit=4):
+    def local(kernel, outs, *args, scalars=True, limit=4, cost=None):
         return pl.pallas_call(
             kernel,
             in_specs=[in_smem] * (2 * scalars) + [in_vmem] * (len(args) - 2 * scalars),
             out_specs=[in_vmem] * len(outs),
             out_shape=[jax.ShapeDtypeStruct(shape, dtype) for shape, dtype in outs],
             compiler_params=pltpu.CompilerParams(vmem_limit_bytes=limit * mib),
-            cost_estimate=cost if scalars else None,
+            cost_estimate=cost,
             name=kernel.__name__,
         )(*args)
 
@@ -295,25 +296,22 @@
         return lax.ppermute(x, "panel", [(i, (i + 2 * by) % 8) for i in range(8)])
 
     half = rows // 2
-    swapped = exchange(other)
-    (own,) = local(own_kernel, [((3, rows, tile), F32)], tile_src, me, coef_h, coef_l, right_kept, limit=16)
-    up, down, up_half, down_half = local(
-        chip_sum_kernel, [((2, half, tile), F32)] * 2 + [((half, tile), F32)] * 2, own, swapped, scalars=False
+    factors = (tile_src, me, coef_h, coef_l, right_kept)
+    one, two = [((1, rows, tile), F32)], [((2, rows, tile), F32)]
+    swapped_far, swapped = exchange(far), exchange(near)
+    (far,) = local(far_kernel, one, *factors, limit=16, cost=cost)
+    up, down = local(far_sum_kernel, [((half, tile), F32)] * 2, far, swapped_far, scalars=False)
+    below, above = shift(up, 1), shift(down, -1)
+    after = exchange(up[:8, :width])
+    (near,) = local(near_kernel, two, *factors, after, limit=16, cost=cost)
+    up, down = local(near_sum_kernel, [((rows, tile), F32)] * 2, near, swapped, below, above, scalars=False)
+    below, above = shift(up, 1), shift(down, -1)
+    after = exchange(up[:8, :width])
+    here, left_h, left_l = local(
+        here_kernel, two + [(left_shape, BF16), (left_shape, BF16)], *factors, left_kept, after, limit=20, cost=cost
     )
-    below, above = shift(up, 1), shift(down, -1)
-    after = exchange(up[0, :8, :width])
-    here, left_h, left_l = local(
-        here_kernel,
-        [((2, rows, tile), F32), (left_shape, BF16), (left_shape, BF16)],
-        tile_src, me, coef_h, coef_l, right_kept, left_kept, after, limit=20,
-    )
-    swapped = exchange(here[0])
-    below, above, swapped = lax.optimization_barrier((below, above, swapped))
-    up, down = local(relay_kernel, [((half, tile), F32)] * 2, up_half, below, down_half, above, scalars=False)
     (moved,) = local(
-        sum_kernel,
-        [((count, 4 * group, tile // 2), F32)],
-        here, swapped, below, above, shift(up, 1), shift(down, -1), scalars=False,
+        sum_kernel, [((count, 4 * group, tile // 2), F32)], here, exchange(here[0]), below, above, scalars=False
     )
     moved = lax.all_to_all(moved, "freq", split_axis=0, concat_axis=0, tiled=True)
 

time: 87.6 us -> 89.6 us (1.023)
  blocking collectives: 33.7 us -> 35.2 us
    all_to_all x1, blocking collectives: 14 us -> 15.4 us  [shards(): lax.all_to_all(gated.reshape(count, 4 * group, tile // 2), 'freq', split_...]
    pallas_call x5 -> x6, Pallas kernels: 3.14 us -> 3.93 us  [local(): pl.pallas_call(kernel, in_specs=[in_smem] * (2 * scalars) + [in_vmem] * (...]
    ppermute x8 -> x10, starting transfers between devices: 11.5 us -> 11.5 us  [exchange(): return lax.ppermute(x, 'panel', swap)]
  transfers between devices with their start and end apart: 16 -> 18, of which waited for: 6 -> 6; matrix products, arithmetic and copies ran while one was open for 0% -> 0% of each run, Pallas kernels for 9% -> 10%
where the time goes in v5:
time: 89.6 us; the launch traced here: 89.4 us
  blocking collectives  35.2 us (39%)
  starting transfers between devices  22.4 us (25%)
  Pallas kernels  18.9 us (21%)
  waiting for transfers between devices  12.4 us (14%)
    all_to_all x1, blocking collectives, shards(): lax.all_to_all(moved, 'freq', split_axis=0, concat_axis=0, tiled=True)  19.9 us
    all_to_all x1, blocking collectives, shards(): lax.all_to_all(gated.reshape(count, 4 * group, tile // 2), 'freq', split_...  15.4 us
    ppermute x8, waiting for transfers between devices, shift(): return lax.ppermute(x, 'panel', [(i, (i + 2 * by) % 8) for i in range(8)])  12.4 us
    ppermute x10, starting transfers between devices, exchange(): return lax.ppermute(x, 'panel', swap)  11.5 us
    ppermute x8, starting transfers between devices, shift(): return lax.ppermute(x, 'panel', [(i, (i + 2 * by) % 8) for i in range(8)])  10.9 us
    pallas_call x4, Pallas kernels, forward(): pl.pallas_call(functools.partial(forward_kernel, steps, last, number // (...  7.85 us
    pallas_call x1, Pallas kernels, shards(): pl.pallas_call(adjoint_kernel, in_specs=[in_smem] + [in_hbm] * 4, out_spe...  5.5 us
    pallas_call x6, Pallas kernels, local(): pl.pallas_call(kernel, in_specs=[in_smem] * (2 * scalars) + [in_vmem] * (...  3.93 us
  transfers between devices with their start and end apart: 18, of which 6 were waited for; matrix products, arithmetic and copies ran while one was open for 0% of the time, Pallas kernels for 10%

profile of v5, /device:TPU:1, one launch (start us, length us, event | category | flops | bytes accessed | tf_op | source)
XLA Modules:
  0.0 89.4 jit_solution(4767451669378866151)
XLA Ops:
  0.0 5.5 %adjoint.1 = (bf16[25,256,128]{2,1,0:T(8,128)(2,1)S(1)}, bf16[25,256,128]{2,1,0:T(8,128)(2,1)S(1)}, bf16[25,256,256]{2,1,0:T(8,128)(2,1)S(1)}, f32[4,6,256,128]{...) custom-call(s32[1]{0:T(128)} %bitcast.me_ref, s32[4,6]{1,0:T(4,128)} %src_ref.13, ...), custom_call_target="tpu_custom_call" | custom-call | tf_op jit(solution)/shard_map/adjoint/pallas_call | solution.py:258
  5.5 3.3 %collective-permute-start = (f32[1,256,256]{2,1,0:T(8,128)S(1)}, f32[1,256,256]{2,1,0:T(8,128)S(1)}, u32[]{:S(2)}, u32[]{:S(2)}) collective-permute-start(f32[1,256,256]{2,1,0:T(8,128)S(1)} %get-tuple-element.28), channel_id=1, source_target_pairs={{0,1},{1,0},{2,3},{3,2},{4,5},{5,4},{6,7},{7,6},{8,9},{9,8},{10,11... | collective-permute-start | bytes 786440 | tf_op jit(solution)/shard_map/ppermute | solution.py:293
  10.5 2.7 %collective-permute-start.4 = (f32[128,256]{1,0:T(8,128)S(1)}, f32[128,256]{1,0:T(8,128)S(1)}, u32[]{:S(2)}, u32[]{:S(2)}) collective-permute-start(f32[128,256]{1,0:T(8,128)S(1)} %get-tuple-element.31), channel_id=1, source_target_pairs={{0,6},{1,7},{2,0},{3,1},{4,2},{5,3},{6,4},{7,5},{8,14},{9,15},{10,... | collective-permute-start | bytes 393224 | tf_op jit(solution)/shard_map/ppermute | solution.py:296
  13.2 1.2 %near_kernel.1.own_ref = f32[2,256,256]{2,1,0:T(8,128)S(1)} custom-call(s32[4,6]{1,0:T(4,128)S(1)} %copy-done.3, s32[1]{0:T(128)} %bitcast.me_ref, bf16[25,256,128]{2,1,0:T(8,128)(2,1)S(1)} %get-tuple-element.24.coef_h, bf16[25,256,128]{2,1,0:T(8,128)(2,1)S(1)} %get-tuple-element.25.coef_l, ...), custom_call_target="tpu_custom_call" | custom-call | flops 3000000000 | bytes 8000000 | tf_op jit(solution)/shard_map/near_kernel/pallas_call | solution.py:280
  14.4 1.2 %collective-permute-done.4.from_above = f32[128,256]{1,0:T(8,128)S(1)} collective-permute-done((f32[128,256]{1,0:T(8,128)S(1)}, f32[128,256]{1,0:T(8,128)S(1)}, u32[]{:S(2)}, u32[]{:S(2)}) %collective-permute-start.4) | collective-permute-done | bytes 131104 | tf_op jit(solution)/shard_map/ppermute | solution.py:296
  15.6 1.1 %collective-permute-done.3.from_below = f32[128,256]{1,0:T(8,128)S(1)} collective-permute-done((f32[128,256]{1,0:T(8,128)S(1)}, f32[128,256]{1,0:T(8,128)S(1)}, u32[]{:S(2)}, u32[]{:S(2)}) %collective-permute-start.3) | collective-permute-done | bytes 131104 | tf_op jit(solution)/shard_map/ppermute | solution.py:296
  16.8 1.0 %collective-permute-start.5 = (f32[8,128]{1,0:T(8,128)S(1)}, f32[8,128]{1,0:T(8,128)S(1)}, u32[]{:S(2)}, u32[]{:S(2)}) collective-permute-start(f32[8,128]{1,0:T(8,128)S(1)} %slice.16), channel_id=1, source_target_pairs={{0,1},{1,0},{2,3},{3,2},{4,5},{5,4},{6,7},{7,6},{8,9},{9,8},{10,11... | collective-permute-start | bytes 12296 | tf_op jit(solution)/shard_map/ppermute | solution.py:293
  17.8 2.7 %collective-permute-start.8 = (f32[256,256]{1,0:T(8,128)S(1)}, f32[256,256]{1,0:T(8,128)S(1)}, u32[]{:S(2)}, u32[]{:S(2)}) collective-permute-start(f32[256,256]{1,0:T(8,128)S(1)} %get-tuple-element.34), channel_id=1, source_target_pairs={{0,6},{1,7},{2,0},{3,1},{4,2},{5,3},{6,4},{7,5},{8,14},{9,15},{10,... | collective-permute-start | bytes 786440 | tf_op jit(solution)/shard_map/ppermute | solution.py:296
  20.5 1.6 %here_kernel.1 = (f32[2,256,256]{2,1,0:T(8,128)S(1)}, bf16[4,6,256,128]{3,2,1,0:T(8,128)(2,1)S(1)}, bf16[4,6,256,128]{3,2,1,0:T(8,128)(2,1)S(1)}) custom-call(s32[4,6]{1,0:T(4,128)S(1)} %copy-done.3, s32[1]{0:T(128)} %bitcast.me_ref, bf16[25,256,128]{2,1,0:T(8,128)(2,1)S(1)} %get-tuple-element.24.coef_h, bf16[25,256,128]{2,1,0:T(8,128)(2,1)S(1)} %get-tuple-element.25.coef_l, ...), custom_call_target="tpu_custom_call" | custom-call | flops 3000000000 | bytes 8000000 | tf_op jit(solution)/shard_map/here_kernel/pallas_call | solution.py:280
  22.8 3.0 %collective-permute-done.8.above = f32[256,256]{1,0:T(8,128)S(1)} collective-permute-done((f32[256,256]{1,0:T(8,128)S(1)}, f32[256,256]{1,0:T(8,128)S(1)}, u32[]{:S(2)}, u32[]{:S(2)}) %collective-permute-start.8) | collective-permute-done | bytes 262176 | tf_op jit(solution)/shard_map/ppermute | solution.py:296
  25.8 1.1 %collective-permute-done.7.below = f32[256,256]{1,0:T(8,128)S(1)} collective-permute-done((f32[256,256]{1,0:T(8,128)S(1)}, f32[256,256]{1,0:T(8,128)S(1)}, u32[]{:S(2)}, u32[]{:S(2)}) %collective-permute-start.7) | collective-permute-done | bytes 262176 | tf_op jit(solution)/shard_map/ppermute | solution.py:296
  27.0 19.9 %all_to_all.10 = f32[32,16,128]{2,1,0:T(8,128)S(1)} all-to-all(f32[32,16,128]{2,1,0:T(8,128)S(1)} %sum_kernel.1), channel_id=1, replica_groups=mesh['freq'=32,'panel'=8] {'freq'}, dimensions={0} | all-to-all | bytes 524288 | tf_op jit(solution)/shard_map/all_to_all | solution.py:316
  46.8 1.6 %gate.1 = f32[512,128]{1,0:T(8,128)S(1)} custom-call(s32[1]{0:T(128)} %bitcast.me_ref, f32[512,128]{1,0:T(8,128)S(1)} %bitcast.12, s32[4,2048]{1,0:T(4,128)S(1)} %copy-done.2, bf16[896,192]{1,0:T(8,128)(2,1)S(1)} %copy-done, bf16[128,896]{1,0:T(8,128)(2,1)S(1)} %copy-done.1), custom_call_target="tpu_custom_call" | custom-call | tf_op jit(solution)/shard_map/gate/pallas_call | solution.py:320
  48.4 15.4 %all_to_all.11.refs_0_ = f32[32,16,128]{2,1,0:T(8,128)S(1)} all-to-all(f32[32,16,128]{2,1,0:T(8,128)S(1)} %bitcast.13), channel_id=1, replica_groups=mesh['freq'=32,'panel'=8] {'freq'}, dimensions={0} | all-to-all | bytes 524288 | tf_op jit(solution)/shard_map/all_to_all | solution.py:337
  63.8 3.8 %collective-permute-start.11 = (f32[32,16,128]{2,1,0:T(8,128)S(1)}, f32[32,16,128]{2,1,0:T(8,128)S(1)}, u32[]{:S(2)}, u32[]{:S(2)}) collective-permute-start(f32[32,16,128]{2,1,0:T(8,128)S(1)} %all_to_all.11.refs_0_), channel_id=1, source_target_pairs={{0,1},{1,0},{2,3},{3,2},{4,5},{5,4},{6,7},{7,6},{8,9},{9,8},{10,11... | collective-permute-start | bytes 786440 | tf_op jit(solution)/shard_map/ppermute | solution.py:293
  68.2 2.1 %collective-permute-start.9 = (f32[32,16,128]{2,1,0:T(8,128)S(1)}, f32[32,16,128]{2,1,0:T(8,128)S(1)}, u32[]{:S(2)}, u32[]{:S(2)}) collective-permute-start(f32[32,16,128]{2,1,0:T(8,128)S(1)} %all_to_all.11.refs_0_), channel_id=1, source_target_pairs={{0,6},{1,7},{2,0},{3,1},{4,2},{5,3},{6,4},{7,5},{8,14},{9,15},{10,... | collective-permute-start | bytes 786440 | tf_op jit(solution)/shard_map/ppermute | solution.py:296
  70.3 1.8 %forward_0.1.refs_5_ = f32[2,128,1024]{2,1,0:T(8,128)S(1)} custom-call(s32[4,6]{1,0:T(4,128)S(1)} %copy-done.3, s32[1]{0:T(128)} %bitcast.me_ref, f32[32,16,128]{2,1,0:T(8,128)S(1)} %all_to_all.11.refs_0_, f32[32,16,128]{2,1,0:T(8,128)S(1)} %collective-permute-done.11.refs_1_, bf16[4,6,256,128]{3,2,1,0:T(8,128)(2,1)S(1)} %get-tuple-element.35.refs_2_.refs_4_, ...), custom_call_target="tpu_custom_call" | custom-call | flops 3000000000 | bytes 8000000 | tf_op jit(solution)/shard_map/forward_0/pallas_call | solution.py:341
  72.0 4.7 %collective-permute-done.10.refs_0_ = f32[32,16,128]{2,1,0:T(8,128)S(1)} collective-permute-done((f32[32,16,128]{2,1,0:T(8,128)S(1)}, f32[32,16,128]{2,1,0:T(8,128)S(1)}, u32[]{:S(2)}, u32[]{:S(2)}) %collective-permute-start.10) | collective-permute-done | bytes 262176 | tf_op jit(solution)/shard_map/ppermute | solution.py:296
  78.4 2.1 %collective-permute-start.12 = (f32[16,16,128]{2,1,0:T(8,128)S(1)}, f32[16,16,128]{2,1,0:T(8,128)S(1)}, u32[]{:S(2)}, u32[]{:S(2)}) collective-permute-start(f32[16,16,128]{2,1,0:T(8,128)S(1)} %slice.18), channel_id=1, source_target_pairs={{0,6},{1,7},{2,0},{3,1},{4,2},{5,3},{6,4},{7,5},{8,14},{9,15},{10,... | collective-permute-start | bytes 393224 | tf_op jit(solution)/shard_map/ppermute | solution.py:296
  80.5 1.8 %forward_1.1.refs_5_ = f32[2,128,1024]{2,1,0:T(8,128)S(1)} custom-call(s32[4,6]{1,0:T(4,128)S(1)} %copy-done.3, s32[1]{0:T(128)} %bitcast.me_ref, f32[32,16,128]{2,1,0:T(8,128)S(1)} %collective-permute-done.9.refs_0_, f32[32,16,128]{2,1,0:T(8,128)S(1)} %collective-permute-done.14.refs_1_, bf16[4,6,256,128]{3,2,1,0:T(8,128)(2,1)S(1)} %get-tuple-element.35.refs_2_.refs_4_, ...), custom_call_target="tpu_custom_call" | custom-call | flops 3000000000 | bytes 8000000 | tf_op jit(solution)/shard_map/forward_1/pallas_call | solution.py:341
  82.3 1.3 %collective-permute-done.13.refs_1_ = f32[16,16,128]{2,1,0:T(8,128)S(1)} collective-permute-done((f32[16,16,128]{2,1,0:T(8,128)S(1)}, f32[16,16,128]{2,1,0:T(8,128)S(1)}, u32[]{:S(2)}, u32[]{:S(2)}) %collective-permute-start.13) | collective-permute-done | bytes 131104 | tf_op jit(solution)/shard_map/ppermute | solution.py:296
  83.6 1.3 %collective-permute-start.15 = (f32[16,16,128]{2,1,0:T(8,128)S(1)}, f32[16,16,128]{2,1,0:T(8,128)S(1)}, u32[]{:S(2)}, u32[]{:S(2)}) collective-permute-start(f32[16,16,128]{2,1,0:T(8,128)S(1)} %collective-permute-done.12.refs_0_), channel_id=1, source_target_pairs={{0,1},{1,0},{2,3},{3,2},{4,5},{5,4},{6,7},{7,6},{8,9},{9,8},{10,11... | collective-permute-start | bytes 393224 | tf_op jit(solution)/shard_map/ppermute | solution.py:293
  84.9 1.8 %forward_3.1.refs_7_ = f32[2,128,1024]{2,1,0:T(8,128)S(1)} custom-call(s32[4,6]{1,0:T(4,128)S(1)} %copy-done.3, s32[1]{0:T(128)} %bitcast.me_ref, f32[32,16,128]{2,1,0:T(8,128)S(1)} %collective-permute-done.10.refs_0_, f32[32,16,128]{2,1,0:T(8,128)S(1)} %collective-permute-done.17.refs_1_, bf16[4,6,256,128]{3,2,1,0:T(8,128)(2,1)S(1)} %get-tuple-element.35.refs_2_.refs_4_, ...), custom_call_target="tpu_custom_call" | custom-call | flops 3000000000 | bytes 8000000 | tf_op jit(solution)/shard_map/forward_3/pallas_call | solution.py:341
  86.7 2.6 %forward_2.1 = f32[2,128,1024]{2,1,0:T(8,128)} custom-call(s32[4,6]{1,0:T(4,128)S(1)} %copy-done.3, s32[1]{0:T(128)} %bitcast.me_ref, f32[16,16,128]{2,1,0:T(8,128)S(1)} %collective-permute-done.12.refs_0_, f32[16,16,128]{2,1,0:T(8,128)S(1)} %collective-permute-done.13.refs_1_, f32[16,16,128]{2,1,0:T(8,128)S(1)} %collective-permute-done.15.refs_2_, ...), custom_call_target="tpu_custom_call" | custom-call | flops 3000000000 | bytes 8000000 | tf_op jit(solution)/shard_map/forward_2/pallas_call | solution.py:341
  (41 shorter events, 4.8 us)
Async XLA Ops:
  0.0 8.9 %copy-start.3 = (s32[4,6]{1,0:T(4,128)S(1)}, s32[4,6]{1,0:T(4,128)}, u32[]{:S(2)}) copy-start(s32[4,6]{1,0:T(4,128)} %src_ref.13) | copy-start | bytes 292
  5.5 4.5 %collective-permute-start = (f32[1,256,256]{2,1,0:T(8,128)S(1)}, f32[1,256,256]{2,1,0:T(8,128)S(1)}, u32[]{:S(2)}, u32[]{:S(2)}) collective-permute-start(f32[1,256,256]{2,1,0:T(8,128)S(1)} %get-tuple-element.28), channel_id=1, source_target_pairs={{0,1},{1,0},{2,3},{3,2},{4,5},{5,4},{6,7},{7,6},{8,9},{9,8},{10,11... | collective-permute-start | bytes 786440 | tf_op jit(solution)/shard_map/ppermute | solution.py:293
  8.8 7.8 %collective-permute-start.2 = (f32[2,256,256]{2,1,0:T(8,128)S(1)}, f32[2,256,256]{2,1,0:T(8,128)S(1)}, u32[]{:S(2)}, u32[]{:S(2)}) collective-permute-start(f32[2,256,256]{2,1,0:T(8,128)S(1)} %get-tuple-element.30), channel_id=1, source_target_pairs={{0,1},{1,0},{2,3},{3,2},{4,5},{5,4},{6,7},{7,6},{8,9},{9,8},{10,11... | collective-permute-start | bytes 1572872 | tf_op jit(solution)/shard_map/ppermute | solution.py:293
  10.0 3.1 %collective-permute-start.1 = (f32[8,128]{1,0:T(8,128)S(1)}, f32[8,128]{1,0:T(8,128)S(1)}, u32[]{:S(2)}, u32[]{:S(2)}) collective-permute-start(f32[8,128]{1,0:T(8,128)S(1)} %slice.15), channel_id=1, source_target_pairs={{0,1},{1,0},{2,3},{3,2},{4,5},{5,4},{6,7},{7,6},{8,9},{9,8},{10,11... | collective-permute-start | bytes 12296 | tf_op jit(solution)/shard_map/ppermute | solution.py:293
  10.5 6.2 %collective-permute-start.3 = (f32[128,256]{1,0:T(8,128)S(1)}, f32[128,256]{1,0:T(8,128)S(1)}, u32[]{:S(2)}, u32[]{:S(2)}) collective-permute-start(f32[128,256]{1,0:T(8,128)S(1)} %get-tuple-element.29), channel_id=1, source_target_pairs={{0,2},{1,3},{2,4},{3,5},{4,6},{5,7},{6,0},{7,1},{8,10},{9,11},{10,... | collective-permute-start | bytes 393224 | tf_op jit(solution)/shard_map/ppermute | solution.py:296
  10.5 5.1 %collective-permute-start.4 = (f32[128,256]{1,0:T(8,128)S(1)}, f32[128,256]{1,0:T(8,128)S(1)}, u32[]{:S(2)}, u32[]{:S(2)}) collective-permute-start(f32[128,256]{1,0:T(8,128)S(1)} %get-tuple-element.31), channel_id=1, source_target_pairs={{0,6},{1,7},{2,0},{3,1},{4,2},{5,3},{6,4},{7,5},{8,14},{9,15},{10,... | collective-permute-start | bytes 393224 | tf_op jit(solution)/shard_map/ppermute | solution.py:296
  16.8 3.7 %collective-permute-start.5 = (f32[8,128]{1,0:T(8,128)S(1)}, f32[8,128]{1,0:T(8,128)S(1)}, u32[]{:S(2)}, u32[]{:S(2)}) collective-permute-start(f32[8,128]{1,0:T(8,128)S(1)} %slice.16), channel_id=1, source_target_pairs={{0,1},{1,0},{2,3},{3,2},{4,5},{5,4},{6,7},{7,6},{8,9},{9,8},{10,11... | collective-permute-start | bytes 12296 | tf_op jit(solution)/shard_map/ppermute | solution.py:293
  17.8 9.1 %collective-permute-start.7 = (f32[256,256]{1,0:T(8,128)S(1)}, f32[256,256]{1,0:T(8,128)S(1)}, u32[]{:S(2)}, u32[]{:S(2)}) collective-permute-start(f32[256,256]{1,0:T(8,128)S(1)} %get-tuple-element.32), channel_id=1, source_target_pairs={{0,2},{1,3},{2,4},{3,5},{4,6},{5,7},{6,0},{7,1},{8,10},{9,11},{10,... | collective-permute-start | bytes 786440 | tf_op jit(solution)/shard_map/ppermute | solution.py:296
  17.8 8.0 %collective-permute-start.8 = (f32[256,256]{1,0:T(8,128)S(1)}, f32[256,256]{1,0:T(8,128)S(1)}, u32[]{:S(2)}, u32[]{:S(2)}) collective-permute-start(f32[256,256]{1,0:T(8,128)S(1)} %get-tuple-element.34), channel_id=1, source_target_pairs={{0,6},{1,7},{2,0},{3,1},{4,2},{5,3},{6,4},{7,5},{8,14},{9,15},{10,... | collective-permute-start | bytes 786440 | tf_op jit(solution)/shard_map/ppermute | solution.py:296
  20.5 26.3 %copy-start = (bf16[896,192]{1,0:T(8,128)(2,1)S(1)}, bf16[896,192]{1,0:T(8,128)(2,1)}, u32[]{:S(2)}) copy-start(bf16[896,192]{1,0:T(8,128)(2,1)} %constant.8.clone.into_ref) | copy-start | bytes 1032196
  20.5 26.3 %copy-start.1 = (bf16[128,896]{1,0:T(8,128)(2,1)S(1)}, bf16[128,896]{1,0:T(8,128)(2,1)}, u32[]{:S(2)}) copy-start(bf16[128,896]{1,0:T(8,128)(2,1)} %constant.9.clone.outof_ref) | copy-start | bytes 688132
  20.5 26.3 %copy-start.2 = (s32[4,2048]{1,0:T(4,128)S(1)}, s32[4,2048]{1,0:T(4,128)}, u32[]{:S(2)}) copy-start(s32[4,2048]{1,0:T(4,128)} %onset_ref.1) | copy-start | bytes 98308
  22.1 48.2 %copy-start.4 = (f32[1,2,128,1024]{3,2,1,0:T(8,128)S(1)}, f32[1,2,128,1024]{3,2,1,0:T(8,128)}, u32[]{:S(2)}) copy-start(f32[1,2,128,1024]{3,2,1,0:T(8,128)} %param.9) | copy-start | bytes 3145732
  22.1 4.8 %collective-permute-start.6 = (f32[256,256]{1,0:T(8,128)S(1)}, f32[256,256]{1,0:T(8,128)S(1)}, u32[]{:S(2)}, u32[]{:S(2)}) collective-permute-start(f32[256,256]{1,0:T(8,128)S(1)} %slice_bitcast_fusion), channel_id=1, source_target_pairs={{0,1},{1,0},{2,3},{3,2},{4,5},{5,4},{6,7},{7,6},{8,9},{9,8},{10,11... | collective-permute-start | bytes 786440 | tf_op jit(solution)/shard_map/ppermute | solution.py:293
  63.8 6.4 %collective-permute-start.11 = (f32[32,16,128]{2,1,0:T(8,128)S(1)}, f32[32,16,128]{2,1,0:T(8,128)S(1)}, u32[]{:S(2)}, u32[]{:S(2)}) collective-permute-start(f32[32,16,128]{2,1,0:T(8,128)S(1)} %all_to_all.11.refs_0_), channel_id=1, source_target_pairs={{0,1},{1,0},{2,3},{3,2},{4,5},{5,4},{6,7},{7,6},{8,9},{9,8},{10,11... | collective-permute-start | bytes 786440 | tf_op jit(solution)/shard_map/ppermute | solution.py:293
  67.6 9.1 %collective-permute-start.10 = (f32[32,16,128]{2,1,0:T(8,128)S(1)}, f32[32,16,128]{2,1,0:T(8,128)S(1)}, u32[]{:S(2)}, u32[]{:S(2)}) collective-permute-start(f32[32,16,128]{2,1,0:T(8,128)S(1)} %all_to_all.11.refs_0_), channel_id=1, source_target_pairs={{0,2},{1,3},{2,4},{3,5},{4,6},{5,7},{6,0},{7,1},{8,10},{9,11},{10,... | collective-permute-start | bytes 786440 | tf_op jit(solution)/shard_map/ppermute | solution.py:296
  68.2 8.5 %collective-permute-start.9 = (f32[32,16,128]{2,1,0:T(8,128)S(1)}, f32[32,16,128]{2,1,0:T(8,128)S(1)}, u32[]{:S(2)}, u32[]{:S(2)}) collective-permute-start(f32[32,16,128]{2,1,0:T(8,128)S(1)} %all_to_all.11.refs_0_), channel_id=1, source_target_pairs={{0,6},{1,7},{2,0},{3,1},{4,2},{5,3},{6,4},{7,5},{8,14},{9,15},{10,... | collective-permute-start | bytes 786440 | tf_op jit(solution)/shard_map/ppermute | solution.py:296
  76.7 3.8 %collective-permute-start.14 = (f32[32,16,128]{2,1,0:T(8,128)S(1)}, f32[32,16,128]{2,1,0:T(8,128)S(1)}, u32[]{:S(2)}, u32[]{:S(2)}) collective-permute-start(f32[32,16,128]{2,1,0:T(8,128)S(1)} %collective-permute-done.9.refs_0_), channel_id=1, source_target_pairs={{0,1},{1,0},{2,3},{3,2},{4,5},{5,4},{6,7},{7,6},{8,9},{9,8},{10,11... | collective-permute-start | bytes 786440 | tf_op jit(solution)/shard_map/ppermute | solution.py:293
  77.6 7.3 %collective-permute-start.17 = (f32[32,16,128]{2,1,0:T(8,128)S(1)}, f32[32,16,128]{2,1,0:T(8,128)S(1)}, u32[]{:S(2)}, u32[]{:S(2)}) collective-permute-start(f32[32,16,128]{2,1,0:T(8,128)S(1)} %collective-permute-done.10.refs_0_), channel_id=1, source_target_pairs={{0,1},{1,0},{2,3},{3,2},{4,5},{5,4},{6,7},{7,6},{8,9},{9,8},{10,11... | collective-permute-start | bytes 786440 | tf_op jit(solution)/shard_map/ppermute | solution.py:293
  77.7 6.0 %collective-permute-start.13 = (f32[16,16,128]{2,1,0:T(8,128)S(1)}, f32[16,16,128]{2,1,0:T(8,128)S(1)}, u32[]{:S(2)}, u32[]{:S(2)}) collective-permute-start(f32[16,16,128]{2,1,0:T(8,128)S(1)} %slice.19), channel_id=1, source_target_pairs={{0,2},{1,3},{2,4},{3,5},{4,6},{5,7},{6,0},{7,1},{8,10},{9,11},{10,... | collective-permute-start | bytes 393224 | tf_op jit(solution)/shard_map/ppermute | solution.py:296
  78.4 5.3 %collective-permute-start.12 = (f32[16,16,128]{2,1,0:T(8,128)S(1)}, f32[16,16,128]{2,1,0:T(8,128)S(1)}, u32[]{:S(2)}, u32[]{:S(2)}) collective-permute-start(f32[16,16,128]{2,1,0:T(8,128)S(1)} %slice.18), channel_id=1, source_target_pairs={{0,6},{1,7},{2,0},{3,1},{4,2},{5,3},{6,4},{7,5},{8,14},{9,15},{10,... | collective-permute-start | bytes 393224 | tf_op jit(solution)/shard_map/ppermute | solution.py:296
  83.6 3.0 %collective-permute-start.15 = (f32[16,16,128]{2,1,0:T(8,128)S(1)}, f32[16,16,128]{2,1,0:T(8,128)S(1)}, u32[]{:S(2)}, u32[]{:S(2)}) collective-permute-start(f32[16,16,128]{2,1,0:T(8,128)S(1)} %collective-permute-done.12.refs_0_), channel_id=1, source_target_pairs={{0,1},{1,0},{2,3},{3,2},{4,5},{5,4},{6,7},{7,6},{8,9},{9,8},{10,11... | collective-permute-start | bytes 393224 | tf_op jit(solution)/shard_map/ppermute | solution.py:293
  84.9 1.8 %collective-permute-start.16 = (f32[16,16,128]{2,1,0:T(8,128)S(1)}, f32[16,16,128]{2,1,0:T(8,128)S(1)}, u32[]{:S(2)}, u32[]{:S(2)}) collective-permute-start(f32[16,16,128]{2,1,0:T(8,128)S(1)} %collective-permute-done.13.refs_1_), channel_id=1, source_target_pairs={{0,1},{1,0},{2,3},{3,2},{4,5},{5,4},{6,7},{7,6},{8,9},{9,8},{10,11... | collective-permute-start | bytes 393224 | tf_op jit(solution)/shard_map/ppermute | solution.py:293

commit v6 on v3

--- a/solution.py
+++ b/solution.py
@@ -173,8 +173,8 @@
             y_ref[picks[h], :] = back[:, h * lanes : (h + 1) * lanes]
 
 
-def forward_kernel(steps, last, pieces, src_ref, me_ref, *refs):
-    number = 2 * len(steps)
+def forward_kernel(targets, last, pieces, src_ref, me_ref, *refs):
+    number = len(targets)
     left_h, left_l, right_ref, total_ref, out_ref, *scratch = refs[number * pieces :]
     panels, slots, tile, width = left_h.shape
     me = me_ref[0]
@@ -195,7 +195,7 @@
     for p in range(panels):
         parts = []
         for i, (high, low) in enumerate(tiles):
-            slot, place = find_slot(src_ref, p, tile_of(me, steps[i // 2], i % 2), slots)
+            slot, place = find_slot(src_ref, p, tile_of(me, *targets[i]), slots)
             right = right_ref[place]
             pair = dot(high, right)
             products = pair[:, :width] + pair[:, width:] + dot(low, right[:, :width])
@@ -338,30 +338,32 @@
     )(me, moved.reshape(2 * rows, tile // 2), onset, jnp.asarray(into), jnp.asarray(outof))
     back = lax.all_to_all(gated.reshape(count, 4 * group, tile // 2), "freq", split_axis=0, concat_axis=0, tiled=True)
 
-    def forward(steps, tiles, total, last=False):
+    def forward(targets, tiles, total, last=False):
         number = len(tiles)
         return pl.pallas_call(
-            functools.partial(forward_kernel, steps, last, number // (2 * len(steps))),
+            functools.partial(forward_kernel, targets, last, number // len(targets)),
             in_specs=[in_smem, in_smem] + [in_vmem] * (number + 4),
             out_specs=in_hbm if last else in_vmem,
             out_shape=jax.ShapeDtypeStruct(total.shape, F32),
             scratch_shapes=[pltpu.VMEM((panels, 2, virtual, tile), F32), pltpu.SemaphoreType.DMA((panels,))] if last else [],
             compiler_params=pltpu.CompilerParams(vmem_limit_bytes=24 * mib),
             cost_estimate=cost,
-            name="forward_" + "_".join(str(step) for step in steps),
+            name="forward_" + "_".join(f"{step}{other}" for step, other in targets),
         )(tile_src, me, *tiles, left_h, left_l, right_kept, total)
 
     above, below = shift(back, -1), shift(back, 1)
-    total = forward((0,), [back, exchange(back)], direct[0])
+    both = lambda step: ((step, 0), (step, 1))
+    total = forward(both(0), [back, exchange(back)], direct[0])
     above, below, total = lax.optimization_barrier((above, below, total))
     cut = count // 2
     far = [shift(above[:cut], -1), shift(below[cut:], 1)]
     above_other, below_other = exchange(above), exchange(below)
-    total = forward((1,), [above, above_other], total)
+    total = forward(both(1), [above, above_other], total)
+    total = forward(both(3), [below, below_other], total)
     *far, total = lax.optimization_barrier((*far, total))
-    far = far + [exchange(part) for part in far]
-    total = forward((3,), [below, below_other], total)
-    return forward((2,), far, total, last=True)[None]
+    far_other = [exchange(part) for part in far]
+    total = forward(((2, 0),), far, total)
+    return forward(((2, 1),), far_other, total, last=True)[None]
 
 
 def solution(mesh):

time: 87.6 us -> 87.3 us (level)
  waiting for transfers between devices: 12.8 us -> 11.4 us
  Pallas kernels: 18.1 us -> 19.3 us
    ppermute x8, waiting for transfers between devices: 12.3 us -> 10.9 us  [shift(): return lax.ppermute(x, 'panel', [(i, (i + 2 * by) % 8) for i in range(8)])]
    pallas_call x4 -> x5, Pallas kernels: 7.85 us -> 9.05 us  [forward(): pl.pallas_call(functools.partial(forward_kernel, targets, last, number //...]
  transfers between devices with their start and end apart: 16 -> 16, of which waited for: 6 -> 5; matrix products, arithmetic and copies ran while one was open for 0% -> 0% of each run, Pallas kernels for 9% -> 11%
where the time goes in v6:
time: 87.3 us; the launch traced here: 87.2 us
  blocking collectives  33.7 us (39%)
  starting transfers between devices  22.2 us (25%)
  Pallas kernels  19.3 us (22%)
  waiting for transfers between devices  11.4 us (13%)
    all_to_all x1, blocking collectives, shards(): lax.all_to_all(moved, 'freq', split_axis=0, concat_axis=0, tiled=True)  19.7 us
    all_to_all x1, blocking collectives, shards(): lax.all_to_all(gated.reshape(count, 4 * group, tile // 2), 'freq', split_...  14 us
    ppermute x8, starting transfers between devices, exchange(): return lax.ppermute(x, 'panel', swap)  11.3 us
    ppermute x8, starting transfers between devices, shift(): return lax.ppermute(x, 'panel', [(i, (i + 2 * by) % 8) for i in range(8)])  10.9 us
    ppermute x8, waiting for transfers between devices, shift(): return lax.ppermute(x, 'panel', [(i, (i + 2 * by) % 8) for i in range(8)])  10.9 us
    pallas_call x5, Pallas kernels, forward(): pl.pallas_call(functools.partial(forward_kernel, targets, last, number //...  9.05 us
    pallas_call x1, Pallas kernels, shards(): pl.pallas_call(adjoint_kernel, in_specs=[in_smem] + [in_hbm] * 4, out_spe...  5.5 us
    pallas_call x5, Pallas kernels, local(): pl.pallas_call(kernel, in_specs=[in_smem] * (2 * scalars) + [in_vmem] * (...  3.14 us
  transfers between devices with their start and end apart: 16, of which 5 were waited for; matrix products, arithmetic and copies ran while one was open for 0% of the time, Pallas kernels for 11%

profile of v6, /device:TPU:1, one launch (start us, length us, event | category | flops | bytes accessed | tf_op | source)
XLA Modules:
  0.0 87.2 jit_solution(4696413821040770197)
XLA Ops:
  0.0 5.5 %adjoint.1 = (bf16[25,256,128]{2,1,0:T(8,128)(2,1)S(1)}, bf16[25,256,128]{2,1,0:T(8,128)(2,1)S(1)}, bf16[25,256,256]{2,1,0:T(8,128)(2,1)S(1)}, f32[4,6,256,128]{3,2,1,0:T(8,128)S(1)}, f32[3,256,256]{2,1,0:T(8,128)S(1)}) custom-call(s32[1]{0:T(128)} %bitcast.me_ref, s32[4,6]{1,0:T(4,128)} %src_ref.13, f32[2,128,1024]{2,1,0:T(8,128)} %bitcast.19, ...), custom_call_target="tpu_custom_call" | custom-call | tf_op jit(solution)/shard_map/adjoint/pallas_call | solution.py:258
  5.5 3.3 %collective-permute-start = (f32[3,256,256]{2,1,0:T(8,128)S(1)}, f32[3,256,256]{2,1,0:T(8,128)S(1)}, u32[]{:S(2)}, u32[]{:S(2)}) collective-permute-start(f32[3,256,256]{2,1,0:T(8,128)S(1)} %get-tuple-element.32), channel_id=1, source_target_pairs={{0,1},{1,0},{2,3},{3,2},{4,5},{5,4},{6,7},{7,6},{8,9},{9,8},{10,11... | collective-permute-start | bytes 2359304 | tf_op jit(solution)/shard_map/ppermute | solution.py:292
  8.8 1.4 %own_kernel.1.own_ref = f32[3,256,256]{2,1,0:T(8,128)S(1)} custom-call(s32[4,6]{1,0:T(4,128)S(1)} %copy-done.3, s32[1]{0:T(128)} %bitcast.me_ref, bf16[25,256,128]{2,1,0:T(8,128)(2,1)S(1)} %get-tuple-element.28.coef_h, bf16[25,256,128]{2,1,0:T(8,128)(2,1)S(1)} %get-tuple-element.29.coef_l, bf16[25,256,256]{2,1,0:T(8,128)(2,1)S(1)} %get-tuple-element.30.right_ref.refs_4_), custom_call_target="tpu_custom_call" | custom-call | flops 3000000000 | bytes 8000000 | tf_op jit(solution)/shard_map/own_kernel/pallas_call | solution.py:279
  11.3 2.7 %collective-permute-start.3 = (f32[2,128,256]{2,1,0:T(8,128)S(1)}, f32[2,128,256]{2,1,0:T(8,128)S(1)}, u32[]{:S(2)}, u32[]{:S(2)}) collective-permute-start(f32[2,128,256]{2,1,0:T(8,128)S(1)} %get-tuple-element.35), channel_id=1, source_target_pairs={{0,6},{1,7},{2,0},{3,1},{4,2},{5,3},{6,4},{7,5},{8,14},{9,15},{10,... | collective-permute-start | bytes 786440 | tf_op jit(solution)/shard_map/ppermute | solution.py:295
  14.0 1.6 %here_kernel.1 = (f32[2,256,256]{2,1,0:T(8,128)S(1)}, bf16[4,6,256,128]{3,2,1,0:T(8,128)(2,1)S(1)}, bf16[4,6,256,128]{3,2,1,0:T(8,128)(2,1)S(1)}) custom-call(s32[4,6]{1,0:T(4,128)S(1)} %copy-done.3, s32[1]{0:T(128)} %bitcast.me_ref, bf16[25,256,128]{2,1,0:T(8,128)(2,1)S(1)} %get-tuple-element.28.coef_h, bf16[25,256,128]{2,1,0:T(8,128)(2,1)S(1)} %get-tuple-element.29.coef_l, ...), custom_call_target="tpu_custom_call" | custom-call | flops 3000000000 | bytes 8000000 | tf_op jit(solution)/shard_map/here_kernel/pallas_call | solution.py:279
  16.4 2.8 %collective-permute-done.3.from_above.above = f32[2,128,256]{2,1,0:T(8,128)S(1)} collective-permute-done((f32[2,128,256]{2,1,0:T(8,128)S(1)}, f32[2,128,256]{2,1,0:T(8,128)S(1)}, u32[]{:S(2)}, u32[]{:S(2)}) %collective-permute-start.3) | collective-permute-done | bytes 262176 | tf_op jit(solution)/shard_map/ppermute | solution.py:295
  19.2 1.1 %collective-permute-done.2.from_below.below = f32[2,128,256]{2,1,0:T(8,128)S(1)} collective-permute-done((f32[2,128,256]{2,1,0:T(8,128)S(1)}, f32[2,128,256]{2,1,0:T(8,128)S(1)}, u32[]{:S(2)}, u32[]{:S(2)}) %collective-permute-start.2) | collective-permute-done | bytes 262176 | tf_op jit(solution)/shard_map/ppermute | solution.py:295
  20.4 2.7 %collective-permute-start.6 = (f32[128,256]{1,0:T(8,128)S(1)}, f32[128,256]{1,0:T(8,128)S(1)}, u32[]{:S(2)}, u32[]{:S(2)}) collective-permute-start(f32[128,256]{1,0:T(8,128)S(1)} %get-tuple-element.42), channel_id=1, source_target_pairs={{0,6},{1,7},{2,0},{3,1},{4,2},{5,3},{6,4},{7,5},{8,14},{9,15},{10,... | collective-permute-start | bytes 393224 | tf_op jit(solution)/shard_map/ppermute | solution.py:295
  23.1 2.4 %collective-permute-done.5.relayed_below = f32[128,256]{1,0:T(8,128)S(1)} collective-permute-done((f32[128,256]{1,0:T(8,128)S(1)}, f32[128,256]{1,0:T(8,128)S(1)}, u32[]{:S(2)}, u32[]{:S(2)}) %collective-permute-start.5) | collective-permute-done | bytes 131104 | tf_op jit(solution)/shard_map/ppermute | solution.py:295
  25.5 19.7 %all_to_all.10 = f32[32,16,128]{2,1,0:T(8,128)S(1)} all-to-all(f32[32,16,128]{2,1,0:T(8,128)S(1)} %sum_kernel.1), channel_id=1, replica_groups=mesh['freq'=32,'panel'=8] {'freq'}, dimensions={0} | all-to-all | bytes 524288 | tf_op jit(solution)/shard_map/all_to_all | solution.py:318
  45.2 1.6 %gate.1 = f32[512,128]{1,0:T(8,128)S(1)} custom-call(s32[1]{0:T(128)} %bitcast.me_ref, f32[512,128]{1,0:T(8,128)S(1)} %bitcast.14, s32[4,2048]{1,0:T(4,128)S(1)} %copy-done.2, bf16[896,192]{1,0:T(8,128)(2,1)S(1)} %copy-done, bf16[128,896]{1,0:T(8,128)(2,1)S(1)} %copy-done.1), custom_call_target="tpu_custom_call" | custom-call | tf_op jit(solution)/shard_map/gate/pallas_call | solution.py:322
  46.9 14.0 %all_to_all.11.refs_0_ = f32[32,16,128]{2,1,0:T(8,128)S(1)} all-to-all(f32[32,16,128]{2,1,0:T(8,128)S(1)} %bitcast.15), channel_id=1, replica_groups=mesh['freq'=32,'panel'=8] {'freq'}, dimensions={0} | all-to-all | bytes 524288 | tf_op jit(solution)/shard_map/all_to_all | solution.py:339
  60.9 4.7 %collective-permute-start.9 = (f32[32,16,128]{2,1,0:T(8,128)S(1)}, f32[32,16,128]{2,1,0:T(8,128)S(1)}, u32[]{:S(2)}, u32[]{:S(2)}) collective-permute-start(f32[32,16,128]{2,1,0:T(8,128)S(1)} %all_to_all.11.refs_0_), channel_id=1, source_target_pairs={{0,1},{1,0},{2,3},{3,2},{4,5},{5,4},{6,7},{7,6},{8,9},{9,8},{10,11... | collective-permute-start | bytes 786440 | tf_op jit(solution)/shard_map/ppermute | solution.py:292
  65.6 1.0 %collective-permute-start.8 = (f32[32,16,128]{2,1,0:T(8,128)S(1)}, f32[32,16,128]{2,1,0:T(8,128)S(1)}, u32[]{:S(2)}, u32[]{:S(2)}) collective-permute-start(f32[32,16,128]{2,1,0:T(8,128)S(1)} %all_to_all.11.refs_0_), channel_id=1, source_target_pairs={{0,2},{1,3},{2,4},{3,5},{4,6},{5,7},{6,0},{7,1},{8,10},{9,11},{10,... | collective-permute-start | bytes 786440 | tf_op jit(solution)/shard_map/ppermute | solution.py:295
  66.6 1.7 %collective-permute-start.7 = (f32[32,16,128]{2,1,0:T(8,128)S(1)}, f32[32,16,128]{2,1,0:T(8,128)S(1)}, u32[]{:S(2)}, u32[]{:S(2)}) collective-permute-start(f32[32,16,128]{2,1,0:T(8,128)S(1)} %all_to_all.11.refs_0_), channel_id=1, source_target_pairs={{0,6},{1,7},{2,0},{3,1},{4,2},{5,3},{6,4},{7,5},{8,14},{9,15},{10,... | collective-permute-start | bytes 786440 | tf_op jit(solution)/shard_map/ppermute | solution.py:295
  68.3 1.8 %forward_00_01.1.refs_5_ = f32[2,128,1024]{2,1,0:T(8,128)S(1)} custom-call(s32[4,6]{1,0:T(4,128)S(1)} %copy-done.3, s32[1]{0:T(128)} %bitcast.me_ref, f32[32,16,128]{2,1,0:T(8,128)S(1)} %all_to_all.11.refs_0_, f32[32,16,128]{2,1,0:T(8,128)S(1)} %collective-permute-done.9.refs_1_, bf16[4,6,256,128]{3,2,1,0:T(8,128)(2,1)S(1)} %get-tuple-element.43.refs_2_, ...), custom_call_target="tpu_custom_call" | custom-call | flops 3000000000 | bytes 8000000 | tf_op jit(solution)/shard_map/forward_00_01/pallas_call | solution.py:343
  70.1 4.7 %collective-permute-done.8.refs_0_ = f32[32,16,128]{2,1,0:T(8,128)S(1)} collective-permute-done((f32[32,16,128]{2,1,0:T(8,128)S(1)}, f32[32,16,128]{2,1,0:T(8,128)S(1)}, u32[]{:S(2)}, u32[]{:S(2)}) %collective-permute-start.8) | collective-permute-done | bytes 262176 | tf_op jit(solution)/shard_map/ppermute | solution.py:295
  75.7 1.1 %collective-permute-start.11 = (f32[16,16,128]{2,1,0:T(8,128)S(1)}, f32[16,16,128]{2,1,0:T(8,128)S(1)}, u32[]{:S(2)}, u32[]{:S(2)}) collective-permute-start(f32[16,16,128]{2,1,0:T(8,128)S(1)} %slice.15), channel_id=1, source_target_pairs={{0,2},{1,3},{2,4},{3,5},{4,6},{5,7},{6,0},{7,1},{8,10},{9,11},{10,... | collective-permute-start | bytes 393224 | tf_op jit(solution)/shard_map/ppermute | solution.py:295
  76.8 1.8 %collective-permute-start.10 = (f32[16,16,128]{2,1,0:T(8,128)S(1)}, f32[16,16,128]{2,1,0:T(8,128)S(1)}, u32[]{:S(2)}, u32[]{:S(2)}) collective-permute-start(f32[16,16,128]{2,1,0:T(8,128)S(1)} %slice.14), channel_id=1, source_target_pairs={{0,6},{1,7},{2,0},{3,1},{4,2},{5,3},{6,4},{7,5},{8,14},{9,15},{10,... | collective-permute-start | bytes 393224 | tf_op jit(solution)/shard_map/ppermute | solution.py:295
  78.6 1.8 %forward_10_11.1.refs_5_ = f32[2,128,1024]{2,1,0:T(8,128)S(1)} custom-call(s32[4,6]{1,0:T(4,128)S(1)} %copy-done.3, s32[1]{0:T(128)} %bitcast.me_ref, f32[32,16,128]{2,1,0:T(8,128)S(1)} %collective-permute-done.7.refs_0_, f32[32,16,128]{2,1,0:T(8,128)S(1)} %collective-permute-done.13.refs_1_, bf16[4,6,256,128]{3,2,1,0:T(8,128)(2,1)S(1)} %get-tuple-element.43.refs_2_, ...), custom_call_target="tpu_custom_call" | custom-call | flops 3000000000 | bytes 8000000 | tf_op jit(solution)/shard_map/forward_10_11/pallas_call | solution.py:343
  80.3 1.8 %forward_30_31.1.refs_5_ = f32[2,128,1024]{2,1,0:T(8,128)S(1)} custom-call(s32[4,6]{1,0:T(4,128)S(1)} %copy-done.3, s32[1]{0:T(128)} %bitcast.me_ref, f32[32,16,128]{2,1,0:T(8,128)S(1)} %collective-permute-done.8.refs_0_, f32[32,16,128]{2,1,0:T(8,128)S(1)} %collective-permute-done.12.refs_1_, bf16[4,6,256,128]{3,2,1,0:T(8,128)(2,1)S(1)} %get-tuple-element.43.refs_2_, ...), custom_call_target="tpu_custom_call" | custom-call | flops 3000000000 | bytes 8000000 | tf_op jit(solution)/shard_map/forward_30_31/pallas_call | solution.py:343
  82.1 1.0 %collective-permute-start.14 = (f32[16,16,128]{2,1,0:T(8,128)S(1)}, f32[16,16,128]{2,1,0:T(8,128)S(1)}, u32[]{:S(2)}, u32[]{:S(2)}) collective-permute-start(f32[16,16,128]{2,1,0:T(8,128)S(1)} %collective-permute-done.10.refs_0_), channel_id=1, source_target_pairs={{0,1},{1,0},{2,3},{3,2},{4,5},{5,4},{6,7},{7,6},{8,9},{9,8},{10,11... | collective-permute-start | bytes 393224 | tf_op jit(solution)/shard_map/ppermute | solution.py:292
  83.2 1.5 %forward_20.1.refs_5_ = f32[2,128,1024]{2,1,0:T(8,128)S(1)} custom-call(s32[4,6]{1,0:T(4,128)S(1)} %copy-done.3, s32[1]{0:T(128)} %bitcast.me_ref, f32[16,16,128]{2,1,0:T(8,128)S(1)} %collective-permute-done.10.refs_0_, f32[16,16,128]{2,1,0:T(8,128)S(1)} %collective-permute-done.11.refs_1_, bf16[4,6,256,128]{3,2,1,0:T(8,128)(2,1)S(1)} %get-tuple-element.43.refs_2_, ...), custom_call_target="tpu_custom_call" | custom-call | flops 3000000000 | bytes 8000000 | tf_op jit(solution)/shard_map/forward_20/pallas_call | solution.py:343
  84.7 2.3 %forward_21.1 = f32[2,128,1024]{2,1,0:T(8,128)} custom-call(s32[4,6]{1,0:T(4,128)S(1)} %copy-done.3, s32[1]{0:T(128)} %bitcast.me_ref, f32[16,16,128]{2,1,0:T(8,128)S(1)} %collective-permute-done.14.refs_0_, f32[16,16,128]{2,1,0:T(8,128)S(1)} %collective-permute-done.15.refs_1_, bf16[4,6,256,128]{3,2,1,0:T(8,128)(2,1)S(1)} %get-tuple-element.43.refs_2_, ...), custom_call_target="tpu_custom_call" | custom-call | flops 3000000000 | bytes 8000000 | tf_op jit(solution)/shard_map/forward_21/pallas_call | solution.py:343
  (36 shorter events, 3.1 us)
Async XLA Ops:
  0.0 8.8 %copy-start.3 = (s32[4,6]{1,0:T(4,128)S(1)}, s32[4,6]{1,0:T(4,128)}, u32[]{:S(2)}) copy-start(s32[4,6]{1,0:T(4,128)} %src_ref.13) | copy-start | bytes 292
  5.5 5.2 %collective-permute-start = (f32[3,256,256]{2,1,0:T(8,128)S(1)}, f32[3,256,256]{2,1,0:T(8,128)S(1)}, u32[]{:S(2)}, u32[]{:S(2)}) collective-permute-start(f32[3,256,256]{2,1,0:T(8,128)S(1)} %get-tuple-element.32), channel_id=1, source_target_pairs={{0,1},{1,0},{2,3},{3,2},{4,5},{5,4},{6,7},{7,6},{8,9},{9,8},{10,11... | collective-permute-start | bytes 2359304 | tf_op jit(solution)/shard_map/ppermute | solution.py:292
  10.8 3.1 %collective-permute-start.1 = (f32[8,128]{1,0:T(8,128)S(1)}, f32[8,128]{1,0:T(8,128)S(1)}, u32[]{:S(2)}, u32[]{:S(2)}) collective-permute-start(f32[8,128]{1,0:T(8,128)S(1)} %slice_bitcast_fusion.1), channel_id=1, source_target_pairs={{0,1},{1,0},{2,3},{3,2},{4,5},{5,4},{6,7},{7,6},{8,9},{9,8},{10,11... | collective-permute-start | bytes 12296 | tf_op jit(solution)/shard_map/ppermute | solution.py:292
  11.3 9.0 %collective-permute-start.2 = (f32[2,128,256]{2,1,0:T(8,128)S(1)}, f32[2,128,256]{2,1,0:T(8,128)S(1)}, u32[]{:S(2)}, u32[]{:S(2)}) collective-permute-start(f32[2,128,256]{2,1,0:T(8,128)S(1)} %get-tuple-element.33), channel_id=1, source_target_pairs={{0,2},{1,3},{2,4},{3,5},{4,6},{5,7},{6,0},{7,1},{8,10},{9,11},{10,... | collective-permute-start | bytes 786440 | tf_op jit(solution)/shard_map/ppermute | solution.py:295
  11.3 7.9 %collective-permute-start.3 = (f32[2,128,256]{2,1,0:T(8,128)S(1)}, f32[2,128,256]{2,1,0:T(8,128)S(1)}, u32[]{:S(2)}, u32[]{:S(2)}) collective-permute-start(f32[2,128,256]{2,1,0:T(8,128)S(1)} %get-tuple-element.35), channel_id=1, source_target_pairs={{0,6},{1,7},{2,0},{3,1},{4,2},{5,3},{6,4},{7,5},{8,14},{9,15},{10,... | collective-permute-start | bytes 786440 | tf_op jit(solution)/shard_map/ppermute | solution.py:295
  15.5 29.7 %copy-start = (bf16[896,192]{1,0:T(8,128)(2,1)S(1)}, bf16[896,192]{1,0:T(8,128)(2,1)}, u32[]{:S(2)}) copy-start(bf16[896,192]{1,0:T(8,128)(2,1)} %constant.8.clone.into_ref) | copy-start | bytes 1032196
  15.6 29.7 %copy-start.1 = (bf16[128,896]{1,0:T(8,128)(2,1)S(1)}, bf16[128,896]{1,0:T(8,128)(2,1)}, u32[]{:S(2)}) copy-start(bf16[128,896]{1,0:T(8,128)(2,1)} %constant.9.clone.outof_ref) | copy-start | bytes 688132
  15.6 29.7 %copy-start.2 = (s32[4,2048]{1,0:T(4,128)S(1)}, s32[4,2048]{1,0:T(4,128)}, u32[]{:S(2)}) copy-start(s32[4,2048]{1,0:T(4,128)} %onset_ref.1) | copy-start | bytes 98308
  15.6 52.7 %copy-start.4 = (f32[1,2,128,1024]{3,2,1,0:T(8,128)S(1)}, f32[1,2,128,1024]{3,2,1,0:T(8,128)}, u32[]{:S(2)}) copy-start(f32[1,2,128,1024]{3,2,1,0:T(8,128)} %param.9) | copy-start | bytes 3145732
  15.6 4.7 %collective-permute-start.4 = (f32[256,256]{1,0:T(8,128)S(1)}, f32[256,256]{1,0:T(8,128)S(1)}, u32[]{:S(2)}, u32[]{:S(2)}) collective-permute-start(f32[256,256]{1,0:T(8,128)S(1)} %slice_bitcast_fusion), channel_id=1, source_target_pairs={{0,1},{1,0},{2,3},{3,2},{4,5},{5,4},{6,7},{7,6},{8,9},{9,8},{10,11... | collective-permute-start | bytes 786440 | tf_op jit(solution)/shard_map/ppermute | solution.py:292
  20.3 5.1 %collective-permute-start.5 = (f32[128,256]{1,0:T(8,128)S(1)}, f32[128,256]{1,0:T(8,128)S(1)}, u32[]{:S(2)}, u32[]{:S(2)}) collective-permute-start(f32[128,256]{1,0:T(8,128)S(1)} %get-tuple-element.41), channel_id=1, source_target_pairs={{0,2},{1,3},{2,4},{3,5},{4,6},{5,7},{6,0},{7,1},{8,10},{9,11},{10,... | collective-permute-start | bytes 393224 | tf_op jit(solution)/shard_map/ppermute | solution.py:295
  20.4 5.0 %collective-permute-start.6 = (f32[128,256]{1,0:T(8,128)S(1)}, f32[128,256]{1,0:T(8,128)S(1)}, u32[]{:S(2)}, u32[]{:S(2)}) collective-permute-start(f32[128,256]{1,0:T(8,128)S(1)} %get-tuple-element.42), channel_id=1, source_target_pairs={{0,6},{1,7},{2,0},{3,1},{4,2},{5,3},{6,4},{7,5},{8,14},{9,15},{10,... | collective-permute-start | bytes 393224 | tf_op jit(solution)/shard_map/ppermute | solution.py:295
  60.9 7.4 %collective-permute-start.9 = (f32[32,16,128]{2,1,0:T(8,128)S(1)}, f32[32,16,128]{2,1,0:T(8,128)S(1)}, u32[]{:S(2)}, u32[]{:S(2)}) collective-permute-start(f32[32,16,128]{2,1,0:T(8,128)S(1)} %all_to_all.11.refs_0_), channel_id=1, source_target_pairs={{0,1},{1,0},{2,3},{3,2},{4,5},{5,4},{6,7},{7,6},{8,9},{9,8},{10,11... | collective-permute-start | bytes 786440 | tf_op jit(solution)/shard_map/ppermute | solution.py:292
  65.6 9.1 %collective-permute-start.8 = (f32[32,16,128]{2,1,0:T(8,128)S(1)}, f32[32,16,128]{2,1,0:T(8,128)S(1)}, u32[]{:S(2)}, u32[]{:S(2)}) collective-permute-start(f32[32,16,128]{2,1,0:T(8,128)S(1)} %all_to_all.11.refs_0_), channel_id=1, source_target_pairs={{0,2},{1,3},{2,4},{3,5},{4,6},{5,7},{6,0},{7,1},{8,10},{9,11},{10,... | collective-permute-start | bytes 786440 | tf_op jit(solution)/shard_map/ppermute | solution.py:295
  66.6 8.1 %collective-permute-start.7 = (f32[32,16,128]{2,1,0:T(8,128)S(1)}, f32[32,16,128]{2,1,0:T(8,128)S(1)}, u32[]{:S(2)}, u32[]{:S(2)}) collective-permute-start(f32[32,16,128]{2,1,0:T(8,128)S(1)} %all_to_all.11.refs_0_), channel_id=1, source_target_pairs={{0,6},{1,7},{2,0},{3,1},{4,2},{5,3},{6,4},{7,5},{8,14},{9,15},{10,... | collective-permute-start | bytes 786440 | tf_op jit(solution)/shard_map/ppermute | solution.py:295
  74.8 3.8 %collective-permute-start.13 = (f32[32,16,128]{2,1,0:T(8,128)S(1)}, f32[32,16,128]{2,1,0:T(8,128)S(1)}, u32[]{:S(2)}, u32[]{:S(2)}) collective-permute-start(f32[32,16,128]{2,1,0:T(8,128)S(1)} %collective-permute-done.7.refs_0_), channel_id=1, source_target_pairs={{0,1},{1,0},{2,3},{3,2},{4,5},{5,4},{6,7},{7,6},{8,9},{9,8},{10,11... | collective-permute-start | bytes 786440 | tf_op jit(solution)/shard_map/ppermute | solution.py:292
  75.6 4.7 %collective-permute-start.12 = (f32[32,16,128]{2,1,0:T(8,128)S(1)}, f32[32,16,128]{2,1,0:T(8,128)S(1)}, u32[]{:S(2)}, u32[]{:S(2)}) collective-permute-start(f32[32,16,128]{2,1,0:T(8,128)S(1)} %collective-permute-done.8.refs_0_), channel_id=1, source_target_pairs={{0,1},{1,0},{2,3},{3,2},{4,5},{5,4},{6,7},{7,6},{8,9},{9,8},{10,11... | collective-permute-start | bytes 786440 | tf_op jit(solution)/shard_map/ppermute | solution.py:292
  75.7 6.4 %collective-permute-start.11 = (f32[16,16,128]{2,1,0:T(8,128)S(1)}, f32[16,16,128]{2,1,0:T(8,128)S(1)}, u32[]{:S(2)}, u32[]{:S(2)}) collective-permute-start(f32[16,16,128]{2,1,0:T(8,128)S(1)} %slice.15), channel_id=1, source_target_pairs={{0,2},{1,3},{2,4},{3,5},{4,6},{5,7},{6,0},{7,1},{8,10},{9,11},{10,... | collective-permute-start | bytes 393224 | tf_op jit(solution)/shard_map/ppermute | solution.py:295
  76.8 5.3 %collective-permute-start.10 = (f32[16,16,128]{2,1,0:T(8,128)S(1)}, f32[16,16,128]{2,1,0:T(8,128)S(1)}, u32[]{:S(2)}, u32[]{:S(2)}) collective-permute-start(f32[16,16,128]{2,1,0:T(8,128)S(1)} %slice.14), channel_id=1, source_target_pairs={{0,6},{1,7},{2,0},{3,1},{4,2},{5,3},{6,4},{7,5},{8,14},{9,15},{10,... | collective-permute-start | bytes 393224 | tf_op jit(solution)/shard_map/ppermute | solution.py:295
  82.1 2.6 %collective-permute-start.14 = (f32[16,16,128]{2,1,0:T(8,128)S(1)}, f32[16,16,128]{2,1,0:T(8,128)S(1)}, u32[]{:S(2)}, u32[]{:S(2)}) collective-permute-start(f32[16,16,128]{2,1,0:T(8,128)S(1)} %collective-permute-done.10.refs_0_), channel_id=1, source_target_pairs={{0,1},{1,0},{2,3},{3,2},{4,5},{5,4},{6,7},{7,6},{8,9},{9,8},{10,11... | collective-permute-start | bytes 393224 | tf_op jit(solution)/shard_map/ppermute | solution.py:292
  83.1 1.6 %collective-permute-start.15 = (f32[16,16,128]{2,1,0:T(8,128)S(1)}, f32[16,16,128]{2,1,0:T(8,128)S(1)}, u32[]{:S(2)}, u32[]{:S(2)}) collective-permute-start(f32[16,16,128]{2,1,0:T(8,128)S(1)} %collective-permute-done.11.refs_1_), channel_id=1, source_target_pairs={{0,1},{1,0},{2,3},{3,2},{4,5},{5,4},{6,7},{7,6},{8,9},{9,8},{10,11... | collective-permute-start | bytes 393224 | tf_op jit(solution)/shard_map/ppermute | solution.py:292
